TPU v7x, 32 devices: a whole 2x2x4 slice. The times are simulated.
32 devices in a mesh: tok: 16 (over z, y, x), col: 2 (over core).
Axes of the slice: x: 2, y: 2, z: 4, core: 2. Of those that a mesh axis runs over, the one named last changes fastest.
Arguments:
- activations: bfloat16 [512, 6144], P('tok', 'col'), may hold values from -61 to 61
- block_slot: int32 [6], replicated, may hold values from 0 to 5, each once
- slot_tile: int32 [32], replicated, may hold values from 0 to 31, each once
Outputs:
- gram_tiles: float32 [32, 1024, 1024], P(('tok', 'col'))
- col_mean: float32 [6144], P('col')
- col_var: float32 [6144], P('col')
Inputs may be any that keep to these rules, and one draw needn't show every extreme that they name: `block_slot`: each stored position once. `slot_tile`: each value once.
All inputs are finite; a program needn't handle non-finite values.
Results may differ from a plain program's by a relative error of at most 0.0003.
Values may be sent and summed in bfloat16 or wider, within the bound.
No kernel may reach another device: no remote copies, remote signals or barrier semaphores. Data moves between devices by JAX's collectives and lax.ppermute only.
A program may use at most 64 MiB of HBM per device.

v0:
```python
import jax
import jax.numpy as jnp
import numpy as np
from jax import lax
from jax.sharding import PartitionSpec as P

BS = 1024


def on_device(activations, block_slot, slot_tile):
    n_tok = lax.axis_size("tok")
    n_col = lax.axis_size("col")
    tok_dev = activations.shape[0]
    total_tokens = tok_dev * n_tok
    col_index = lax.axis_index("col")
    values = activations.astype(jnp.float32)
    col_sum = lax.psum(jnp.sum(values, axis=0), "tok")
    col_mean = col_sum / total_tokens
    squares = lax.psum(jnp.sum((values - col_mean) ** 2, axis=0), "tok")
    col_var = squares / total_tokens
    gathered = lax.all_gather(activations, "col", axis=1, tiled=True)
    block_count = gathered.shape[1] // BS
    pair_count = block_count * (block_count + 1) // 2
    rows_np, cols_np = np.triu_indices(block_count)
    row_table = jnp.asarray(rows_np.astype(np.int32))
    col_table = jnp.asarray(cols_np.astype(np.int32))
    slot_grid = slot_tile.reshape(n_tok, n_col)
    peer_tiles = lax.dynamic_index_in_dim(slot_grid, col_index, 1, keepdims=False)
    clamped = jnp.where(peer_tiles < pair_count, peer_tiles, 0)
    first_slot = block_slot[row_table[clamped]]
    second_slot = block_slot[col_table[clamped]]
    blocks = gathered.reshape(tok_dev, block_count, BS)
    picked = jnp.take(blocks, jnp.stack([first_slot, second_slot], axis=1), axis=1)
    outgoing = picked.transpose(1, 0, 2, 3).reshape(n_tok, tok_dev, 2 * BS)
    arrived = lax.all_to_all(outgoing, "tok", split_axis=0, concat_axis=0, tiled=True)
    arrived = arrived.reshape(n_tok * tok_dev, 2 * BS)
    own_slot = lax.axis_index("tok") * n_col + col_index
    own_tile = lax.dynamic_index_in_dim(slot_tile, own_slot, 0, keepdims=False)
    left_block = arrived[:, :BS]
    right_block = arrived[:, BS:]
    product = (
        lax.dot_general(
            left_block, right_block, (((0,), (0,)), ((), ())), preferred_element_type=jnp.float32
        )
        / total_tokens
    )
    product = jnp.where(own_tile < pair_count, product, jnp.zeros_like(product))
    return (product[None], col_mean, col_var)


def solution(mesh):
    return jax.shard_map(
        on_device,
        mesh=mesh,
        in_specs=(P("tok", "col"), P(), P()),
        out_specs=(P(("tok", "col"), None, None), P("col"), P("col")),
        check_vma=False,
    )
```

profile of v0, /device:TPU:0, one launch (start us, length us, event | category | flops | bytes accessed | tf_op | source)
XLA Modules:
  0.0 200.0 jit_solution(13010305735175130137)
XLA Ops:
  0.6 0.0 copy-start
  0.6 0.0 copy-start.1
  0.7 0.8 reshape.144
  1.4 0.2 fusion.4
  1.6 1.3 gather_fusion
  3.0 0.1 copy.16
  3.0 0.1 fusion.5
  3.2 1.3 gather_fusion.2
  4.5 0.1 copy.19
  4.6 0.1 fusion.6
  4.7 0.0 copy-done
  4.7 0.7 gather_fusion.1
  5.4 0.7 gather_fusion.3
  6.1 0.1 copy.23
  6.1 0.1 reshape.182
  6.3 0.0 copy-done.1
  6.3 2.2 %all_gather.3 = bf16[32,6144]{1,0:T(8,128)(2,1)S(1)} all-gather(bf16[32,3072]{1,0:T(8,128)(2,1)S(1)} %copy-done.1), channel_id=1, replica_groups=mesh['tok'=16,'col'=2] {'col'}, dimensions={1}, use_global_device_ids=true | all-gather | bytes 589824 | tf_op jit(solution)/shard_map/all_gather | solution.py:21
  8.5 0.1 copy.22
  8.6 0.7 gather_fusion.4
  9.3 0.3 select_bitcast_fusion.1
  9.5 1.5 copy.27
  11.1 0.0 copy-start.3
  11.1 8.4 %all-to-all-start = ((bf16[16,32,2048]{2,1,0:T(8,128)(2,1)}), bf16[16,32,2048]{2,1,0:T(8,128)(2,1)S(1)}, u32[]{:S(2)}, u32[]{:S(2)}) async-start(bf16[16,32,2048]{2,1,0:T(8,128)(2,1)} %bitcast.14), calls=%async_computation | async-start | bytes 4194304 | tf_op jit(solution)/shard_map/all_to_all | solution.py:35
  19.5 0.0 copy-done.3
  19.5 0.6 dynamic_slice.8
  20.8 103.5 %psum.14 = f32[3072]{0:T(1024)S(1)} all-reduce(f32[3072]{0:T(1024)S(1)} %convert_reduce_fusion), channel_id=1, replica_groups=mesh['tok'=16,'col'=2] {'tok'}, use_global_device_ids=true, to_apply=%region_1.0 | all-reduce | flops 3072 | bytes 24576 | tf_op jit(solution)/shard_map/psum | solution.py:17
  124.3 0.0 copy-start.2
  124.3 0.1 fusion.3
  124.3 71.7 %psum.15 = f32[3072]{0:T(1024)S(1)} all-reduce(f32[3072]{0:T(1024)S(1)} %fusion.3), channel_id=1, replica_groups=mesh['tok'=16,'col'=2] {'tok'}, use_global_device_ids=true, to_apply=%region_3.0 | all-reduce | flops 3072 | bytes 24576 | tf_op jit(solution)/shard_map/psum | solution.py:19
  196.1 0.6 broadcast_multiply_fusion
  196.7 0.0 all-to-all-done
  196.7 3.3 %select_bitcast_fusion = f32[1,1024,1024]{2,1,0:T(8,128)} fusion(pred[]{:T(512)} %bitcast, bf16[512,2048]{1,0:T(8,128)(2,1)S(1)} %bitcast.23), kind=kOutput, calls=%fused_computation.5 | convolution fusion | flops 1075838976 | bytes 6291457 | tf_op jit(solution)/shard_map/dot_general | solution.py:42
  200.0 0.0 copy-done.2
  (9 shorter events, 0.1 us)
Async XLA Ops:
  0.6 4.1 %copy-start = (s32[6]{0:T(128)S(1)}, s32[6]{0:T(128)}, u32[]{:S(2)}) copy-start(s32[6]{0:T(128)} %param.6) | copy-start | bytes 76
  0.6 5.6 %copy-start.1 = (bf16[32,3072]{1,0:T(8,128)(2,1)S(1)}, bf16[32,3072]{1,0:T(8,128)(2,1)}, u32[]{:S(2)}) copy-start(bf16[32,3072]{1,0:T(8,128)(2,1)} %param.5) | copy-start | bytes 589828
  11.1 8.4 %copy-start.3 = (s32[32]{0:T(128)S(1)}, s32[32]{0:T(128)}, u32[]{:S(2)}) copy-start(s32[32]{0:T(128)} %param.7) | copy-start | bytes 388
  11.1 185.6 %all-to-all-start = ((bf16[16,32,2048]{2,1,0:T(8,128)(2,1)}), bf16[16,32,2048]{2,1,0:T(8,128)(2,1)S(1)}, u32[]{:S(2)}, u32[]{:S(2)}) async-start(bf16[16,32,2048]{2,1,0:T(8,128)(2,1)} %bitcast.14), calls=%async_computation | async-start | bytes 4194304 | tf_op jit(solution)/shard_map/all_to_all | solution.py:35
  124.3 75.7 %copy-start.2 = (f32[3072]{0:T(1024)}, f32[3072]{0:T(1024)S(1)}, u32[]{:S(2)}) copy-start(f32[3072]{0:T(1024)S(1)} %broadcast_multiply_fusion.1) | copy-start | bytes 36868
where the time goes:
time: 200 us
  blocking collectives  177 us (88%)
  starting transfers between devices  8.36 us (4%)
  local copies, waits for them, and re-layouts  8.04 us (4%)
  matrix products  3.31 us (2%)
    psum x1, blocking collectives, on_device(): col_sum = lax.psum(jnp.sum(values, axis=0), 'tok')  103 us
    psum x1, blocking collectives, on_device(): squares = lax.psum(jnp.sum((values - col_mean) ** 2, axis=0), 'tok')  71.7 us
    all_to_all x1, starting transfers between devices, on_device(): lax.all_to_all(outgoing, 'tok', split_axis=0, concat_axis=0, tiled=True)  8.36 us
  transfers between devices with their start and end apart: 1, of which 0 were waited for; matrix products, arithmetic and copies ran while one was open for 1% of the time, Pallas kernels for 0%

commit v1 on v0

v1 whole, which is shorter than its diff:
```python
import jax
import jax.numpy as jnp
import numpy as np
from jax import lax
from jax.experimental import pallas as pl
from jax.experimental.pallas import tpu as pltpu
from jax.sharding import PartitionSpec as P

BS = 1024


def split_tok(n_tok):
    n_in = 1
    while n_in * n_in < n_tok:
        n_in *= 2
    return n_tok // n_in, n_in


def outer_waves(n_out):
    waves = [[0]]
    for k in range(1, n_out // 2 + 1):
        waves.append([k] if 2 * k == n_out else [k, n_out - k])
    return waves


def pair_of(tile, block_count):
    pair_count = block_count * (block_count + 1) // 2
    tile = jnp.where(tile < pair_count, tile, 0)
    row = jnp.int32(0)
    start = jnp.int32(0)
    for r in range(1, block_count):
        first = r * block_count - r * (r - 1) // 2
        beyond = tile >= first
        row = jnp.where(beyond, r, row)
        start = jnp.where(beyond, first, start)
    return row, tile - start + row


def select_kernel(n_in, n_col, block_count, n_shards, *refs):
    slot_ref, tile_ref = refs[0], refs[1]
    shards = refs[2 : 2 + n_shards * n_col]
    outs = refs[2 + n_shards * n_col :]
    tok_dev, width = shards[0].shape
    held = width // BS
    tok = lax.axis_index("tok")
    col = lax.axis_index("col")
    inner = lax.rem(tok, n_in)
    for k in range(n_in):
        peer = tok - inner + (inner ^ k)
        pair = pair_of(tile_ref[peer * n_col + col], block_count)
        for side in range(2):
            block = slot_ref[pair[side]]
            owner = lax.div(block, held)
            column = pl.multiple_of((block - owner * held) * BS, BS)
            away = lax.rem(owner - col + n_col, n_col)
            for r in range(n_col):

                @pl.when(away == r)
                def _():
                    for s in range(n_shards):
                        outs[k][s * tok_dev : (s + 1) * tok_dev, side * BS : (side + 1) * BS] = (
                            shards[s * n_col + r][:, pl.ds(column, BS)]
                        )


def select(n_in, n_col, block_count, block_slot, slot_tile, shards):
    rows = len(shards) * shards[0][0].shape[0]
    smem = pl.BlockSpec(memory_space=pltpu.SMEM)
    vmem = pl.BlockSpec(memory_space=pltpu.VMEM)
    flat = [a for shard in shards for a in shard]
    return pl.pallas_call(
        lambda *refs: select_kernel(n_in, n_col, block_count, len(shards), *refs),
        out_shape=[jax.ShapeDtypeStruct((rows, 2 * BS), jnp.bfloat16)] * n_in,
        in_specs=[smem, smem] + [vmem] * len(flat),
        out_specs=[vmem] * n_in,
        name="select",
    )(block_slot, slot_tile, *flat)


def on_device(activations, block_slot, slot_tile):
    n_tok = lax.axis_size("tok")
    n_col = lax.axis_size("col")
    n_out, n_in = split_tok(n_tok)
    tok_dev, width = activations.shape
    total_tokens = tok_dev * n_tok
    block_count = width * n_col // BS
    pair_count = block_count * (block_count + 1) // 2

    def from_outer(a, k):
        pairs = [(t, (t // n_in + k) % n_out * n_in + t % n_in) for t in range(n_tok)]
        return lax.ppermute(a, "tok", pairs)

    def from_inner(a, k):
        return lax.ppermute(a, "tok", [(t, t ^ k) for t in range(n_tok)])

    def all_columns(a):
        return [a] + [
            lax.ppermute(a, "col", [(c, (c - r) % n_col) for c in range(n_col)])
            for r in range(1, n_col)
        ]

    shard = {0: activations}
    full = {0: all_columns(activations)}
    waves = outer_waves(n_out)
    for wave in waves[1:]:
        for k in wave:
            shard[k] = from_outer(activations, k)
    pieces = []
    for wave in waves:
        for k in wave:
            if k:
                full[k] = all_columns(shard[k])
        picked = select(n_in, n_col, block_count, block_slot, slot_tile, [full[k] for k in wave])
        pieces.append(picked[0])
        for k in range(1, n_in):
            pieces.append(from_inner(picked[k], k))

    def merge(a, b, count):
        return a[0] + b[0], a[1] + b[1] + (a[0] - b[0]) ** 2 / (2 * count)

    stats = []
    for k in range(n_out):
        values = shard[k].astype(jnp.float32)
        part = jnp.sum(values, axis=0)
        stats.append((part, jnp.sum((values - part / tok_dev) ** 2, axis=0)))
    count = tok_dev
    while len(stats) > 1:
        half = len(stats) // 2
        stats = [merge(stats[k], stats[k + half], count) for k in range(half)]
        count *= 2
    mine = stats[0]
    k = 1
    while k < n_in:
        other = from_inner(jnp.stack(mine), k)
        mine = merge(mine, (other[0], other[1]), count)
        count *= 2
        k *= 2
    col_mean = mine[0] / total_tokens
    col_var = mine[1] / total_tokens

    arrived = jnp.concatenate(pieces, axis=0)
    own_slot = lax.axis_index("tok") * n_col + lax.axis_index("col")
    own_tile = lax.dynamic_index_in_dim(slot_tile, own_slot, 0, keepdims=False)
    product = (
        lax.dot_general(
            arrived[:, :BS],
            arrived[:, BS:],
            (((0,), (0,)), ((), ())),
            preferred_element_type=jnp.float32,
        )
        / total_tokens
    )
    product = jnp.where(own_tile < pair_count, product, jnp.zeros_like(product))
    return (product[None], col_mean, col_var)


def solution(mesh):
    return jax.shard_map(
        on_device,
        mesh=mesh,
        in_specs=(P("tok", "col"), P(), P()),
        out_specs=(P(("tok", "col"), None, None), P("col"), P("col")),
        check_vma=False,
    )
```

time: 200 us -> 70.6 us (0.35)
  blocking collectives: 177 us -> 0 us
  waiting for transfers between devices: 0.01 us -> 27.6 us
  starting transfers between devices: 8.36 us -> 22.3 us
  Pallas kernels: 0 us -> 6.65 us
  local copies, waits for them, and re-layouts: 8.04 us -> 5.73 us
    psum x2 -> x0, blocking collectives: 175 us -> none  [the longest x1 103 us: on_device(): col_sum = lax.psum(jnp.sum(values, axis=0), 'tok')]
    ppermute x0 -> x18, waiting for transfers between devices: none -> 27.6 us  [the longest x3 13.7 us: from_outer(): return lax.ppermute(a, 'tok', pairs)]
    ppermute x0 -> x18, starting transfers between devices: none -> 22.3 us  [the longest x11 15.6 us: from_inner(): return lax.ppermute(a, 'tok', [(t, t ^ k) for t in range(n_tok)])]
    all_to_all x1 -> x0, starting transfers between devices: 8.36 us -> none  [on_device(): lax.all_to_all(outgoing, 'tok', split_axis=0, concat_axis=0, tiled=True)]
    pallas_call x0 -> x3, Pallas kernels: none -> 6.65 us  [select(): pl.pallas_call(lambda *refs: select_kernel(n_in, n_col, block_count, len(...]
    gather x7 -> x0, local copies, waits for them, and re-layouts: 4.81 us -> none  [the longest x3 2.07 us: on_device(): second_slot = block_slot[col_table[clamped]]]
    unnamed x8 -> x27, local copies, waits for them, and re-layouts: 0.02 us -> 4.46 us
    reshape x3 -> x0, local copies, waits for them, and re-layouts: 2.34 us -> none  [the longest x1 1.54 us: on_device(): outgoing = picked.transpose(1, 0, 2, 3).reshape(n_tok, tok_dev, 2 * BS)]
  transfers between devices with their start and end apart: 1 -> 18, of which waited for: 0 -> 6; matrix products, arithmetic and copies ran while one was open for 1% -> 9% of each run, Pallas kernels for 0% -> 9%
where the time goes in v1:
time: 70.6 us; the launch traced here: 70.3 us
  waiting for transfers between devices  27.6 us (39%)
  starting transfers between devices  22.3 us (32%)
  Pallas kernels  6.65 us (9%)
  local copies, waits for them, and re-layouts  5.73 us (8%)
  matrix products  3.31 us (5%)
  other arithmetic  3.14 us (4%)
  between operations  1.58 us (2%)
    ppermute x11, starting transfers between devices, from_inner(): return lax.ppermute(a, 'tok', [(t, t ^ k) for t in range(n_tok)])  15.6 us
    ppermute x3, waiting for transfers between devices, from_outer(): return lax.ppermute(a, 'tok', pairs)  13.7 us
    ppermute x11, waiting for transfers between devices, from_inner(): return lax.ppermute(a, 'tok', [(t, t ^ k) for t in range(n_tok)])  13.7 us
    pallas_call x3, Pallas kernels, select(): pl.pallas_call(lambda *refs: select_kernel(n_in, n_col, block_count, len(...  6.65 us
    ppermute x3, starting transfers between devices, from_outer(): return lax.ppermute(a, 'tok', pairs)  6.11 us
    unnamed x27, local copies, waits for them, and re-layouts  4.46 us
    dot_general x1, matrix products, on_device(): lax.dot_general(arrived[:, :BS], arrived[:, BS:], (((0,), (0,)), ((), ())...  3.31 us
  transfers between devices with their start and end apart: 18, of which 6 were waited for; matrix products, arithmetic and copies ran while one was open for 9% of the time, Pallas kernels for 9%

profile of v1, /device:TPU:0, one launch (start us, length us, event | category | flops | bytes accessed | tf_op | source)
XLA Modules:
  0.0 70.3 jit_solution(8663738336181955778)
XLA Ops:
  0.6 5.1 %collective-permute-start.6 = (bf16[32,3072]{1,0:T(8,128)(2,1)}, bf16[32,3072]{1,0:T(8,128)(2,1)S(1)}, u32[]{:S(2)}, u32[]{:S(2)}) collective-permute-start(bf16[32,3072]{1,0:T(8,128)(2,1)} %refs_2_.1), channel_id=1, source_target_pairs={{0,24},{2,26},{4,28},{6,30},{8,0},{10,2},{12,4},{14,6},{16,8},{18,... | collective-permute-start | bytes 589832 | tf_op jit(solution)/shard_map/ppermute | solution.py:91
  5.7 0.0 collective-permute-start.4
  5.7 0.0 collective-permute-start
  5.7 1.0 %collective-permute-start.11 = (bf16[32,3072]{1,0:T(8,128)(2,1)}, bf16[32,3072]{1,0:T(8,128)(2,1)S(1)}, u32[]{:S(2)}, u32[]{:S(2)}) collective-permute-start(bf16[32,3072]{1,0:T(8,128)(2,1)} %refs_2_.1), channel_id=1, source_target_pairs={{0,16},{2,18},{4,20},{6,22},{8,24},{10,26},{12,28},{14,30},{16,0},... | collective-permute-start | bytes 589832 | tf_op jit(solution)/shard_map/ppermute | solution.py:91
  6.7 1.0 %convert_reduce_fusion.3 = f32[3072]{0:T(1024)S(1)} fusion(bf16[32,3072]{1,0:T(8,128)(2,1)} %refs_2_.1), kind=kLoop, calls=%fused_computation.10 | loop fusion | flops 193536 | bytes 208896 | tf_op jit(solution)/shard_map/reduce_sum | solution.py:124
  7.8 1.0 %fusion.3 = f32[3072]{0:T(1024)S(1)} fusion(bf16[32,3072]{1,0:T(8,128)(2,1)} %refs_2_.1, f32[3072]{0:T(1024)S(1)} %broadcast_multiply_fusion.3), kind=kLoop, calls=%fused_computation.12 | loop fusion | flops 390144 | bytes 221184 | tf_op jit(solution)/shard_map/reduce_sum | solution.py:125
  8.8 2.6 %collective-permute-done.6.refs_4_ = bf16[32,3072]{1,0:T(8,128)(2,1)S(1)} collective-permute-done((bf16[32,3072]{1,0:T(8,128)(2,1)}, bf16[32,3072]{1,0:T(8,128)(2,1)S(1)}, u32[]{:S(2)}, u32[]{:S(2)}) %collective-permute-start.6) | collective-permute-done | bytes 196640 | tf_op jit(solution)/shard_map/ppermute | solution.py:91
  11.4 0.0 copy-start.1
  11.4 4.9 %collective-permute-done.4.refs_2_ = bf16[32,3072]{1,0:T(8,128)(2,1)S(1)} collective-permute-done((bf16[32,3072]{1,0:T(8,128)(2,1)}, bf16[32,3072]{1,0:T(8,128)(2,1)S(1)}, u32[]{:S(2)}, u32[]{:S(2)}) %collective-permute-start.4) | collective-permute-done | bytes 196640 | tf_op jit(solution)/shard_map/ppermute | solution.py:91
  16.4 0.0 copy-start.2
  16.4 6.2 %collective-permute-done.11.refs_2_ = bf16[32,3072]{1,0:T(8,128)(2,1)S(1)} collective-permute-done((bf16[32,3072]{1,0:T(8,128)(2,1)}, bf16[32,3072]{1,0:T(8,128)(2,1)S(1)}, u32[]{:S(2)}, u32[]{:S(2)}) %collective-permute-start.11) | collective-permute-done | bytes 196640 | tf_op jit(solution)/shard_map/ppermute | solution.py:91
  22.6 0.0 copy-start
  22.7 0.1 fusion.9
  22.8 0.1 fusion.7
  22.9 0.1 fusion.5
  23.0 1.6 %collective-permute-start.16 = (f32[2,3072]{1,0:T(2,128)S(1)}, f32[2,3072]{1,0:T(2,128)S(1)}, u32[]{:S(2)}, u32[]{:S(2)}) collective-permute-start(f32[2,3072]{1,0:T(2,128)S(1)} %pad_maximum_fusion), channel_id=1, source_target_pairs={{0,2},{2,0},{4,6},{6,4},{8,10},{10,8},{12,14},{14,12},{16,18},{18,... | collective-permute-start | bytes 73736 | tf_op jit(solution)/shard_map/ppermute | solution.py:94
  24.6 1.2 %dynamic_slice.4 = s32[1]{0:T(128)} dynamic-slice(s32[32]{0:T(128)} %refs_1_.5, s32[]{:T(128)S(6)} %select_n.12), dynamic_slice_sizes={1} | dynamic-slice | bytes 12 | tf_op jit(solution)/shard_map/jit(dynamic_index_in_dim)/dynamic_slice | solution.py:143
  26.5 0.0 collective-permute-done.refs_3_
  26.5 0.0 copy-start.3
  26.5 0.7 copy-done.3
  27.1 2.1 %select.3 = (bf16[32,2048]{1,0:T(8,128)(2,1)}, bf16[32,2048]{1,0:T(8,128)(2,1)}, bf16[32,2048]{1,0:T(8,128)(2,1)}, bf16[32,2048]{1,0:T(8,128)(2,1)}) custom-call(s32[6]{0:T(128)} %refs_0_.5, s32[32]{0:T(128)} %refs_1_.5, bf16[32,3072]{1,0:T(8,128)(2,1)} %refs_2_.1, bf16[32,3072]{1,0:T(8,128)(2,1)} %copy-done.3), custom_call_target="tpu_custom_call" | custom-call | tf_op jit(solution)/shard_map/select/pallas_call | solution.py:71
  29.2 0.5 collective-permute-start.1
  29.8 1.5 %collective-permute-start.2 = (bf16[32,2048]{1,0:T(8,128)(2,1)}, bf16[32,2048]{1,0:T(8,128)(2,1)S(1)}, u32[]{:S(2)}, u32[]{:S(2)}) collective-permute-start(bf16[32,2048]{1,0:T(8,128)(2,1)} %get-tuple-element.17), channel_id=1, source_target_pairs={{0,4},{2,6},{4,0},{6,2},{8,12},{10,14},{12,8},{14,10},{16,20},{18,... | collective-permute-start | bytes 393224 | tf_op jit(solution)/shard_map/ppermute | solution.py:94
  31.3 1.4 %collective-permute-start.3 = (bf16[32,2048]{1,0:T(8,128)(2,1)}, bf16[32,2048]{1,0:T(8,128)(2,1)S(1)}, u32[]{:S(2)}, u32[]{:S(2)}) collective-permute-start(bf16[32,2048]{1,0:T(8,128)(2,1)} %get-tuple-element.18), channel_id=1, source_target_pairs={{0,6},{2,4},{4,2},{6,0},{8,14},{10,12},{12,10},{14,8},{16,22},{18,... | collective-permute-start | bytes 393224 | tf_op jit(solution)/shard_map/ppermute | solution.py:94
  32.7 0.0 collective-permute-done.16
  32.8 1.6 %collective-permute-start.17 = (f32[2,3072]{1,0:T(2,128)S(1)}, f32[2,3072]{1,0:T(2,128)S(1)}, u32[]{:S(2)}, u32[]{:S(2)}) collective-permute-start(f32[2,3072]{1,0:T(2,128)S(1)} %pad_maximum_fusion.1), channel_id=1, source_target_pairs={{0,4},{2,6},{4,0},{6,2},{8,12},{10,14},{12,8},{14,10},{16,20},{18,... | collective-permute-start | bytes 73736 | tf_op jit(solution)/shard_map/ppermute | solution.py:94
  34.4 0.9 %constant_dynamic-update-slice_fusion.11 = bf16[512,2048]{1,0:T(8,128)(2,1)S(1)} fusion(bf16[32,2048]{1,0:T(8,128)(2,1)} %get-tuple-element.15), kind=kLoop, calls=%fused_computation.30 | loop fusion | bytes 262144
  35.3 0.1 collective-permute-start.7
  35.4 1.7 %collective-permute-done.17 = f32[2,3072]{1,0:T(2,128)S(1)} collective-permute-done((f32[2,3072]{1,0:T(2,128)S(1)}, f32[2,3072]{1,0:T(2,128)S(1)}, u32[]{:S(2)}, u32[]{:S(2)}) %collective-permute-start.17) | collective-permute-done | bytes 24608 | tf_op jit(solution)/shard_map/ppermute | solution.py:94
  37.1 0.0 collective-permute-start.5
  37.1 0.6 add_multiply_fusion
  37.8 0.0 collective-permute-done.1
  37.8 0.5 collective-permute-start.12
  38.3 0.0 collective-permute-done.2
  38.3 0.0 collective-permute-done.7.refs_5_
  38.3 0.0 copy-start.5
  38.3 0.2 collective-permute-done.5.refs_3_
  38.6 0.0 copy-done.1
  38.6 0.0 copy-done.2
  38.6 0.4 copy-done.5
  39.0 0.0 copy-start.6
  39.0 0.7 copy-done.6
  39.7 2.5 %select.4 = (bf16[64,2048]{1,0:T(8,128)(2,1)}, bf16[64,2048]{1,0:T(8,128)(2,1)}, bf16[64,2048]{1,0:T(8,128)(2,1)}, bf16[64,2048]{1,0:T(8,128)(2,1)}) custom-call(s32[6]{0:T(128)} %refs_0_.5, s32[32]{0:T(128)} %refs_1_.5, bf16[32,3072]{1,0:T(8,128)(2,1)} %copy-done.2, bf16[32,3072]{1,0:T(8,128)(2,1)} %copy-done.6, bf16[32,3072]{1,0:T(8,128)(2,1)} %copy-done.1, ...), custom_call_target="tpu_custom_call" | custom-call | tf_op jit(solution)/shard_map/select/pallas_call | solution.py:71
  42.1 2.5 %collective-permute-start.8 = (bf16[64,2048]{1,0:T(8,128)(2,1)}, bf16[64,2048]{1,0:T(8,128)(2,1)S(1)}, u32[]{:S(2)}, u32[]{:S(2)}) collective-permute-start(bf16[64,2048]{1,0:T(8,128)(2,1)} %get-tuple-element.20), channel_id=1, source_target_pairs={{0,2},{2,0},{4,6},{6,4},{8,10},{10,8},{12,14},{14,12},{16,18},{18,... | collective-permute-start | bytes 786440 | tf_op jit(solution)/shard_map/ppermute | solution.py:94
  44.6 0.0 collective-permute-done.3
  44.6 0.0 collective-permute-done.12.refs_3_
  44.6 0.0 copy-done
  44.6 0.0 copy-start.4
  44.6 0.7 copy-done.4
  45.3 2.1 %select.5 = (bf16[32,2048]{1,0:T(8,128)(2,1)}, bf16[32,2048]{1,0:T(8,128)(2,1)}, bf16[32,2048]{1,0:T(8,128)(2,1)}, bf16[32,2048]{1,0:T(8,128)(2,1)}) custom-call(s32[6]{0:T(128)} %refs_0_.5, s32[32]{0:T(128)} %refs_1_.5, bf16[32,3072]{1,0:T(8,128)(2,1)} %copy-done, bf16[32,3072]{1,0:T(8,128)(2,1)} %copy-done.4), custom_call_target="tpu_custom_call" | custom-call | tf_op jit(solution)/shard_map/select/pallas_call | solution.py:71
  47.4 0.0 collective-permute-start.13
  47.4 2.0 %collective-permute-start.14 = (bf16[32,2048]{1,0:T(8,128)(2,1)}, bf16[32,2048]{1,0:T(8,128)(2,1)S(1)}, u32[]{:S(2)}, u32[]{:S(2)}) collective-permute-start(bf16[32,2048]{1,0:T(8,128)(2,1)} %get-tuple-element.25), channel_id=1, source_target_pairs={{0,4},{2,6},{4,0},{6,2},{8,12},{10,14},{12,8},{14,10},{16,20},{18,... | collective-permute-start | bytes 393224 | tf_op jit(solution)/shard_map/ppermute | solution.py:94
  49.5 1.4 %collective-permute-start.15 = (bf16[32,2048]{1,0:T(8,128)(2,1)}, bf16[32,2048]{1,0:T(8,128)(2,1)S(1)}, u32[]{:S(2)}, u32[]{:S(2)}) collective-permute-start(bf16[32,2048]{1,0:T(8,128)(2,1)} %get-tuple-element.26), channel_id=1, source_target_pairs={{0,6},{2,4},{4,2},{6,0},{8,14},{10,12},{12,10},{14,8},{16,22},{18,... | collective-permute-start | bytes 393224 | tf_op jit(solution)/shard_map/ppermute | solution.py:94
  50.9 1.5 %collective-permute-start.9 = (bf16[64,2048]{1,0:T(8,128)(2,1)}, bf16[64,2048]{1,0:T(8,128)(2,1)S(1)}, u32[]{:S(2)}, u32[]{:S(2)}) collective-permute-start(bf16[64,2048]{1,0:T(8,128)(2,1)} %get-tuple-element.21), channel_id=1, source_target_pairs={{0,4},{2,6},{4,0},{6,2},{8,12},{10,14},{12,8},{14,10},{16,20},{18,... | collective-permute-start | bytes 786440 | tf_op jit(solution)/shard_map/ppermute | solution.py:94
  52.4 1.0 %constant_dynamic-update-slice_fusion.7 = bf16[512,2048]{1,0:T(8,128)(2,1)S(1)} fusion(bf16[512,2048]{1,0:T(8,128)(2,1)S(1)} %constant_dynamic-update-slice_fusion.8, bf16[64,2048]{1,0:T(8,128)(2,1)} %get-tuple-element.19), kind=kLoop, calls=%fused_computation.26 | loop fusion | bytes 524288
  53.4 0.0 collective-permute-done.8
  53.4 1.5 %collective-permute-start.10 = (bf16[64,2048]{1,0:T(8,128)(2,1)}, bf16[64,2048]{1,0:T(8,128)(2,1)S(1)}, u32[]{:S(2)}, u32[]{:S(2)}) collective-permute-start(bf16[64,2048]{1,0:T(8,128)(2,1)} %get-tuple-element.22), channel_id=1, source_target_pairs={{0,6},{2,4},{4,2},{6,0},{8,14},{10,12},{12,10},{14,8},{16,22},{18,... | collective-permute-start | bytes 786440 | tf_op jit(solution)/shard_map/ppermute | solution.py:94
  55.0 11.9 %collective-permute-done.9 = bf16[64,2048]{1,0:T(8,128)(2,1)S(1)} collective-permute-done((bf16[64,2048]{1,0:T(8,128)(2,1)}, bf16[64,2048]{1,0:T(8,128)(2,1)S(1)}, u32[]{:S(2)}, u32[]{:S(2)}) %collective-permute-start.9) | collective-permute-done | bytes 262176 | tf_op jit(solution)/shard_map/ppermute | solution.py:94
  66.9 0.0 collective-permute-done.10
  66.9 0.0 copy-done.7
  66.9 0.0 collective-permute-done.13
  67.0 0.0 collective-permute-done.14
  67.0 0.0 collective-permute-done.15
  67.0 3.3 %select_bitcast_fusion = f32[1,1024,1024]{2,1,0:T(8,128)} fusion(pred[]{:T(512)} %bitcast, bf16[512,2048]{1,0:T(8,128)(2,1)S(1)} %constant_dynamic-update-slice_fusion), kind=kOutput, calls=%fused_computation | convolution fusion | flops 1075838976 | bytes 6291457 | tf_op jit(solution)/shard_map/dot_general | solution.py:145
  (23 shorter events, 0.4 us)
Async XLA Ops:
  0.6 10.7 %collective-permute-start.6 = (bf16[32,3072]{1,0:T(8,128)(2,1)}, bf16[32,3072]{1,0:T(8,128)(2,1)S(1)}, u32[]{:S(2)}, u32[]{:S(2)}) collective-permute-start(bf16[32,3072]{1,0:T(8,128)(2,1)} %refs_2_.1), channel_id=1, source_target_pairs={{0,24},{2,26},{4,28},{6,30},{8,0},{10,2},{12,4},{14,6},{16,8},{18,... | collective-permute-start | bytes 589832 | tf_op jit(solution)/shard_map/ppermute | solution.py:91
  5.7 10.6 %collective-permute-start.4 = (bf16[32,3072]{1,0:T(8,128)(2,1)}, bf16[32,3072]{1,0:T(8,128)(2,1)S(1)}, u32[]{:S(2)}, u32[]{:S(2)}) collective-permute-start(bf16[32,3072]{1,0:T(8,128)(2,1)} %refs_2_.1), channel_id=1, source_target_pairs={{0,8},{2,10},{4,12},{6,14},{8,16},{10,18},{12,20},{14,22},{16,24},... | collective-permute-start | bytes 589832 | tf_op jit(solution)/shard_map/ppermute | solution.py:91
  5.7 20.7 %collective-permute-start = (bf16[32,3072]{1,0:T(8,128)(2,1)}, bf16[32,3072]{1,0:T(8,128)(2,1)S(1)}, u32[]{:S(2)}, u32[]{:S(2)}) collective-permute-start(bf16[32,3072]{1,0:T(8,128)(2,1)} %refs_2_.1), channel_id=1, source_target_pairs={{0,1},{1,0},{2,3},{3,2},{4,5},{5,4},{6,7},{7,6},{8,9},{9,8},{10,11... | collective-permute-start | bytes 589832 | tf_op jit(solution)/shard_map/ppermute | solution.py:98
  5.7 16.9 %collective-permute-start.11 = (bf16[32,3072]{1,0:T(8,128)(2,1)}, bf16[32,3072]{1,0:T(8,128)(2,1)S(1)}, u32[]{:S(2)}, u32[]{:S(2)}) collective-permute-start(bf16[32,3072]{1,0:T(8,128)(2,1)} %refs_2_.1), channel_id=1, source_target_pairs={{0,16},{2,18},{4,20},{6,22},{8,24},{10,26},{12,28},{14,30},{16,0},... | collective-permute-start | bytes 589832 | tf_op jit(solution)/shard_map/ppermute | solution.py:91
  11.4 27.2 %copy-start.1 = (bf16[32,3072]{1,0:T(8,128)(2,1)}, bf16[32,3072]{1,0:T(8,128)(2,1)S(1)}, u32[]{:S(2)}) copy-start(bf16[32,3072]{1,0:T(8,128)(2,1)S(1)} %collective-permute-done.6.refs_4_) | copy-start | bytes 589828
  16.4 22.2 %copy-start.2 = (bf16[32,3072]{1,0:T(8,128)(2,1)}, bf16[32,3072]{1,0:T(8,128)(2,1)S(1)}, u32[]{:S(2)}) copy-start(bf16[32,3072]{1,0:T(8,128)(2,1)S(1)} %collective-permute-done.4.refs_2_) | copy-start | bytes 589828
  22.6 22.0 %copy-start = (bf16[32,3072]{1,0:T(8,128)(2,1)}, bf16[32,3072]{1,0:T(8,128)(2,1)S(1)}, u32[]{:S(2)}) copy-start(bf16[32,3072]{1,0:T(8,128)(2,1)S(1)} %collective-permute-done.11.refs_2_) | copy-start | bytes 589828
  23.0 9.7 %collective-permute-start.16 = (f32[2,3072]{1,0:T(2,128)S(1)}, f32[2,3072]{1,0:T(2,128)S(1)}, u32[]{:S(2)}, u32[]{:S(2)}) collective-permute-start(f32[2,3072]{1,0:T(2,128)S(1)} %pad_maximum_fusion), channel_id=1, source_target_pairs={{0,2},{2,0},{4,6},{6,4},{8,10},{10,8},{12,14},{14,12},{16,18},{18,... | collective-permute-start | bytes 73736 | tf_op jit(solution)/shard_map/ppermute | solution.py:94
  26.5 0.7 copy-start.3
  29.2 8.5 %collective-permute-start.1 = (bf16[32,2048]{1,0:T(8,128)(2,1)}, bf16[32,2048]{1,0:T(8,128)(2,1)S(1)}, u32[]{:S(2)}, u32[]{:S(2)}) collective-permute-start(bf16[32,2048]{1,0:T(8,128)(2,1)} %get-tuple-element.16), channel_id=1, source_target_pairs={{0,2},{2,0},{4,6},{6,4},{8,10},{10,8},{12,14},{14,12},{16,18},{18,... | collective-permute-start | bytes 393224 | tf_op jit(solution)/shard_map/ppermute | solution.py:94
  29.8 8.5 %collective-permute-start.2 = (bf16[32,2048]{1,0:T(8,128)(2,1)}, bf16[32,2048]{1,0:T(8,128)(2,1)S(1)}, u32[]{:S(2)}, u32[]{:S(2)}) collective-permute-start(bf16[32,2048]{1,0:T(8,128)(2,1)} %get-tuple-element.17), channel_id=1, source_target_pairs={{0,4},{2,6},{4,0},{6,2},{8,12},{10,14},{12,8},{14,10},{16,20},{18,... | collective-permute-start | bytes 393224 | tf_op jit(solution)/shard_map/ppermute | solution.py:94
  31.3 13.3 %collective-permute-start.3 = (bf16[32,2048]{1,0:T(8,128)(2,1)}, bf16[32,2048]{1,0:T(8,128)(2,1)S(1)}, u32[]{:S(2)}, u32[]{:S(2)}) collective-permute-start(bf16[32,2048]{1,0:T(8,128)(2,1)} %get-tuple-element.18), channel_id=1, source_target_pairs={{0,6},{2,4},{4,2},{6,0},{8,14},{10,12},{12,10},{14,8},{16,22},{18,... | collective-permute-start | bytes 393224 | tf_op jit(solution)/shard_map/ppermute | solution.py:94
  32.8 4.3 %collective-permute-start.17 = (f32[2,3072]{1,0:T(2,128)S(1)}, f32[2,3072]{1,0:T(2,128)S(1)}, u32[]{:S(2)}, u32[]{:S(2)}) collective-permute-start(f32[2,3072]{1,0:T(2,128)S(1)} %pad_maximum_fusion.1), channel_id=1, source_target_pairs={{0,4},{2,6},{4,0},{6,2},{8,12},{10,14},{12,8},{14,10},{16,20},{18,... | collective-permute-start | bytes 73736 | tf_op jit(solution)/shard_map/ppermute | solution.py:94
  35.3 3.0 %collective-permute-start.7 = (bf16[32,3072]{1,0:T(8,128)(2,1)S(1)}, bf16[32,3072]{1,0:T(8,128)(2,1)S(1)}, u32[]{:S(2)}, u32[]{:S(2)}) collective-permute-start(bf16[32,3072]{1,0:T(8,128)(2,1)S(1)} %collective-permute-done.6.refs_4_), channel_id=1, source_target_pairs={{0,1},{1,0},{2,3},{3,2},{4,5},{5,4},{6,7},{7,6},{8,9},{9,8},{10,11... | collective-permute-start | bytes 589832 | tf_op jit(solution)/shard_map/ppermute | solution.py:98
  37.1 1.4 %collective-permute-start.5 = (bf16[32,3072]{1,0:T(8,128)(2,1)S(1)}, bf16[32,3072]{1,0:T(8,128)(2,1)S(1)}, u32[]{:S(2)}, u32[]{:S(2)}) collective-permute-start(bf16[32,3072]{1,0:T(8,128)(2,1)S(1)} %collective-permute-done.4.refs_2_), channel_id=1, source_target_pairs={{0,1},{1,0},{2,3},{3,2},{4,5},{5,4},{6,7},{7,6},{8,9},{9,8},{10,11... | collective-permute-start | bytes 589832 | tf_op jit(solution)/shard_map/ppermute | solution.py:98
  37.8 6.9 %collective-permute-start.12 = (bf16[32,3072]{1,0:T(8,128)(2,1)S(1)}, bf16[32,3072]{1,0:T(8,128)(2,1)S(1)}, u32[]{:S(2)}, u32[]{:S(2)}) collective-permute-start(bf16[32,3072]{1,0:T(8,128)(2,1)S(1)} %collective-permute-done.11.refs_2_), channel_id=1, source_target_pairs={{0,1},{1,0},{2,3},{3,2},{4,5},{5,4},{6,7},{7,6},{8,9},{9,8},{10,11... | collective-permute-start | bytes 589832 | tf_op jit(solution)/shard_map/ppermute | solution.py:98
  38.3 0.7 copy-start.5
  39.0 0.7 copy-start.6
  42.1 11.3 %collective-permute-start.8 = (bf16[64,2048]{1,0:T(8,128)(2,1)}, bf16[64,2048]{1,0:T(8,128)(2,1)S(1)}, u32[]{:S(2)}, u32[]{:S(2)}) collective-permute-start(bf16[64,2048]{1,0:T(8,128)(2,1)} %get-tuple-element.20), channel_id=1, source_target_pairs={{0,2},{2,0},{4,6},{6,4},{8,10},{10,8},{12,14},{14,12},{16,18},{18,... | collective-permute-start | bytes 786440 | tf_op jit(solution)/shard_map/ppermute | solution.py:94
  44.6 0.7 copy-start.4
  47.4 19.5 %copy-start.7 = (bf16[32,2048]{1,0:T(8,128)(2,1)S(1)}, bf16[32,2048]{1,0:T(8,128)(2,1)}, u32[]{:S(2)}) copy-start(bf16[32,2048]{1,0:T(8,128)(2,1)} %get-tuple-element.23) | copy-start | bytes 393220
  47.4 19.5 %collective-permute-start.13 = (bf16[32,2048]{1,0:T(8,128)(2,1)}, bf16[32,2048]{1,0:T(8,128)(2,1)S(1)}, u32[]{:S(2)}, u32[]{:S(2)}) collective-permute-start(bf16[32,2048]{1,0:T(8,128)(2,1)} %get-tuple-element.24), channel_id=1, source_target_pairs={{0,2},{2,0},{4,6},{6,4},{8,10},{10,8},{12,14},{14,12},{16,18},{18,... | collective-permute-start | bytes 393224 | tf_op jit(solution)/shard_map/ppermute | solution.py:94
  47.4 19.6 %collective-permute-start.14 = (bf16[32,2048]{1,0:T(8,128)(2,1)}, bf16[32,2048]{1,0:T(8,128)(2,1)S(1)}, u32[]{:S(2)}, u32[]{:S(2)}) collective-permute-start(bf16[32,2048]{1,0:T(8,128)(2,1)} %get-tuple-element.25), channel_id=1, source_target_pairs={{0,4},{2,6},{4,0},{6,2},{8,12},{10,14},{12,8},{14,10},{16,20},{18,... | collective-permute-start | bytes 393224 | tf_op jit(solution)/shard_map/ppermute | solution.py:94
  49.5 17.5 %collective-permute-start.15 = (bf16[32,2048]{1,0:T(8,128)(2,1)}, bf16[32,2048]{1,0:T(8,128)(2,1)S(1)}, u32[]{:S(2)}, u32[]{:S(2)}) collective-permute-start(bf16[32,2048]{1,0:T(8,128)(2,1)} %get-tuple-element.26), channel_id=1, source_target_pairs={{0,6},{2,4},{4,2},{6,0},{8,14},{10,12},{12,10},{14,8},{16,22},{18,... | collective-permute-start | bytes 393224 | tf_op jit(solution)/shard_map/ppermute | solution.py:94
  50.9 16.0 %collective-permute-start.9 = (bf16[64,2048]{1,0:T(8,128)(2,1)}, bf16[64,2048]{1,0:T(8,128)(2,1)S(1)}, u32[]{:S(2)}, u32[]{:S(2)}) collective-permute-start(bf16[64,2048]{1,0:T(8,128)(2,1)} %get-tuple-element.21), channel_id=1, source_target_pairs={{0,4},{2,6},{4,0},{6,2},{8,12},{10,14},{12,8},{14,10},{16,20},{18,... | collective-permute-start | bytes 786440 | tf_op jit(solution)/shard_map/ppermute | solution.py:94
  53.4 13.5 %collective-permute-start.10 = (bf16[64,2048]{1,0:T(8,128)(2,1)}, bf16[64,2048]{1,0:T(8,128)(2,1)S(1)}, u32[]{:S(2)}, u32[]{:S(2)}) collective-permute-start(bf16[64,2048]{1,0:T(8,128)(2,1)} %get-tuple-element.22), channel_id=1, source_target_pairs={{0,6},{2,4},{4,2},{6,0},{8,14},{10,12},{12,10},{14,8},{16,22},{18,... | collective-permute-start | bytes 786440 | tf_op jit(solution)/shard_map/ppermute | solution.py:94

commit v2 on v1

v2 whole, which is shorter than its diff:
```python
import jax
import jax.numpy as jnp
import numpy as np
from jax import lax
from jax.experimental import pallas as pl
from jax.experimental.pallas import tpu as pltpu
from jax.sharding import PartitionSpec as P

BS = 1024


def split_tok(n_tok):
    n_in = 1
    while n_in * n_in < n_tok:
        n_in *= 2
    return n_tok // n_in, n_in


def outer_waves(n_out):
    waves = [[0], [1, 2], [3]] if n_out >= 4 else [[k] for k in range(n_out)]
    return waves + [[k, k + 1] for k in range(4, n_out, 2)]


def pair_of(tile, block_count):
    pair_count = block_count * (block_count + 1) // 2
    tile = jnp.where(tile < pair_count, tile, 0)
    row = jnp.int32(0)
    start = jnp.int32(0)
    for r in range(1, block_count):
        first = r * block_count - r * (r - 1) // 2
        beyond = tile >= first
        row = jnp.where(beyond, r, row)
        start = jnp.where(beyond, first, start)
    return row, tile - start + row


def select_kernel(n_in, n_col, block_count, n_shards, *refs):
    slot_ref, tile_ref = refs[0], refs[1]
    shards = refs[2 : 2 + n_shards * n_col]
    outs = refs[2 + n_shards * n_col :]
    tok_dev, width = shards[0].shape
    held = width // BS
    tok = lax.axis_index("tok")
    col = lax.axis_index("col")
    inner = lax.rem(tok, n_in)
    for k in range(n_in):
        peer = tok - inner + (inner ^ k)
        pair = pair_of(tile_ref[peer * n_col + col], block_count)
        for side in range(2):
            block = slot_ref[pair[side]]
            owner = lax.div(block, held)
            column = pl.multiple_of((block - owner * held) * BS, BS)
            away = lax.rem(owner - col + n_col, n_col)
            for r in range(n_col):

                @pl.when(away == r)
                def _():
                    for s in range(n_shards):
                        outs[k][s * tok_dev : (s + 1) * tok_dev, side * BS : (side + 1) * BS] = (
                            shards[s * n_col + r][:, pl.ds(column, BS)]
                        )


def select(n_in, n_col, block_count, block_slot, slot_tile, shards, near):
    rows = len(shards) * shards[0][0].shape[0]
    flat = [near.put(a) for shard in shards for a in shard]
    return pl.pallas_call(
        lambda *refs: select_kernel(n_in, n_col, block_count, len(shards), *refs),
        out_shape=[near.out((rows, 2 * BS), jnp.bfloat16)] * n_in,
        in_specs=[SMEM, SMEM] + [VMEM] * len(flat),
        out_specs=[VMEM] * n_in,
        cost_estimate=pl.CostEstimate(flops=0, transcendentals=0, bytes_accessed=8 * rows * 2 * BS),
        name="select",
    )(block_slot, slot_tile, *flat)


def merge(a, b, count):
    return a[0] + b[0], a[1] + b[1] + (a[0] - b[0]) ** 2 / (2 * count)


def stats_kernel(*refs):
    shards, out = refs[:-1], refs[-1]
    count = shards[0].shape[0]
    parts = []
    for ref in shards:
        values = ref[...].astype(jnp.float32)
        part = jnp.sum(values, axis=0, keepdims=True)
        parts.append((part, jnp.sum((values - part / count) ** 2, axis=0, keepdims=True)))
    while len(parts) > 1:
        half = len(parts) // 2
        parts = [merge(parts[k], parts[k + half], count) for k in range(half)]
        count *= 2
    out[0:1, :] = parts[0][0]
    out[1:2, :] = parts[0][1]


def local_stats(shards, near):
    tok_dev, width = shards[0].shape
    return pl.pallas_call(
        stats_kernel,
        out_shape=near.out((2, width), jnp.float32),
        in_specs=[VMEM] * len(shards),
        out_specs=VMEM,
        cost_estimate=pl.CostEstimate(
            flops=4 * len(shards) * tok_dev * width,
            transcendentals=0,
            bytes_accessed=2 * len(shards) * tok_dev * width,
        ),
        name="stats",
    )(*[near.put(a) for a in shards])


def gram_kernel(n_col, pair_count, tile_ref, *refs):
    pieces, (out, left, right, chunk, sems) = refs[:-5], refs[-5:]
    total_tokens = left.shape[0]
    start = 0
    for ref in pieces:
        rows = ref.shape[0]
        left[start : start + rows, :] = ref[:, :BS]
        right[start : start + rows, :] = ref[:, BS:]
        start += rows
    mine = tile_ref[lax.axis_index("tok") * n_col + lax.axis_index("col")]
    rows = chunk.shape[1]
    copies = [None, None]
    for m in range(BS // rows):
        slot = m % 2
        if copies[slot] is not None:
            copies[slot].wait()
        product = lax.dot_general(
            left[:, m * rows : (m + 1) * rows],
            right[...],
            (((0,), (0,)), ((), ())),
            preferred_element_type=jnp.float32,
        )
        chunk[slot] = jnp.where(mine < pair_count, product / total_tokens, 0.0)
        copies[slot] = pltpu.make_async_copy(
            chunk.at[slot], out.at[0, m * rows : (m + 1) * rows, :], sems.at[slot]
        )
        copies[slot].start()
    for copy in copies:
        copy.wait()


def gram(n_col, pair_count, slot_tile, pieces, near):
    total_tokens = sum(a.shape[0] for a in pieces)
    return pl.pallas_call(
        lambda *refs: gram_kernel(n_col, pair_count, *refs),
        out_shape=jax.ShapeDtypeStruct((1, BS, BS), jnp.float32),
        in_specs=[SMEM] + [VMEM] * len(pieces),
        out_specs=pl.BlockSpec(memory_space=pl.ANY),
        scratch_shapes=[
            pltpu.VMEM((total_tokens, BS), jnp.bfloat16),
            pltpu.VMEM((total_tokens, BS), jnp.bfloat16),
            pltpu.VMEM((2, BS // 4, BS), jnp.float32),
            pltpu.SemaphoreType.DMA((2,)),
        ],
        cost_estimate=pl.CostEstimate(
            flops=2 * total_tokens * BS * BS, transcendentals=0, bytes_accessed=4 * BS * BS
        ),
        name="gram",
    )(slot_tile, *[near.put(a) for a in pieces])


SMEM = pl.BlockSpec(memory_space=pltpu.SMEM)
VMEM = pl.BlockSpec(memory_space=pltpu.VMEM)


class Near:
    def __init__(self, fits):
        self.fits = fits

    def put(self, a):
        return pltpu.with_memory_space_constraint(a, pltpu.VMEM) if self.fits else a

    def out(self, shape, dtype):
        return pltpu.VMEM(shape, dtype) if self.fits else jax.ShapeDtypeStruct(shape, dtype)


def after(value, *earlier):
    return lax.optimization_barrier((value, *earlier))[0]


def by_blocks(activations, block_slot, slot_tile):
    n_tok = lax.axis_size("tok")
    n_col = lax.axis_size("col")
    n_out, n_in = split_tok(n_tok)
    tok_dev, width = activations.shape
    total_tokens = tok_dev * n_tok
    block_count = width * n_col // BS
    pair_count = block_count * (block_count + 1) // 2
    held = 2 * tok_dev * (n_out * n_col * width + 2 * n_tok * 2 * BS)
    near = Near(held <= 12 << 20)

    def from_outer(a, k):
        return lax.ppermute(a, "tok", [(t, t ^ (k * n_in)) for t in range(n_tok)])

    def from_inner(a, k):
        return lax.ppermute(a, "tok", [(t, t ^ k) for t in range(n_tok)])

    def all_columns(a):
        return [a] + [
            lax.ppermute(a, "col", [(c, (c - r) % n_col) for c in range(n_col)])
            for r in range(1, n_col)
        ]

    waves = outer_waves(n_out)
    shard = {0: activations}
    source = activations
    pieces = []
    done = None
    for w, wave in enumerate(waves):
        full = []
        for k in wave:
            if k:
                shard[k] = after(from_outer(activations if w < 2 else source, k), done)
            full.append(all_columns(shard[k]))
        source = after(activations, *[shard[k] for k in wave if k])
        picked = select(n_in, n_col, block_count, block_slot, slot_tile, full, near)
        if pieces:
            picked = lax.optimization_barrier((*picked, *arrived))[:n_in]
        done = picked[0]
        pieces.append(picked[0])
        arrived = [from_inner(picked[k], k) for k in range(1, n_in)]
        pieces.extend(arrived)

    mine = local_stats([after(shard[k], done) for k in range(n_out)], near)
    mine = (mine[0], mine[1])
    count = tok_dev * n_out
    k = 1
    while k < n_in:
        other = from_inner(jnp.stack(mine), k)
        mine = merge(mine, (other[0], other[1]), count)
        count *= 2
        k *= 2
    product = gram(n_col, pair_count, slot_tile, pieces, near)
    return (product, mine[0] / total_tokens, mine[1] / total_tokens)


def wanted(tile_ref, slot_ref, col, block_count, n_col):
    pair = pair_of(tile_ref[lax.axis_index("tok") * n_col + col], block_count)
    return slot_ref[pair[0]], slot_ref[pair[1]]


def stat_tree(parts, count):
    while len(parts) > 1:
        half = len(parts) // 2
        parts = [merge(parts[k], parts[k + half], count) for k in range(half)]
        count *= 2
    return parts[0]


def shard_stats(ref):
    values = ref[...].astype(jnp.float32)
    part = jnp.sum(values, axis=0, keepdims=True)
    mean = part / values.shape[0]
    return part, jnp.sum((values - mean) ** 2, axis=0, keepdims=True)


def take_block(block, col, held, pieces, starts, dst):
    owner = lax.div(block, held)
    column = pl.multiple_of((block - owner * held) * BS, BS)

    @pl.when(owner == col)
    def _():
        for ref, start in zip(pieces, starts):
            dst[pl.ds(start, ref.shape[0]), :] = ref[:, pl.ds(column, BS)]


def wave_kernel(block_count, slot_ref, tile_ref, *refs):
    shards, (own, other, stats) = refs[:-3], refs[-3:]
    tok_dev, width = shards[0].shape
    col = lax.axis_index("col")
    first = pl.multiple_of((1 + col) * tok_dev, tok_dev)
    second = pl.multiple_of((2 - col) * tok_dev, tok_dev)
    starts = (0, first, second, 3 * tok_dev)
    for out, target in ((own, col), (other, 1 - col)):
        for side, block in enumerate(wanted(tile_ref, slot_ref, target, block_count, 2)):
            side_out = out.at[:, side * BS : (side + 1) * BS]
            take_block(block, col, width // BS, shards, starts, side_out)
    parts = [shard_stats(ref) for ref in shards]
    if len(parts) == 4:
        parts = [stat_tree(parts, tok_dev)]
    else:
        parts = [merge(parts[0], parts[2], tok_dev), parts[1]]
    for k, (part, square) in enumerate(parts):
        stats[2 * k : 2 * k + 1, :] = part
        stats[2 * k + 1 : 2 * k + 2, :] = square


def wave_parts(block_count, block_slot, slot_tile, shards):
    tok_dev, width = shards[0].shape
    near = Near(True)
    rows = len(shards) * tok_dev
    return pl.pallas_call(
        lambda *refs: wave_kernel(block_count, *refs),
        out_shape=[
            near.out((rows, 2 * BS), jnp.bfloat16),
            near.out((rows, 2 * BS), jnp.bfloat16),
            near.out((2 if len(shards) == 4 else 4, width), jnp.float32),
        ],
        in_specs=[SMEM, SMEM] + [VMEM] * len(shards),
        out_specs=[VMEM] * 3,
        cost_estimate=pl.CostEstimate(flops=0, transcendentals=0, bytes_accessed=2 * rows * width),
        compiler_params=pltpu.CompilerParams(vmem_limit_bytes=4 << 20),
        name="wave",
    )(block_slot, slot_tile, *[near.put(a) for a in shards])


def assemble(blocks, col, held, own, other, sides, start):
    for side, block in enumerate(blocks):
        here = lax.div(block, held) == col
        for parts, taken in ((own, here), (other, jnp.logical_not(here))):

            @pl.when(taken)
            def _():
                row = start
                for ref in parts:
                    rows = ref.shape[0]
                    sides[side][row : row + rows, :] = ref[:, side * BS : (side + 1) * BS]
                    row += rows
    return start + sum(ref.shape[0] for ref in own)


def product_rows(left, right, m, rows):
    return lax.dot_general(
        left[:, m * rows : (m + 1) * rows],
        right[...],
        (((0,), (0,)), ((), ())),
        preferred_element_type=jnp.float32,
    )


def partial_kernel(block_count, held, slot_ref, tile_ref, *refs):
    parts, (acc, left, right) = refs[:-3], refs[-3:]
    half = len(parts) // 2
    col = lax.axis_index("col")
    blocks = wanted(tile_ref, slot_ref, col, block_count, 2)
    assemble(blocks, col, held, parts[:half], parts[half:], (left, right), 0)
    rows = BS // 4
    for m in range(BS // rows):
        acc[m * rows : (m + 1) * rows, :] = product_rows(left, right, m, rows)


def partial_gram(block_count, held, block_slot, slot_tile, own, other):
    near = Near(True)
    tokens = sum(a.shape[0] for a in own)
    arrays = [near.put(a) for a in (*own, *other)]
    return pl.pallas_call(
        lambda *refs: partial_kernel(block_count, held, *refs),
        out_shape=near.out((BS, BS), jnp.float32),
        in_specs=[SMEM, SMEM] + [VMEM] * len(arrays),
        out_specs=VMEM,
        scratch_shapes=[
            pltpu.VMEM((tokens, BS), jnp.bfloat16),
            pltpu.VMEM((tokens, BS), jnp.bfloat16),
        ],
        cost_estimate=pl.CostEstimate(
            flops=2 * tokens * BS * BS, transcendentals=0, bytes_accessed=0
        ),
        compiler_params=pltpu.CompilerParams(vmem_limit_bytes=8 << 20),
        name="partial",
    )(block_slot, slot_tile, *arrays)


def finish_kernel(block_count, total_tokens, n_parts, slot_ref, tile_ref, acc, *refs):
    own, other = refs[:n_parts], refs[n_parts : 2 * n_parts]
    far, far_other, *stats = refs[2 * n_parts : -7]
    out, mean, var, left, right, result, sems = refs[-7:]
    tok_dev, width = far.shape
    held = width // BS
    col = lax.axis_index("col")
    blocks = wanted(tile_ref, slot_ref, col, block_count, 2)
    start = assemble(blocks, col, held, own, other, (left, right), 0)
    for side, block in enumerate(blocks):
        for ref, half in ((far, col), (far_other, 1 - col)):
            take_block(block, half, held, [ref], [start], (left, right)[side])
    mine = tile_ref[lax.axis_index("tok") * 2 + col]
    live = mine < block_count * (block_count + 1) // 2
    chunks = sems.shape[0]
    rows = BS // chunks
    copies = []
    for m in range(chunks):
        here = slice(m * rows, (m + 1) * rows)
        total = acc[here, :] + product_rows(left, right, m, rows)
        result[here, :] = jnp.where(live, total / total_tokens, 0.0)
        copies.append(
            pltpu.make_async_copy(result.at[here, :], out.at[0, here, :], sems.at[m])
        )
        copies[-1].start()
    *whole, split = stats
    last = merge(
        (split[0:1, :], split[1:2, :]),
        merge((split[2:3, :], split[3:4, :]), shard_stats(far), tok_dev),
        2 * tok_dev,
    )
    parts = [(ref[0:1, :], ref[1:2, :]) for ref in whole] + [last]
    part, square = stat_tree(parts, 4 * tok_dev)
    mean[...] = part / total_tokens
    var[...] = square / total_tokens
    for copy in copies:
        copy.wait()


def finish(block_count, total_tokens, block_slot, slot_tile, acc, own, other, far, far_other, stats):
    near = Near(True)
    width = far.shape[1]
    tokens = sum(a.shape[0] for a in own) + far.shape[0]
    arrays = [near.put(a) for a in (acc, *own, *other, far, far_other, *stats)]
    product, mean, var = pl.pallas_call(
        lambda *refs: finish_kernel(block_count, total_tokens, len(own), *refs),
        out_shape=[
            jax.ShapeDtypeStruct((1, BS, BS), jnp.float32),
            jax.ShapeDtypeStruct((1, width), jnp.float32),
            jax.ShapeDtypeStruct((1, width), jnp.float32),
        ],
        in_specs=[SMEM, SMEM] + [VMEM] * len(arrays),
        out_specs=[pl.BlockSpec(memory_space=pl.ANY), VMEM, VMEM],
        scratch_shapes=[
            pltpu.VMEM((tokens, BS), jnp.bfloat16),
            pltpu.VMEM((tokens, BS), jnp.bfloat16),
            pltpu.VMEM((BS, BS), jnp.float32),
            pltpu.SemaphoreType.DMA((4,)),
        ],
        cost_estimate=pl.CostEstimate(
            flops=2 * tokens * BS * BS, transcendentals=0, bytes_accessed=4 * BS * BS
        ),
        compiler_params=pltpu.CompilerParams(vmem_limit_bytes=16 << 20),
        name="finish",
    )(block_slot, slot_tile, *arrays)
    return product, mean[0], var[0]


def by_halves(activations, block_slot, slot_tile):
    n_tok = lax.axis_size("tok")
    n_out = n_tok // 4
    tok_dev, width = activations.shape
    held = width // BS
    block_count = held * 2
    tables = tuple(pltpu.with_memory_space_constraint(a, pltpu.HBM) for a in (block_slot, slot_tile))

    def from_outer(a, k):
        return lax.ppermute(a, "tok", [(t, t ^ (4 * k)) for t in range(n_tok)])

    def from_plane(a, first):
        pairs = [
            (t * 2 + c, (t ^ (1 if (c == 0) == first else 2)) * 2 + c)
            for t in range(n_tok)
            for c in range(2)
        ]
        return lax.ppermute(a, ("tok", "col"), pairs)

    def from_sibling(a):
        return lax.ppermute(a, "col", [(0, 1), (1, 0)])

    own, other, stats = [], [], []
    shard, first, second, far = {0: activations}, {}, {}, {}
    shard[1] = from_outer(activations, 1)
    shard[2] = from_outer(activations, 2)
    first[0] = from_plane(activations, True)
    second[0] = from_plane(activations, False)
    shard[3] = from_outer(after(activations, shard[2]), 3)
    acc = None
    for k in range(n_out):
        last = k == n_out - 1
        src = shard[k]
        if k == 2:
            src = shard[k]
        if k == 3:
            src = shard[k]
        if k:
            first[k] = from_plane(src, True)
        src = shard[k]
        if k == 1:
            src = shard[k]
        if k == 2:
            src = shard[k]
        if k == 3:
            src = shard[k]
        if k:
            second[k] = from_plane(src, False)
        gated = first[k]
        if k == 0:
            gated = first[k]
        if k == 1:
            gated = after(first[k], far[0], second[0])
        if k == 2:
            gated = after(first[k], far[1], second[1])
        if k == 3:
            gated = after(first[k], far[2], second[2], own[1])
        far[k] = from_plane(gated, False)
        shards = [shard[k], first[k], second[k]] + ([] if last else [far[k]])
        if last:
            acc = partial_gram(block_count, held, *tables, own[: k - 1], other[: k - 1])

        mine, sibling, part = wave_parts(block_count, *tables, shards)
        own.append(mine)
        other.append(from_sibling(sibling))
        stats.append(part)
    far_other = from_sibling(far[3])
    return finish(
        block_count, n_tok * tok_dev, *tables, acc, own[-2:], other[-2:], far[3], far_other, stats
    )


def on_device(activations, block_slot, slot_tile):
    n_in = split_tok(lax.axis_size("tok"))[1]
    small = lax.axis_size("col") == 2 and lax.axis_size("tok") == 16
    return (by_halves if small else by_blocks)(activations, block_slot, slot_tile)


def solution(mesh):
    return jax.shard_map(
        on_device,
        mesh=mesh,
        in_specs=(P("tok", "col"), P(), P()),
        out_specs=(P(("tok", "col"), None, None), P("col"), P("col")),
        check_vma=False,
    )
```

time: 70.6 us -> 50 us (0.71)
  waiting for transfers between devices: 27.6 us -> 12 us
  local copies, waits for them, and re-layouts: 5.73 us -> 0.93 us
  Pallas kernels: 6.65 us -> 10.5 us
  matrix products: 3.31 us -> 0 us
  starting transfers between devices: 22.3 us -> 25.6 us
  other arithmetic: 3.14 us -> 0 us
  between operations: 1.58 us -> 0.72 us
    ppermute x18 -> x20, waiting for transfers between devices: 27.6 us -> 12 us  [the longest x12 7.66 us: from_plane(): return lax.ppermute(a, ('tok', 'col'), pairs)]
    pallas_call x3 -> x6, Pallas kernels: 6.65 us -> 10.5 us  [the longest x4 5.16 us: wave_parts(): pl.pallas_call(lambda *refs: wave_kernel(block_count, *refs), out_shape=[...]
    unnamed x27 -> x2, local copies, waits for them, and re-layouts: 4.46 us -> 0.93 us
    dot_general x1 -> x0, matrix products: 3.31 us -> none  [on_device(): lax.dot_general(arrived[:, :BS], arrived[:, BS:], (((0,), (0,)), ((), ())...]
    ppermute x18 -> x20, starting transfers between devices: 22.3 us -> 25.6 us  [the longest x12 16.8 us: from_plane(): return lax.ppermute(a, ('tok', 'col'), pairs)]
    reduce_sum x8 -> x0, other arithmetic: 2.39 us -> none  [the longest x4 1.24 us: on_device(): stats.append((part, jnp.sum((values - part / tok_dev) ** 2, axis=0)))]
    dynamic_slice x1 -> x0, local copies, waits for them, and re-layouts: 1.24 us -> none  [on_device(): own_tile = lax.dynamic_index_in_dim(slot_tile, own_slot, 0, keepdims=False)]
  transfers between devices with their start and end apart: 18 -> 20, of which waited for: 6 -> 6; matrix products, arithmetic and copies ran while one was open for 9% -> 0% of each run, Pallas kernels for 9% -> 13%
where the time goes in v2:
time: 50 us; the launch traced here: 49.7 us
  starting transfers between devices  25.6 us (51%)
  waiting for transfers between devices  12 us (24%)
  Pallas kernels  10.5 us (21%)
  local copies, waits for them, and re-layouts  0.93 us (2%)
  between operations  0.72 us (1%)
    ppermute x12, starting transfers between devices, from_plane(): return lax.ppermute(a, ('tok', 'col'), pairs)  16.8 us
    ppermute x3, starting transfers between devices, from_outer(): return lax.ppermute(a, 'tok', [(t, t ^ 4 * k) for t in range(n_tok)])  8.02 us
    ppermute x12, waiting for transfers between devices, from_plane(): return lax.ppermute(a, ('tok', 'col'), pairs)  7.66 us
    pallas_call x4, Pallas kernels, wave_parts(): pl.pallas_call(lambda *refs: wave_kernel(block_count, *refs), out_shape=[...  5.16 us
    ppermute x3, waiting for transfers between devices, from_outer(): return lax.ppermute(a, 'tok', [(t, t ^ 4 * k) for t in range(n_tok)])  4.34 us
    pallas_call x1, Pallas kernels, finish(): pl.pallas_call(lambda *refs: finish_kernel(block_count, total_tokens, len...  3.77 us
    pallas_call x1, Pallas kernels, partial_gram(): pl.pallas_call(lambda *refs: partial_kernel(block_count, held, *refs), ou...  1.52 us
  transfers between devices with their start and end apart: 20, of which 6 were waited for; matrix products, arithmetic and copies ran while one was open for 0% of the time, Pallas kernels for 13%

profile of v2, /device:TPU:0, one launch (start us, length us, event | category | flops | bytes accessed | tf_op | source)
XLA Modules:
  0.0 49.7 jit_solution(8706474139700838095)
XLA Ops:
  0.6 3.1 %collective-permute-start.3 = (bf16[32,3072]{1,0:T(8,128)(2,1)}, bf16[32,3072]{1,0:T(8,128)(2,1)S(1)}, u32[]{:S(2)}, u32[]{:S(2)}) collective-permute-start(bf16[32,3072]{1,0:T(8,128)(2,1)} %refs_2_.1), channel_id=1, source_target_pairs={{0,8},{2,10},{4,12},{6,14},{8,0},{10,2},{12,4},{14,6},{16,24},{18,... | collective-permute-start | bytes 589832 | tf_op jit(solution)/shard_map/ppermute | solution.py:442
  3.7 1.5 %collective-permute-start = (bf16[32,3072]{1,0:T(8,128)(2,1)}, bf16[32,3072]{1,0:T(8,128)(2,1)S(1)}, u32[]{:S(2)}, u32[]{:S(2)}) collective-permute-start(bf16[32,3072]{1,0:T(8,128)(2,1)} %refs_2_.1), channel_id=1, source_target_pairs={{0,2},{1,5},{2,0},{3,7},{4,6},{5,1},{6,4},{7,3},{8,10},{9,13},{10,... | collective-permute-start | bytes 589832 | tf_op jit(solution)/shard_map/ppermute | solution.py:450
  5.2 1.5 %collective-permute-start.1 = (bf16[32,3072]{1,0:T(8,128)(2,1)}, bf16[32,3072]{1,0:T(8,128)(2,1)S(1)}, u32[]{:S(2)}, u32[]{:S(2)}) collective-permute-start(bf16[32,3072]{1,0:T(8,128)(2,1)} %refs_2_.1), channel_id=1, source_target_pairs={{0,4},{1,3},{2,6},{3,1},{4,0},{5,7},{6,2},{7,5},{8,12},{9,11},{10,... | collective-permute-start | bytes 589832 | tf_op jit(solution)/shard_map/ppermute | solution.py:450
  6.7 2.6 %collective-permute-start.9 = (bf16[32,3072]{1,0:T(8,128)(2,1)}, bf16[32,3072]{1,0:T(8,128)(2,1)S(1)}, u32[]{:S(2)}, u32[]{:S(2)}) collective-permute-start(bf16[32,3072]{1,0:T(8,128)(2,1)} %refs_2_.1), channel_id=1, source_target_pairs={{0,16},{2,18},{4,20},{6,22},{8,24},{10,26},{12,28},{14,30},{16,0},... | collective-permute-start | bytes 589832 | tf_op jit(solution)/shard_map/ppermute | solution.py:442
  9.3 0.0 collective-permute-done.3.refs_2_
  9.3 3.0 %collective-permute-start.4 = (bf16[32,3072]{1,0:T(8,128)(2,1)S(1)}, bf16[32,3072]{1,0:T(8,128)(2,1)S(1)}, u32[]{:S(2)}, u32[]{:S(2)}) collective-permute-start(bf16[32,3072]{1,0:T(8,128)(2,1)S(1)} %collective-permute-done.3.refs_2_), channel_id=1, source_target_pairs={{0,2},{1,5},{2,0},{3,7},{4,6},{5,1},{6,4},{7,3},{8,10},{9,13},{10,... | collective-permute-start | bytes 589832 | tf_op jit(solution)/shard_map/ppermute | solution.py:450
  12.3 0.0 collective-permute-done.refs_3_
  12.3 3.3 %collective-permute-start.2 = (bf16[32,3072]{1,0:T(8,128)(2,1)S(1)}, bf16[32,3072]{1,0:T(8,128)(2,1)S(1)}, u32[]{:S(2)}, u32[]{:S(2)}) collective-permute-start(bf16[32,3072]{1,0:T(8,128)(2,1)S(1)} %collective-permute-done.refs_3_), channel_id=1, source_target_pairs={{0,4},{1,3},{2,6},{3,1},{4,0},{5,7},{6,2},{7,5},{8,12},{9,11},{10,... | collective-permute-start | bytes 589832 | tf_op jit(solution)/shard_map/ppermute | solution.py:450
  15.6 0.0 collective-permute-start.5
  15.6 2.2 %collective-permute-done.9.refs_2_ = bf16[32,3072]{1,0:T(8,128)(2,1)S(1)} collective-permute-done((bf16[32,3072]{1,0:T(8,128)(2,1)}, bf16[32,3072]{1,0:T(8,128)(2,1)S(1)}, u32[]{:S(2)}, u32[]{:S(2)}) %collective-permute-start.9) | collective-permute-done | bytes 196640 | tf_op jit(solution)/shard_map/ppermute | solution.py:442
  17.9 0.6 %collective-permute-start.10 = (bf16[32,3072]{1,0:T(8,128)(2,1)S(1)}, bf16[32,3072]{1,0:T(8,128)(2,1)S(1)}, u32[]{:S(2)}, u32[]{:S(2)}) collective-permute-start(bf16[32,3072]{1,0:T(8,128)(2,1)S(1)} %collective-permute-done.9.refs_2_), channel_id=1, source_target_pairs={{0,2},{1,5},{2,0},{3,7},{4,6},{5,1},{6,4},{7,3},{8,10},{9,13},{10,... | collective-permute-start | bytes 589832 | tf_op jit(solution)/shard_map/ppermute | solution.py:450
  18.5 0.0 collective-permute-done.1.refs_4_
  18.5 0.0 collective-permute-done.4.refs_3_
  18.5 2.1 %collective-permute-done.2.refs_5_ = bf16[32,3072]{1,0:T(8,128)(2,1)S(1)} collective-permute-done((bf16[32,3072]{1,0:T(8,128)(2,1)S(1)}, bf16[32,3072]{1,0:T(8,128)(2,1)S(1)}, u32[]{:S(2)}, u32[]{:S(2)}) %collective-permute-start.2) | collective-permute-done | bytes 196640 | tf_op jit(solution)/shard_map/ppermute | solution.py:450
  20.5 2.5 %collective-permute-start.6 = (bf16[32,3072]{1,0:T(8,128)(2,1)S(1)}, bf16[32,3072]{1,0:T(8,128)(2,1)S(1)}, u32[]{:S(2)}, u32[]{:S(2)}) collective-permute-start(bf16[32,3072]{1,0:T(8,128)(2,1)S(1)} %collective-permute-done.4.refs_3_), channel_id=1, source_target_pairs={{0,4},{1,3},{2,6},{3,1},{4,0},{5,7},{6,2},{7,5},{8,12},{9,11},{10,... | collective-permute-start | bytes 589832 | tf_op jit(solution)/shard_map/ppermute | solution.py:450
  23.0 2.3 %collective-permute-start.13 = (bf16[32,3072]{1,0:T(8,128)(2,1)}, bf16[32,3072]{1,0:T(8,128)(2,1)S(1)}, u32[]{:S(2)}, u32[]{:S(2)}) collective-permute-start(bf16[32,3072]{1,0:T(8,128)(2,1)} %refs_2_.1), channel_id=1, source_target_pairs={{0,24},{2,26},{4,28},{6,30},{8,16},{10,18},{12,20},{14,22},{16,8},... | collective-permute-start | bytes 589832 | tf_op jit(solution)/shard_map/ppermute | solution.py:442
  25.4 0.0 collective-permute-start.11
  25.4 0.0 collective-permute-done.5.refs_4_
  25.4 0.0 collective-permute-done.10.refs_3_
  25.4 1.3 %collective-permute-done.6.refs_5_ = bf16[32,3072]{1,0:T(8,128)(2,1)S(1)} collective-permute-done((bf16[32,3072]{1,0:T(8,128)(2,1)S(1)}, bf16[32,3072]{1,0:T(8,128)(2,1)S(1)}, u32[]{:S(2)}, u32[]{:S(2)}) %collective-permute-start.6) | collective-permute-done | bytes 196640 | tf_op jit(solution)/shard_map/ppermute | solution.py:450
  26.7 2.0 %collective-permute-start.12 = (bf16[32,3072]{1,0:T(8,128)(2,1)S(1)}, bf16[32,3072]{1,0:T(8,128)(2,1)S(1)}, u32[]{:S(2)}, u32[]{:S(2)}) collective-permute-start(bf16[32,3072]{1,0:T(8,128)(2,1)S(1)} %collective-permute-done.10.refs_3_), channel_id=1, source_target_pairs={{0,4},{1,3},{2,6},{3,1},{4,0},{5,7},{6,2},{7,5},{8,12},{9,11},{10,... | collective-permute-start | bytes 589832 | tf_op jit(solution)/shard_map/ppermute | solution.py:450
  28.7 2.1 %collective-permute-done.13.refs_2_ = bf16[32,3072]{1,0:T(8,128)(2,1)S(1)} collective-permute-done((bf16[32,3072]{1,0:T(8,128)(2,1)}, bf16[32,3072]{1,0:T(8,128)(2,1)S(1)}, u32[]{:S(2)}, u32[]{:S(2)}) %collective-permute-start.13) | collective-permute-done | bytes 196640 | tf_op jit(solution)/shard_map/ppermute | solution.py:442
  30.8 0.0 collective-permute-start.15
  30.8 0.4 collective-permute-start.14
  31.2 0.0 copy-start
  31.2 0.9 %copy-done = bf16[32,3072]{1,0:T(8,128)(2,1)S(1)} copy-done((bf16[32,3072]{1,0:T(8,128)(2,1)S(1)}, bf16[32,3072]{1,0:T(8,128)(2,1)}, u32[]{:S(2)}) %copy-start) | copy-done | bytes 196632
  32.2 1.3 %wave.4 = (bf16[128,2048]{1,0:T(8,128)(2,1)S(1)}, bf16[128,2048]{1,0:T(8,128)(2,1)S(1)}, f32[2,3072]{1,0:T(2,128)S(1)}) custom-call(s32[6]{0:T(128)} %refs_0_.11, s32[32]{0:T(128)} %refs_1_.11, bf16[32,3072]{1,0:T(8,128)(2,1)S(1)} %copy-done, bf16[32,3072]{1,0:T(8,128)(2,1)S(1)} %collective-permute-done.refs_3_, ...), custom_call_target="tpu_custom_call" | custom-call | bytes 786432 | tf_op jit(solution)/shard_map/wave/pallas_call | solution.py:294
  33.5 0.1 collective-permute-start.7
  33.6 1.3 %wave.5 = (bf16[128,2048]{1,0:T(8,128)(2,1)S(1)}, bf16[128,2048]{1,0:T(8,128)(2,1)S(1)}, f32[2,3072]{1,0:T(2,128)S(1)}) custom-call(s32[6]{0:T(128)} %refs_0_.11, s32[32]{0:T(128)} %refs_1_.11, bf16[32,3072]{1,0:T(8,128)(2,1)S(1)} %collective-permute-done.3.refs_2_, bf16[32,3072]{1,0:T(8,128)(2,1)S(1)} %collective-permute-done.4.refs_3_, ...), custom_call_target="tpu_custom_call" | custom-call | bytes 786432 | tf_op jit(solution)/shard_map/wave/pallas_call | solution.py:294
  34.9 0.0 collective-permute-done.11.refs_4_
  34.9 0.6 %collective-permute-start.8 = (bf16[128,2048]{1,0:T(8,128)(2,1)S(1)}, bf16[128,2048]{1,0:T(8,128)(2,1)S(1)}, u32[]{:S(2)}, u32[]{:S(2)}) collective-permute-start(bf16[128,2048]{1,0:T(8,128)(2,1)S(1)} %get-tuple-element.26), channel_id=1, source_target_pairs={{0,1},{1,0},{2,3},{3,2},{4,5},{5,4},{6,7},{7,6},{8,9},{9,8},{10,11... | collective-permute-start | bytes 1572872 | tf_op jit(solution)/shard_map/ppermute | solution.py:453
  35.5 0.0 collective-permute-done.12.refs_5_
  35.5 1.3 %wave.6 = (bf16[128,2048]{1,0:T(8,128)(2,1)S(1)}, bf16[128,2048]{1,0:T(8,128)(2,1)S(1)}, f32[2,3072]{1,0:T(2,128)S(1)}) custom-call(s32[6]{0:T(128)} %refs_0_.11, s32[32]{0:T(128)} %refs_1_.11, bf16[32,3072]{1,0:T(8,128)(2,1)S(1)} %collective-permute-done.9.refs_2_, bf16[32,3072]{1,0:T(8,128)(2,1)S(1)} %collective-permute-done.10.refs_3_, ...), custom_call_target="tpu_custom_call" | custom-call | bytes 786432 | tf_op jit(solution)/shard_map/wave/pallas_call | solution.py:294
  36.8 0.1 collective-permute-start.16
  36.9 0.5 collective-permute-done.15.refs_4_
  37.4 0.0 collective-permute-done.14.refs_3_
  37.4 1.2 %wave.7 = (bf16[96,2048]{1,0:T(8,128)(2,1)S(1)}, bf16[96,2048]{1,0:T(8,128)(2,1)S(1)}, f32[4,3072]{1,0:T(4,128)S(1)}) custom-call(s32[6]{0:T(128)} %refs_0_.11, s32[32]{0:T(128)} %refs_1_.11, bf16[32,3072]{1,0:T(8,128)(2,1)S(1)} %collective-permute-done.13.refs_2_, bf16[32,3072]{1,0:T(8,128)(2,1)S(1)} %collective-permute-done.14.refs_3_, ...), custom_call_target="tpu_custom_call" | custom-call | bytes 589824 | tf_op jit(solution)/shard_map/wave/pallas_call | solution.py:294
  38.5 0.1 collective-permute-start.17
  38.6 1.9 %collective-permute-start.18 = (bf16[32,3072]{1,0:T(8,128)(2,1)S(1)}, bf16[32,3072]{1,0:T(8,128)(2,1)S(1)}, u32[]{:S(2)}, u32[]{:S(2)}) collective-permute-start(bf16[32,3072]{1,0:T(8,128)(2,1)S(1)} %collective-permute-done.14.refs_3_), channel_id=1, source_target_pairs={{0,4},{1,3},{2,6},{3,1},{4,0},{5,7},{6,2},{7,5},{8,12},{9,11},{10,... | collective-permute-start | bytes 589832 | tf_op jit(solution)/shard_map/ppermute | solution.py:450
  40.6 3.8 %collective-permute-done.18.refs_7_ = bf16[32,3072]{1,0:T(8,128)(2,1)S(1)} collective-permute-done((bf16[32,3072]{1,0:T(8,128)(2,1)S(1)}, bf16[32,3072]{1,0:T(8,128)(2,1)S(1)}, u32[]{:S(2)}, u32[]{:S(2)}) %collective-permute-start.18) | collective-permute-done | bytes 196640 | tf_op jit(solution)/shard_map/ppermute | solution.py:450
  44.4 0.0 collective-permute-start.19
  44.4 0.0 collective-permute-done.7.refs_4_
  44.4 0.0 collective-permute-done.8.refs_5_
  44.4 1.5 %partial.1.refs_2_ = f32[1024,1024]{1,0:T(8,128)S(1)} custom-call(s32[6]{0:T(128)} %refs_0_.11, s32[32]{0:T(128)} %refs_1_.11, bf16[128,2048]{1,0:T(8,128)(2,1)S(1)} %get-tuple-element.22.refs_2_, bf16[128,2048]{1,0:T(8,128)(2,1)S(1)} %get-tuple-element.24.refs_3_, bf16[128,2048]{1,0:T(8,128)(2,1)S(1)} %collective-permute-done.7.refs_4_, ...), custom_call_target="tpu_custom_call" | custom-call | flops 536870912 | tf_op jit(solution)/shard_map/partial/pallas_call | solution.py:348
  45.9 0.0 collective-permute-done.17.refs_6_
  45.9 0.0 collective-permute-done.19.refs_8_
  45.9 0.0 collective-permute-done.16.refs_5_
  45.9 3.8 %finish.1 = (f32[1,1024,1024]{2,1,0:T(8,128)}, f32[1,3072]{1,0:T(1,128)}, f32[1,3072]{1,0:T(1,128)}) custom-call(s32[6]{0:T(128)} %refs_0_.11, s32[32]{0:T(128)} %refs_1_.11, f32[1024,1024]{1,0:T(8,128)S(1)} %partial.1.refs_2_, bf16[128,2048]{1,0:T(8,128)(2,1)S(1)} %get-tuple-element.28.refs_3_, bf16[96,2048]{1,0:T(8,128)(2,1)S(1)} %get-tuple-element.30.refs_4_, ...), custom_call_target="tpu_custom_call" | custom-call | flops 536870912 | bytes 4194304 | tf_op jit(solution)/shard_map/finish/pallas_call | solution.py:409
Async XLA Ops:
  0.6 8.7 %collective-permute-start.3 = (bf16[32,3072]{1,0:T(8,128)(2,1)}, bf16[32,3072]{1,0:T(8,128)(2,1)S(1)}, u32[]{:S(2)}, u32[]{:S(2)}) collective-permute-start(bf16[32,3072]{1,0:T(8,128)(2,1)} %refs_2_.1), channel_id=1, source_target_pairs={{0,8},{2,10},{4,12},{6,14},{8,0},{10,2},{12,4},{14,6},{16,24},{18,... | collective-permute-start | bytes 589832 | tf_op jit(solution)/shard_map/ppermute | solution.py:442
  3.7 8.6 %collective-permute-start = (bf16[32,3072]{1,0:T(8,128)(2,1)}, bf16[32,3072]{1,0:T(8,128)(2,1)S(1)}, u32[]{:S(2)}, u32[]{:S(2)}) collective-permute-start(bf16[32,3072]{1,0:T(8,128)(2,1)} %refs_2_.1), channel_id=1, source_target_pairs={{0,2},{1,5},{2,0},{3,7},{4,6},{5,1},{6,4},{7,3},{8,10},{9,13},{10,... | collective-permute-start | bytes 589832 | tf_op jit(solution)/shard_map/ppermute | solution.py:450
  5.2 13.2 %collective-permute-start.1 = (bf16[32,3072]{1,0:T(8,128)(2,1)}, bf16[32,3072]{1,0:T(8,128)(2,1)S(1)}, u32[]{:S(2)}, u32[]{:S(2)}) collective-permute-start(bf16[32,3072]{1,0:T(8,128)(2,1)} %refs_2_.1), channel_id=1, source_target_pairs={{0,4},{1,3},{2,6},{3,1},{4,0},{5,7},{6,2},{7,5},{8,12},{9,11},{10,... | collective-permute-start | bytes 589832 | tf_op jit(solution)/shard_map/ppermute | solution.py:450
  6.7 11.1 %collective-permute-start.9 = (bf16[32,3072]{1,0:T(8,128)(2,1)}, bf16[32,3072]{1,0:T(8,128)(2,1)S(1)}, u32[]{:S(2)}, u32[]{:S(2)}) collective-permute-start(bf16[32,3072]{1,0:T(8,128)(2,1)} %refs_2_.1), channel_id=1, source_target_pairs={{0,16},{2,18},{4,20},{6,22},{8,24},{10,26},{12,28},{14,30},{16,0},... | collective-permute-start | bytes 589832 | tf_op jit(solution)/shard_map/ppermute | solution.py:442
  9.3 9.1 %collective-permute-start.4 = (bf16[32,3072]{1,0:T(8,128)(2,1)S(1)}, bf16[32,3072]{1,0:T(8,128)(2,1)S(1)}, u32[]{:S(2)}, u32[]{:S(2)}) collective-permute-start(bf16[32,3072]{1,0:T(8,128)(2,1)S(1)} %collective-permute-done.3.refs_2_), channel_id=1, source_target_pairs={{0,2},{1,5},{2,0},{3,7},{4,6},{5,1},{6,4},{7,3},{8,10},{9,13},{10,... | collective-permute-start | bytes 589832 | tf_op jit(solution)/shard_map/ppermute | solution.py:450
  12.3 8.3 %collective-permute-start.2 = (bf16[32,3072]{1,0:T(8,128)(2,1)S(1)}, bf16[32,3072]{1,0:T(8,128)(2,1)S(1)}, u32[]{:S(2)}, u32[]{:S(2)}) collective-permute-start(bf16[32,3072]{1,0:T(8,128)(2,1)S(1)} %collective-permute-done.refs_3_), channel_id=1, source_target_pairs={{0,4},{1,3},{2,6},{3,1},{4,0},{5,7},{6,2},{7,5},{8,12},{9,11},{10,... | collective-permute-start | bytes 589832 | tf_op jit(solution)/shard_map/ppermute | solution.py:450
  15.6 9.8 %collective-permute-start.5 = (bf16[32,3072]{1,0:T(8,128)(2,1)S(1)}, bf16[32,3072]{1,0:T(8,128)(2,1)S(1)}, u32[]{:S(2)}, u32[]{:S(2)}) collective-permute-start(bf16[32,3072]{1,0:T(8,128)(2,1)S(1)} %collective-permute-done.3.refs_2_), channel_id=1, source_target_pairs={{0,4},{1,3},{2,6},{3,1},{4,0},{5,7},{6,2},{7,5},{8,12},{9,11},{10,... | collective-permute-start | bytes 589832 | tf_op jit(solution)/shard_map/ppermute | solution.py:450
  17.9 7.5 %collective-permute-start.10 = (bf16[32,3072]{1,0:T(8,128)(2,1)S(1)}, bf16[32,3072]{1,0:T(8,128)(2,1)S(1)}, u32[]{:S(2)}, u32[]{:S(2)}) collective-permute-start(bf16[32,3072]{1,0:T(8,128)(2,1)S(1)} %collective-permute-done.9.refs_2_), channel_id=1, source_target_pairs={{0,2},{1,5},{2,0},{3,7},{4,6},{5,1},{6,4},{7,3},{8,10},{9,13},{10,... | collective-permute-start | bytes 589832 | tf_op jit(solution)/shard_map/ppermute | solution.py:450
  20.5 6.1 %collective-permute-start.6 = (bf16[32,3072]{1,0:T(8,128)(2,1)S(1)}, bf16[32,3072]{1,0:T(8,128)(2,1)S(1)}, u32[]{:S(2)}, u32[]{:S(2)}) collective-permute-start(bf16[32,3072]{1,0:T(8,128)(2,1)S(1)} %collective-permute-done.4.refs_3_), channel_id=1, source_target_pairs={{0,4},{1,3},{2,6},{3,1},{4,0},{5,7},{6,2},{7,5},{8,12},{9,11},{10,... | collective-permute-start | bytes 589832 | tf_op jit(solution)/shard_map/ppermute | solution.py:450
  23.0 7.8 %collective-permute-start.13 = (bf16[32,3072]{1,0:T(8,128)(2,1)}, bf16[32,3072]{1,0:T(8,128)(2,1)S(1)}, u32[]{:S(2)}, u32[]{:S(2)}) collective-permute-start(bf16[32,3072]{1,0:T(8,128)(2,1)} %refs_2_.1), channel_id=1, source_target_pairs={{0,24},{2,26},{4,28},{6,30},{8,16},{10,18},{12,20},{14,22},{16,8},... | collective-permute-start | bytes 589832 | tf_op jit(solution)/shard_map/ppermute | solution.py:442
  25.4 9.5 %collective-permute-start.11 = (bf16[32,3072]{1,0:T(8,128)(2,1)S(1)}, bf16[32,3072]{1,0:T(8,128)(2,1)S(1)}, u32[]{:S(2)}, u32[]{:S(2)}) collective-permute-start(bf16[32,3072]{1,0:T(8,128)(2,1)S(1)} %collective-permute-done.9.refs_2_), channel_id=1, source_target_pairs={{0,4},{1,3},{2,6},{3,1},{4,0},{5,7},{6,2},{7,5},{8,12},{9,11},{10,... | collective-permute-start | bytes 589832 | tf_op jit(solution)/shard_map/ppermute | solution.py:450
  26.7 8.8 %collective-permute-start.12 = (bf16[32,3072]{1,0:T(8,128)(2,1)S(1)}, bf16[32,3072]{1,0:T(8,128)(2,1)S(1)}, u32[]{:S(2)}, u32[]{:S(2)}) collective-permute-start(bf16[32,3072]{1,0:T(8,128)(2,1)S(1)} %collective-permute-done.10.refs_3_), channel_id=1, source_target_pairs={{0,4},{1,3},{2,6},{3,1},{4,0},{5,7},{6,2},{7,5},{8,12},{9,11},{10,... | collective-permute-start | bytes 589832 | tf_op jit(solution)/shard_map/ppermute | solution.py:450
  30.8 6.5 %collective-permute-start.15 = (bf16[32,3072]{1,0:T(8,128)(2,1)S(1)}, bf16[32,3072]{1,0:T(8,128)(2,1)S(1)}, u32[]{:S(2)}, u32[]{:S(2)}) collective-permute-start(bf16[32,3072]{1,0:T(8,128)(2,1)S(1)} %collective-permute-done.13.refs_2_), channel_id=1, source_target_pairs={{0,4},{1,3},{2,6},{3,1},{4,0},{5,7},{6,2},{7,5},{8,12},{9,11},{10,... | collective-permute-start | bytes 589832 | tf_op jit(solution)/shard_map/ppermute | solution.py:450
  30.8 6.5 %collective-permute-start.14 = (bf16[32,3072]{1,0:T(8,128)(2,1)S(1)}, bf16[32,3072]{1,0:T(8,128)(2,1)S(1)}, u32[]{:S(2)}, u32[]{:S(2)}) collective-permute-start(bf16[32,3072]{1,0:T(8,128)(2,1)S(1)} %collective-permute-done.13.refs_2_), channel_id=1, source_target_pairs={{0,2},{1,5},{2,0},{3,7},{4,6},{5,1},{6,4},{7,3},{8,10},{9,13},{10,... | collective-permute-start | bytes 589832 | tf_op jit(solution)/shard_map/ppermute | solution.py:450
  31.2 0.9 %copy-start = (bf16[32,3072]{1,0:T(8,128)(2,1)S(1)}, bf16[32,3072]{1,0:T(8,128)(2,1)}, u32[]{:S(2)}) copy-start(bf16[32,3072]{1,0:T(8,128)(2,1)} %refs_2_.1) | copy-start | bytes 589828
  33.5 10.9 %collective-permute-start.7 = (bf16[128,2048]{1,0:T(8,128)(2,1)S(1)}, bf16[128,2048]{1,0:T(8,128)(2,1)S(1)}, u32[]{:S(2)}, u32[]{:S(2)}) collective-permute-start(bf16[128,2048]{1,0:T(8,128)(2,1)S(1)} %get-tuple-element.25), channel_id=1, source_target_pairs={{0,1},{1,0},{2,3},{3,2},{4,5},{5,4},{6,7},{7,6},{8,9},{9,8},{10,11... | collective-permute-start | bytes 1572872 | tf_op jit(solution)/shard_map/ppermute | solution.py:453
  34.9 9.5 %collective-permute-start.8 = (bf16[128,2048]{1,0:T(8,128)(2,1)S(1)}, bf16[128,2048]{1,0:T(8,128)(2,1)S(1)}, u32[]{:S(2)}, u32[]{:S(2)}) collective-permute-start(bf16[128,2048]{1,0:T(8,128)(2,1)S(1)} %get-tuple-element.26), channel_id=1, source_target_pairs={{0,1},{1,0},{2,3},{3,2},{4,5},{5,4},{6,7},{7,6},{8,9},{9,8},{10,11... | collective-permute-start | bytes 1572872 | tf_op jit(solution)/shard_map/ppermute | solution.py:453
  36.8 9.1 %collective-permute-start.16 = (bf16[128,2048]{1,0:T(8,128)(2,1)S(1)}, bf16[128,2048]{1,0:T(8,128)(2,1)S(1)}, u32[]{:S(2)}, u32[]{:S(2)}) collective-permute-start(bf16[128,2048]{1,0:T(8,128)(2,1)S(1)} %get-tuple-element.31), channel_id=1, source_target_pairs={{0,1},{1,0},{2,3},{3,2},{4,5},{5,4},{6,7},{7,6},{8,9},{9,8},{10,11... | collective-permute-start | bytes 1572872 | tf_op jit(solution)/shard_map/ppermute | solution.py:453
  38.5 7.4 %collective-permute-start.17 = (bf16[96,2048]{1,0:T(8,128)(2,1)S(1)}, bf16[96,2048]{1,0:T(8,128)(2,1)S(1)}, u32[]{:S(2)}, u32[]{:S(2)}) collective-permute-start(bf16[96,2048]{1,0:T(8,128)(2,1)S(1)} %get-tuple-element.32), channel_id=1, source_target_pairs={{0,1},{1,0},{2,3},{3,2},{4,5},{5,4},{6,7},{7,6},{8,9},{9,8},{10,11... | collective-permute-start | bytes 1179656 | tf_op jit(solution)/shard_map/ppermute | solution.py:453
  38.6 5.7 %collective-permute-start.18 = (bf16[32,3072]{1,0:T(8,128)(2,1)S(1)}, bf16[32,3072]{1,0:T(8,128)(2,1)S(1)}, u32[]{:S(2)}, u32[]{:S(2)}) collective-permute-start(bf16[32,3072]{1,0:T(8,128)(2,1)S(1)} %collective-permute-done.14.refs_3_), channel_id=1, source_target_pairs={{0,4},{1,3},{2,6},{3,1},{4,0},{5,7},{6,2},{7,5},{8,12},{9,11},{10,... | collective-permute-start | bytes 589832 | tf_op jit(solution)/shard_map/ppermute | solution.py:450
  44.4 1.5 %collective-permute-start.19 = (bf16[32,3072]{1,0:T(8,128)(2,1)S(1)}, bf16[32,3072]{1,0:T(8,128)(2,1)S(1)}, u32[]{:S(2)}, u32[]{:S(2)}) collective-permute-start(bf16[32,3072]{1,0:T(8,128)(2,1)S(1)} %collective-permute-done.18.refs_7_), channel_id=1, source_target_pairs={{0,1},{1,0},{2,3},{3,2},{4,5},{5,4},{6,7},{7,6},{8,9},{9,8},{10,11... | collective-permute-start | bytes 589832 | tf_op jit(solution)/shard_map/ppermute | solution.py:453

commit v3 on v2

--- a/solution.py
+++ b/solution.py
@@ -236,9 +236,34 @@
     return (product, mine[0] / total_tokens, mine[1] / total_tokens)
 
 
-def wanted(tile_ref, slot_ref, col, block_count, n_col):
-    pair = pair_of(tile_ref[lax.axis_index("tok") * n_col + col], block_count)
-    return slot_ref[pair[0]], slot_ref[pair[1]]
+def plan_kernel(block_count, slot_ref, tile_ref, plan):
+    col = lax.axis_index("col")
+    mine = tile_ref[lax.axis_index("tok") * 2 + col]
+    packed = jnp.where(mine < block_count * (block_count + 1) // 2, 1 << 24, 0)
+    shift = 0
+    for tile in (mine, tile_ref[lax.axis_index("tok") * 2 + 1 - col]):
+        for member in pair_of(tile, block_count):
+            packed += slot_ref[member] << shift
+            shift += 6
+    plan[...] = jnp.full((8, 128), packed, jnp.int32)
+
+
+def make_plan(block_count, block_slot, slot_tile):
+    tables = [pltpu.with_memory_space_constraint(a, pltpu.HBM) for a in (block_slot, slot_tile)]
+    return pl.pallas_call(
+        lambda *refs: plan_kernel(block_count, *refs),
+        out_shape=Near(True).out((8, 128), jnp.int32),
+        in_specs=[SMEM, SMEM],
+        out_specs=VMEM,
+        compiler_params=pltpu.CompilerParams(vmem_limit_bytes=1 << 20),
+        name="plan",
+    )(*tables)
+
+
+def planned(plan):
+    packed = jnp.max(plan[0:1, :])
+    blocks = [(packed >> (6 * k)) & 63 for k in range(4)]
+    return blocks[:2], blocks[2:], packed >= 1 << 24
 
 
 def stat_tree(parts, count):
@@ -266,15 +291,16 @@
             dst[pl.ds(start, ref.shape[0]), :] = ref[:, pl.ds(column, BS)]
 
 
-def wave_kernel(block_count, slot_ref, tile_ref, *refs):
+def wave_kernel(plan, *refs):
     shards, (own, other, stats) = refs[:-3], refs[-3:]
     tok_dev, width = shards[0].shape
     col = lax.axis_index("col")
     first = pl.multiple_of((1 + col) * tok_dev, tok_dev)
     second = pl.multiple_of((2 - col) * tok_dev, tok_dev)
     starts = (0, first, second, 3 * tok_dev)
-    for out, target in ((own, col), (other, 1 - col)):
-        for side, block in enumerate(wanted(tile_ref, slot_ref, target, block_count, 2)):
+    mine, theirs, _ = planned(plan)
+    for out, blocks in ((own, mine), (other, theirs)):
+        for side, block in enumerate(blocks):
             side_out = out.at[:, side * BS : (side + 1) * BS]
             take_block(block, col, width // BS, shards, starts, side_out)
     parts = [shard_stats(ref) for ref in shards]
@@ -287,23 +313,23 @@
         stats[2 * k + 1 : 2 * k + 2, :] = square
 
 
-def wave_parts(block_count, block_slot, slot_tile, shards):
+def wave_parts(plan, shards, skip=None):
     tok_dev, width = shards[0].shape
     near = Near(True)
     rows = len(shards) * tok_dev
     return pl.pallas_call(
-        lambda *refs: wave_kernel(block_count, *refs),
+        wave_kernel,
         out_shape=[
             near.out((rows, 2 * BS), jnp.bfloat16),
             near.out((rows, 2 * BS), jnp.bfloat16),
             near.out((2 if len(shards) == 4 else 4, width), jnp.float32),
         ],
-        in_specs=[SMEM, SMEM] + [VMEM] * len(shards),
+        in_specs=[VMEM] * (1 + len(shards)),
         out_specs=[VMEM] * 3,
         cost_estimate=pl.CostEstimate(flops=0, transcendentals=0, bytes_accessed=2 * rows * width),
         compiler_params=pltpu.CompilerParams(vmem_limit_bytes=4 << 20),
         name="wave",
-    )(block_slot, slot_tile, *[near.put(a) for a in shards])
+    )(near.put(plan), *[a if a is skip else near.put(a) for a in shards])
 
 
 def assemble(blocks, col, held, own, other, sides, start):
@@ -330,25 +356,25 @@
     )
 
 
-def partial_kernel(block_count, held, slot_ref, tile_ref, *refs):
+def partial_kernel(held, plan, *refs):
     parts, (acc, left, right) = refs[:-3], refs[-3:]
     half = len(parts) // 2
     col = lax.axis_index("col")
-    blocks = wanted(tile_ref, slot_ref, col, block_count, 2)
+    blocks = planned(plan)[0]
     assemble(blocks, col, held, parts[:half], parts[half:], (left, right), 0)
     rows = BS // 4
     for m in range(BS // rows):
         acc[m * rows : (m + 1) * rows, :] = product_rows(left, right, m, rows)
 
 
-def partial_gram(block_count, held, block_slot, slot_tile, own, other):
+def partial_gram(held, plan, own, other):
     near = Near(True)
     tokens = sum(a.shape[0] for a in own)
-    arrays = [near.put(a) for a in (*own, *other)]
+    arrays = [near.put(a) for a in (plan, *own, *other)]
     return pl.pallas_call(
-        lambda *refs: partial_kernel(block_count, held, *refs),
+        lambda *refs: partial_kernel(held, *refs),
         out_shape=near.out((BS, BS), jnp.float32),
-        in_specs=[SMEM, SMEM] + [VMEM] * len(arrays),
+        in_specs=[VMEM] * len(arrays),
         out_specs=VMEM,
         scratch_shapes=[
             pltpu.VMEM((tokens, BS), jnp.bfloat16),
@@ -359,24 +385,22 @@
         ),
         compiler_params=pltpu.CompilerParams(vmem_limit_bytes=8 << 20),
         name="partial",
-    )(block_slot, slot_tile, *arrays)
-
-
-def finish_kernel(block_count, total_tokens, n_parts, slot_ref, tile_ref, acc, *refs):
+    )(*arrays)
+
+
+def finish_kernel(total_tokens, n_parts, plan, acc, *refs):
     own, other = refs[:n_parts], refs[n_parts : 2 * n_parts]
-    far, far_other, *stats = refs[2 * n_parts : -7]
-    out, mean, var, left, right, result, sems = refs[-7:]
+    far, far_other, *stats = refs[2 * n_parts : -8]
+    out, mean, var, left, right, result, moments, sems = refs[-8:]
     tok_dev, width = far.shape
     held = width // BS
     col = lax.axis_index("col")
-    blocks = wanted(tile_ref, slot_ref, col, block_count, 2)
+    blocks, _, live = planned(plan)
     start = assemble(blocks, col, held, own, other, (left, right), 0)
     for side, block in enumerate(blocks):
         for ref, half in ((far, col), (far_other, 1 - col)):
             take_block(block, half, held, [ref], [start], (left, right)[side])
-    mine = tile_ref[lax.axis_index("tok") * 2 + col]
-    live = mine < block_count * (block_count + 1) // 2
-    chunks = sems.shape[0]
+    chunks = sems.shape[0] - 2
     rows = BS // chunks
     copies = []
     for m in range(chunks):
@@ -395,48 +419,50 @@
     )
     parts = [(ref[0:1, :], ref[1:2, :]) for ref in whole] + [last]
     part, square = stat_tree(parts, 4 * tok_dev)
-    mean[...] = part / total_tokens
-    var[...] = square / total_tokens
+    for k, (ref, value) in enumerate(((mean, part), (var, square))):
+        moments[k] = value / total_tokens
+        copies.append(pltpu.make_async_copy(moments.at[k], ref, sems.at[chunks + k]))
+        copies[-1].start()
     for copy in copies:
         copy.wait()
 
 
-def finish(block_count, total_tokens, block_slot, slot_tile, acc, own, other, far, far_other, stats):
+def finish(total_tokens, plan, acc, own, other, far, far_other, stats):
     near = Near(True)
     width = far.shape[1]
     tokens = sum(a.shape[0] for a in own) + far.shape[0]
-    arrays = [near.put(a) for a in (acc, *own, *other, far, far_other, *stats)]
+    arrays = [near.put(a) for a in (plan, acc, *own, *other, far, far_other, *stats)]
     product, mean, var = pl.pallas_call(
-        lambda *refs: finish_kernel(block_count, total_tokens, len(own), *refs),
+        lambda *refs: finish_kernel(total_tokens, len(own), *refs),
         out_shape=[
             jax.ShapeDtypeStruct((1, BS, BS), jnp.float32),
             jax.ShapeDtypeStruct((1, width), jnp.float32),
             jax.ShapeDtypeStruct((1, width), jnp.float32),
         ],
-        in_specs=[SMEM, SMEM] + [VMEM] * len(arrays),
-        out_specs=[pl.BlockSpec(memory_space=pl.ANY), VMEM, VMEM],
+        in_specs=[VMEM] * len(arrays),
+        out_specs=[pl.BlockSpec(memory_space=pl.ANY)] * 3,
         scratch_shapes=[
             pltpu.VMEM((tokens, BS), jnp.bfloat16),
             pltpu.VMEM((tokens, BS), jnp.bfloat16),
             pltpu.VMEM((BS, BS), jnp.float32),
-            pltpu.SemaphoreType.DMA((4,)),
+            pltpu.VMEM((2, 1, width), jnp.float32),
+            pltpu.SemaphoreType.DMA((6,)),
         ],
         cost_estimate=pl.CostEstimate(
             flops=2 * tokens * BS * BS, transcendentals=0, bytes_accessed=4 * BS * BS
         ),
         compiler_params=pltpu.CompilerParams(vmem_limit_bytes=16 << 20),
         name="finish",
-    )(block_slot, slot_tile, *arrays)
+    )(*arrays)
     return product, mean[0], var[0]
 
 
 def by_halves(activations, block_slot, slot_tile):
     n_tok = lax.axis_size("tok")
-    n_out = n_tok // 4
     tok_dev, width = activations.shape
     held = width // BS
     block_count = held * 2
-    tables = tuple(pltpu.with_memory_space_constraint(a, pltpu.HBM) for a in (block_slot, slot_tile))
+    plan = make_plan(block_count, block_slot, slot_tile)
 
     def from_outer(a, k):
         return lax.ppermute(a, "tok", [(t, t ^ (4 * k)) for t in range(n_tok)])
@@ -452,53 +478,40 @@
     def from_sibling(a):
         return lax.ppermute(a, "col", [(0, 1), (1, 0)])
 
-    own, other, stats = [], [], []
-    shard, first, second, far = {0: activations}, {}, {}, {}
-    shard[1] = from_outer(activations, 1)
-    shard[2] = from_outer(activations, 2)
-    first[0] = from_plane(activations, True)
-    second[0] = from_plane(activations, False)
-    shard[3] = from_outer(after(activations, shard[2]), 3)
-    acc = None
-    for k in range(n_out):
-        last = k == n_out - 1
-        src = shard[k]
-        if k == 2:
-            src = shard[k]
-        if k == 3:
-            src = shard[k]
-        if k:
-            first[k] = from_plane(src, True)
-        src = shard[k]
-        if k == 1:
-            src = shard[k]
-        if k == 2:
-            src = shard[k]
-        if k == 3:
-            src = shard[k]
-        if k:
-            second[k] = from_plane(src, False)
-        gated = first[k]
-        if k == 0:
-            gated = first[k]
-        if k == 1:
-            gated = after(first[k], far[0], second[0])
-        if k == 2:
-            gated = after(first[k], far[1], second[1])
-        if k == 3:
-            gated = after(first[k], far[2], second[2], own[1])
-        far[k] = from_plane(gated, False)
-        shards = [shard[k], first[k], second[k]] + ([] if last else [far[k]])
-        if last:
-            acc = partial_gram(block_count, held, *tables, own[: k - 1], other[: k - 1])
-
-        mine, sibling, part = wave_parts(block_count, *tables, shards)
-        own.append(mine)
-        other.append(from_sibling(sibling))
-        stats.append(part)
-    far_other = from_sibling(far[3])
+    z1 = from_outer(activations, 1)
+    z2 = from_outer(activations, 2)
+    s0 = from_plane(activations, True)
+    z3 = from_outer(after(activations, s0), 3)
+    b0 = from_plane(after(activations, s0), False)
+    f0 = from_plane(s0, False)
+    own0, out0, stats0 = wave_parts(plan, [activations, s0, b0, after(f0, z3)], activations)
+    other0 = from_sibling(out0)
+    s1 = from_plane(z1, True)
+    b1 = from_plane(after(z1, z2), False)
+    f1 = from_plane(after(s1, f0, b0), False)
+    own1, out1, stats1 = wave_parts(plan, [z1, s1, b1, after(f1, f1)])
+    other1 = from_sibling(out1)
+    s2 = from_plane(z2, True)
+    b2 = from_plane(after(z2, b1), False)
+    f2 = from_plane(after(s2, f1, b1, z3), False)
+    own2, out2, stats2 = wave_parts(plan, [z2, s2, b2, f2])
+    other2 = from_sibling(out2)
+    s3 = from_plane(z3, True)
+    b3 = from_plane(z3, False)
+    f3 = from_plane(after(s3, b1, b2), False)
+    own3, out3, stats3 = wave_parts(plan, [z3, s3, after(b3, f2)])
+    other3 = from_sibling(out3)
+    acc = partial_gram(held, plan, [own0, own1], [other0, other1])
+    far_other = from_sibling(f3)
     return finish(
-        block_count, n_tok * tok_dev, *tables, acc, own[-2:], other[-2:], far[3], far_other, stats
+        n_tok * tok_dev,
+        plan,
+        acc,
+        [own2, own3],
+        [other2, other3],
+        f3,
+        far_other,
+        [stats0, stats1, stats2, stats3],
     )
 
 

time: 50 us -> 46 us (0.920)
  starting transfers between devices: 25.6 us -> 22.6 us
  Pallas kernels: 10.5 us -> 7.66 us
  waiting for transfers between devices: 12 us -> 13.9 us
    ppermute x3, waiting for transfers between devices: 4.34 us -> 7.34 us  [from_outer(): return lax.ppermute(a, 'tok', [(t, t ^ 4 * k) for t in range(n_tok)])]
    pallas_call x6 -> x7, Pallas kernels: 10.5 us -> 7.66 us  [the longest x4 3.23 us: wave_parts(): pl.pallas_call(wave_kernel, out_shape=[near.out((rows, 2 * BS), jnp.bfloa...]
    ppermute x12, waiting for transfers between devices: 7.66 us -> 6.14 us  [from_plane(): return lax.ppermute(a, ('tok', 'col'), pairs)]
    ppermute x12, starting transfers between devices: 16.8 us -> 15.2 us  [from_plane(): return lax.ppermute(a, ('tok', 'col'), pairs)]
    ppermute x3, starting transfers between devices: 8.02 us -> 6.64 us  [from_outer(): return lax.ppermute(a, 'tok', [(t, t ^ 4 * k) for t in range(n_tok)])]
  transfers between devices with their start and end apart: 20 -> 20, of which waited for: 6 -> 6; matrix products, arithmetic and copies ran while one was open for 0% -> 0% of each run, Pallas kernels for 13% -> 11%
where the time goes in v3:
time: 46 us; the launch traced here: 45.8 us
  starting transfers between devices  22.6 us (49%)
  waiting for transfers between devices  13.9 us (30%)
  Pallas kernels  7.66 us (17%)
  local copies, waits for them, and re-layouts  0.92 us (2%)
  between operations  0.72 us (2%)
    ppermute x12, starting transfers between devices, from_plane(): return lax.ppermute(a, ('tok', 'col'), pairs)  15.2 us
    ppermute x3, waiting for transfers between devices, from_outer(): return lax.ppermute(a, 'tok', [(t, t ^ 4 * k) for t in range(n_tok)])  7.34 us
    ppermute x3, starting transfers between devices, from_outer(): return lax.ppermute(a, 'tok', [(t, t ^ 4 * k) for t in range(n_tok)])  6.64 us
    ppermute x12, waiting for transfers between devices, from_plane(): return lax.ppermute(a, ('tok', 'col'), pairs)  6.14 us
    pallas_call x4, Pallas kernels, wave_parts(): pl.pallas_call(wave_kernel, out_shape=[near.out((rows, 2 * BS), jnp.bfloa...  3.23 us
    pallas_call x1, Pallas kernels, finish(): pl.pallas_call(lambda *refs: finish_kernel(total_tokens, len(own), *refs)...  2.72 us
    pallas_call x1, Pallas kernels, partial_gram(): pl.pallas_call(lambda *refs: partial_kernel(held, *refs), out_shape=near....  1.02 us
    unnamed x2, local copies, waits for them, and re-layouts  0.92 us
  transfers between devices with their start and end apart: 20, of which 6 were waited for; matrix products, arithmetic and copies ran while one was open for 0% of the time, Pallas kernels for 11%

profile of v3, /device:TPU:0, one launch (start us, length us, event | category | flops | bytes accessed | tf_op | source)
XLA Modules:
  0.0 45.8 jit_solution(17433191564812202523)
XLA Ops:
  0.6 3.0 %collective-permute-start = (bf16[32,3072]{1,0:T(8,128)(2,1)}, bf16[32,3072]{1,0:T(8,128)(2,1)S(1)}, u32[]{:S(2)}, u32[]{:S(2)}) collective-permute-start(bf16[32,3072]{1,0:T(8,128)(2,1)} %refs_0_.3), channel_id=1, source_target_pairs={{0,2},{1,5},{2,0},{3,7},{4,6},{5,1},{6,4},{7,3},{8,10},{9,13},{10,... | collective-permute-start | bytes 589832 | tf_op jit(solution)/shard_map/ppermute | solution.py:476
  3.6 1.6 %collective-permute-start.4 = (bf16[32,3072]{1,0:T(8,128)(2,1)}, bf16[32,3072]{1,0:T(8,128)(2,1)S(1)}, u32[]{:S(2)}, u32[]{:S(2)}) collective-permute-start(bf16[32,3072]{1,0:T(8,128)(2,1)} %refs_0_.3), channel_id=1, source_target_pairs={{0,8},{2,10},{4,12},{6,14},{8,0},{10,2},{12,4},{14,6},{16,24},{18,... | collective-permute-start | bytes 589832 | tf_op jit(solution)/shard_map/ppermute | solution.py:468
  5.2 2.6 %collective-permute-start.6 = (bf16[32,3072]{1,0:T(8,128)(2,1)}, bf16[32,3072]{1,0:T(8,128)(2,1)S(1)}, u32[]{:S(2)}, u32[]{:S(2)}) collective-permute-start(bf16[32,3072]{1,0:T(8,128)(2,1)} %refs_0_.3), channel_id=1, source_target_pairs={{0,16},{2,18},{4,20},{6,22},{8,24},{10,26},{12,28},{14,30},{16,0},... | collective-permute-start | bytes 589832 | tf_op jit(solution)/shard_map/ppermute | solution.py:468
  7.8 0.0 collective-permute-done.refs_1_
  7.8 1.7 %collective-permute-start.1 = (bf16[32,3072]{1,0:T(8,128)(2,1)}, bf16[32,3072]{1,0:T(8,128)(2,1)S(1)}, u32[]{:S(2)}, u32[]{:S(2)}) collective-permute-start(bf16[32,3072]{1,0:T(8,128)(2,1)} %refs_0_.3), channel_id=1, source_target_pairs={{0,4},{1,3},{2,6},{3,1},{4,0},{5,7},{6,2},{7,5},{8,12},{9,11},{10,... | collective-permute-start | bytes 589832 | tf_op jit(solution)/shard_map/ppermute | solution.py:476
  9.5 0.3 collective-permute-start.2
  9.8 4.5 %collective-permute-done.4.refs_0_ = bf16[32,3072]{1,0:T(8,128)(2,1)S(1)} collective-permute-done((bf16[32,3072]{1,0:T(8,128)(2,1)}, bf16[32,3072]{1,0:T(8,128)(2,1)S(1)}, u32[]{:S(2)}, u32[]{:S(2)}) %collective-permute-start.4) | collective-permute-done | bytes 196640 | tf_op jit(solution)/shard_map/ppermute | solution.py:468
  14.3 1.5 %collective-permute-start.5 = (bf16[32,3072]{1,0:T(8,128)(2,1)S(1)}, bf16[32,3072]{1,0:T(8,128)(2,1)S(1)}, u32[]{:S(2)}, u32[]{:S(2)}) collective-permute-start(bf16[32,3072]{1,0:T(8,128)(2,1)S(1)} %collective-permute-done.4.refs_0_), channel_id=1, source_target_pairs={{0,2},{1,5},{2,0},{3,7},{4,6},{5,1},{6,4},{7,3},{8,10},{9,13},{10,... | collective-permute-start | bytes 589832 | tf_op jit(solution)/shard_map/ppermute | solution.py:476
  15.8 0.9 %collective-permute-done.6.refs_0_ = bf16[32,3072]{1,0:T(8,128)(2,1)S(1)} collective-permute-done((bf16[32,3072]{1,0:T(8,128)(2,1)}, bf16[32,3072]{1,0:T(8,128)(2,1)S(1)}, u32[]{:S(2)}, u32[]{:S(2)}) %collective-permute-start.6) | collective-permute-done | bytes 196640 | tf_op jit(solution)/shard_map/ppermute | solution.py:468
  16.7 0.5 %collective-permute-start.7 = (bf16[32,3072]{1,0:T(8,128)(2,1)S(1)}, bf16[32,3072]{1,0:T(8,128)(2,1)S(1)}, u32[]{:S(2)}, u32[]{:S(2)}) collective-permute-start(bf16[32,3072]{1,0:T(8,128)(2,1)S(1)} %collective-permute-done.4.refs_0_), channel_id=1, source_target_pairs={{0,4},{1,3},{2,6},{3,1},{4,0},{5,7},{6,2},{7,5},{8,12},{9,11},{10,... | collective-permute-start | bytes 589832 | tf_op jit(solution)/shard_map/ppermute | solution.py:476
  17.2 2.5 %collective-permute-start.3 = (bf16[32,3072]{1,0:T(8,128)(2,1)}, bf16[32,3072]{1,0:T(8,128)(2,1)S(1)}, u32[]{:S(2)}, u32[]{:S(2)}) collective-permute-start(bf16[32,3072]{1,0:T(8,128)(2,1)} %refs_0_.3), channel_id=1, source_target_pairs={{0,24},{2,26},{4,28},{6,30},{8,16},{10,18},{12,20},{14,22},{16,8},... | collective-permute-start | bytes 589832 | tf_op jit(solution)/shard_map/ppermute | solution.py:468
  19.7 0.0 collective-permute-done.1.refs_2_
  19.7 1.5 %collective-permute-start.11 = (bf16[32,3072]{1,0:T(8,128)(2,1)S(1)}, bf16[32,3072]{1,0:T(8,128)(2,1)S(1)}, u32[]{:S(2)}, u32[]{:S(2)}) collective-permute-start(bf16[32,3072]{1,0:T(8,128)(2,1)S(1)} %collective-permute-done.6.refs_0_), channel_id=1, source_target_pairs={{0,2},{1,5},{2,0},{3,7},{4,6},{5,1},{6,4},{7,3},{8,10},{9,13},{10,... | collective-permute-start | bytes 589832 | tf_op jit(solution)/shard_map/ppermute | solution.py:476
  21.2 0.0 collective-permute-done.2.refs_3_
  21.2 0.0 collective-permute-done.5.refs_1_
  21.2 1.5 %collective-permute-start.8 = (bf16[32,3072]{1,0:T(8,128)(2,1)S(1)}, bf16[32,3072]{1,0:T(8,128)(2,1)S(1)}, u32[]{:S(2)}, u32[]{:S(2)}) collective-permute-start(bf16[32,3072]{1,0:T(8,128)(2,1)S(1)} %collective-permute-done.5.refs_1_), channel_id=1, source_target_pairs={{0,4},{1,3},{2,6},{3,1},{4,0},{5,7},{6,2},{7,5},{8,12},{9,11},{10,... | collective-permute-start | bytes 589832 | tf_op jit(solution)/shard_map/ppermute | solution.py:476
  22.7 0.0 collective-permute-done.7.refs_2_
  22.7 0.5 %collective-permute-start.12 = (bf16[32,3072]{1,0:T(8,128)(2,1)S(1)}, bf16[32,3072]{1,0:T(8,128)(2,1)S(1)}, u32[]{:S(2)}, u32[]{:S(2)}) collective-permute-start(bf16[32,3072]{1,0:T(8,128)(2,1)S(1)} %collective-permute-done.6.refs_0_), channel_id=1, source_target_pairs={{0,4},{1,3},{2,6},{3,1},{4,0},{5,7},{6,2},{7,5},{8,12},{9,11},{10,... | collective-permute-start | bytes 589832 | tf_op jit(solution)/shard_map/ppermute | solution.py:476
  23.2 2.0 %collective-permute-done.3.refs_0_ = bf16[32,3072]{1,0:T(8,128)(2,1)S(1)} collective-permute-done((bf16[32,3072]{1,0:T(8,128)(2,1)}, bf16[32,3072]{1,0:T(8,128)(2,1)S(1)}, u32[]{:S(2)}, u32[]{:S(2)}) %collective-permute-start.3) | collective-permute-done | bytes 196640 | tf_op jit(solution)/shard_map/ppermute | solution.py:468
  25.2 2.2 %collective-permute-done.11.refs_1_ = bf16[32,3072]{1,0:T(8,128)(2,1)S(1)} collective-permute-done((bf16[32,3072]{1,0:T(8,128)(2,1)S(1)}, bf16[32,3072]{1,0:T(8,128)(2,1)S(1)}, u32[]{:S(2)}, u32[]{:S(2)}) %collective-permute-start.11) | collective-permute-done | bytes 196640 | tf_op jit(solution)/shard_map/ppermute | solution.py:476
  27.4 0.0 collective-permute-done.8.refs_3_
  27.4 1.5 %collective-permute-start.13 = (bf16[32,3072]{1,0:T(8,128)(2,1)S(1)}, bf16[32,3072]{1,0:T(8,128)(2,1)S(1)}, u32[]{:S(2)}, u32[]{:S(2)}) collective-permute-start(bf16[32,3072]{1,0:T(8,128)(2,1)S(1)} %collective-permute-done.11.refs_1_), channel_id=1, source_target_pairs={{0,4},{1,3},{2,6},{3,1},{4,0},{5,7},{6,2},{7,5},{8,12},{9,11},{10,... | collective-permute-start | bytes 589832 | tf_op jit(solution)/shard_map/ppermute | solution.py:476
  29.0 1.1 %collective-permute-start.14 = (bf16[32,3072]{1,0:T(8,128)(2,1)S(1)}, bf16[32,3072]{1,0:T(8,128)(2,1)S(1)}, u32[]{:S(2)}, u32[]{:S(2)}) collective-permute-start(bf16[32,3072]{1,0:T(8,128)(2,1)S(1)} %collective-permute-done.3.refs_0_), channel_id=1, source_target_pairs={{0,2},{1,5},{2,0},{3,7},{4,6},{5,1},{6,4},{7,3},{8,10},{9,13},{10,... | collective-permute-start | bytes 589832 | tf_op jit(solution)/shard_map/ppermute | solution.py:476
  30.0 1.0 %collective-permute-start.15 = (bf16[32,3072]{1,0:T(8,128)(2,1)S(1)}, bf16[32,3072]{1,0:T(8,128)(2,1)S(1)}, u32[]{:S(2)}, u32[]{:S(2)}) collective-permute-start(bf16[32,3072]{1,0:T(8,128)(2,1)S(1)} %collective-permute-done.3.refs_0_), channel_id=1, source_target_pairs={{0,4},{1,3},{2,6},{3,1},{4,0},{5,7},{6,2},{7,5},{8,12},{9,11},{10,... | collective-permute-start | bytes 589832 | tf_op jit(solution)/shard_map/ppermute | solution.py:476
  31.0 0.7 %plan.1.refs_0_ = s32[8,128]{1,0:T(8,128)S(1)} custom-call(s32[6]{0:T(128)} %refs_0_.2, s32[32]{0:T(128)} %refs_1_.1), custom_call_target="tpu_custom_call" | custom-call | tf_op jit(solution)/shard_map/plan/pallas_call | solution.py:253
  31.7 0.0 copy-start
  31.7 0.9 %copy-done = bf16[32,3072]{1,0:T(8,128)(2,1)S(1)} copy-done((bf16[32,3072]{1,0:T(8,128)(2,1)S(1)}, bf16[32,3072]{1,0:T(8,128)(2,1)}, u32[]{:S(2)}) %copy-start) | copy-done | bytes 196632
  32.7 0.8 %wave.4 = (bf16[128,2048]{1,0:T(8,128)(2,1)S(1)}, bf16[128,2048]{1,0:T(8,128)(2,1)S(1)}, f32[2,3072]{1,0:T(2,128)S(1)}) custom-call(s32[8,128]{1,0:T(8,128)S(1)} %plan.1.refs_0_, bf16[32,3072]{1,0:T(8,128)(2,1)S(1)} %copy-done, bf16[32,3072]{1,0:T(8,128)(2,1)S(1)} %collective-permute-done.refs_1_, bf16[32,3072]{1,0:T(8,128)(2,1)S(1)} %collective-permute-done.1.refs_2_, ...), custom_call_target="tpu_custom_call" | custom-call | bytes 786432 | tf_op jit(solution)/shard_map/wave/pallas_call | solution.py:320
  33.5 0.1 collective-permute-start.9
  33.6 0.8 %wave.5 = (bf16[128,2048]{1,0:T(8,128)(2,1)S(1)}, bf16[128,2048]{1,0:T(8,128)(2,1)S(1)}, f32[2,3072]{1,0:T(2,128)S(1)}) custom-call(s32[8,128]{1,0:T(8,128)S(1)} %plan.1.refs_0_, bf16[32,3072]{1,0:T(8,128)(2,1)S(1)} %collective-permute-done.4.refs_0_, bf16[32,3072]{1,0:T(8,128)(2,1)S(1)} %collective-permute-done.5.refs_1_, ...), custom_call_target="tpu_custom_call" | custom-call | bytes 786432 | tf_op jit(solution)/shard_map/wave/pallas_call | solution.py:320
  34.5 0.0 collective-permute-done.12.refs_2_
  34.5 0.5 %collective-permute-start.10 = (bf16[128,2048]{1,0:T(8,128)(2,1)S(1)}, bf16[128,2048]{1,0:T(8,128)(2,1)S(1)}, u32[]{:S(2)}, u32[]{:S(2)}) collective-permute-start(bf16[128,2048]{1,0:T(8,128)(2,1)S(1)} %get-tuple-element.35), channel_id=1, source_target_pairs={{0,1},{1,0},{2,3},{3,2},{4,5},{5,4},{6,7},{7,6},{8,9},{9,8},{10,11... | collective-permute-start | bytes 1572872 | tf_op jit(solution)/shard_map/ppermute | solution.py:479
  35.0 0.0 collective-permute-done.13.refs_3_
  35.0 0.8 %wave.6 = (bf16[128,2048]{1,0:T(8,128)(2,1)S(1)}, bf16[128,2048]{1,0:T(8,128)(2,1)S(1)}, f32[2,3072]{1,0:T(2,128)S(1)}) custom-call(s32[8,128]{1,0:T(8,128)S(1)} %plan.1.refs_0_, bf16[32,3072]{1,0:T(8,128)(2,1)S(1)} %collective-permute-done.6.refs_0_, bf16[32,3072]{1,0:T(8,128)(2,1)S(1)} %collective-permute-done.11.refs_1_, ...), custom_call_target="tpu_custom_call" | custom-call | bytes 786432 | tf_op jit(solution)/shard_map/wave/pallas_call | solution.py:320
  35.8 0.1 collective-permute-start.16
  35.9 0.0 collective-permute-done.14.refs_1_
  35.9 1.1 %collective-permute-start.18 = (bf16[32,3072]{1,0:T(8,128)(2,1)S(1)}, bf16[32,3072]{1,0:T(8,128)(2,1)S(1)}, u32[]{:S(2)}, u32[]{:S(2)}) collective-permute-start(bf16[32,3072]{1,0:T(8,128)(2,1)S(1)} %collective-permute-done.14.refs_1_), channel_id=1, source_target_pairs={{0,4},{1,3},{2,6},{3,1},{4,0},{5,7},{6,2},{7,5},{8,12},{9,11},{10,... | collective-permute-start | bytes 589832 | tf_op jit(solution)/shard_map/ppermute | solution.py:476
  37.0 0.0 collective-permute-done.15.refs_2_
  37.0 0.7 %wave.7 = (bf16[96,2048]{1,0:T(8,128)(2,1)S(1)}, bf16[96,2048]{1,0:T(8,128)(2,1)S(1)}, f32[4,3072]{1,0:T(4,128)S(1)}) custom-call(s32[8,128]{1,0:T(8,128)S(1)} %plan.1.refs_0_, bf16[32,3072]{1,0:T(8,128)(2,1)S(1)} %collective-permute-done.3.refs_0_, bf16[32,3072]{1,0:T(8,128)(2,1)S(1)} %collective-permute-done.14.refs_1_, ...), custom_call_target="tpu_custom_call" | custom-call | bytes 589824 | tf_op jit(solution)/shard_map/wave/pallas_call | solution.py:320
  37.7 0.1 collective-permute-start.17
  37.8 3.9 %collective-permute-done.18.refs_6_ = bf16[32,3072]{1,0:T(8,128)(2,1)S(1)} collective-permute-done((bf16[32,3072]{1,0:T(8,128)(2,1)S(1)}, bf16[32,3072]{1,0:T(8,128)(2,1)S(1)}, u32[]{:S(2)}, u32[]{:S(2)}) %collective-permute-start.18) | collective-permute-done | bytes 196640 | tf_op jit(solution)/shard_map/ppermute | solution.py:476
  41.6 0.0 collective-permute-start.19
  41.6 0.0 collective-permute-done.9.refs_3_
  41.6 0.0 collective-permute-done.10.refs_4_
  41.6 1.0 %partial.1.refs_1_ = f32[1024,1024]{1,0:T(8,128)S(1)} custom-call(s32[8,128]{1,0:T(8,128)S(1)} %plan.1.refs_0_, bf16[128,2048]{1,0:T(8,128)(2,1)S(1)} %get-tuple-element.29.refs_1_, bf16[128,2048]{1,0:T(8,128)(2,1)S(1)} %get-tuple-element.33.refs_2_, bf16[128,2048]{1,0:T(8,128)(2,1)S(1)} %collective-permute-done.9.refs_3_, ...), custom_call_target="tpu_custom_call" | custom-call | flops 536870912 | tf_op jit(solution)/shard_map/partial/pallas_call | solution.py:374
  42.7 0.4 collective-permute-done.19.refs_7_
  43.1 0.0 collective-permute-done.17.refs_5_
  43.1 0.0 collective-permute-done.16.refs_4_
  43.1 2.7 %finish.1 = (f32[1,1024,1024]{2,1,0:T(8,128)}, f32[1,3072]{1,0:T(1,128)}, f32[1,3072]{1,0:T(1,128)}) custom-call(s32[8,128]{1,0:T(8,128)S(1)} %plan.1.refs_0_, f32[1024,1024]{1,0:T(8,128)S(1)} %partial.1.refs_1_, bf16[128,2048]{1,0:T(8,128)(2,1)S(1)} %get-tuple-element.38.refs_2_, bf16[96,2048]{1,0:T(8,128)(2,1)S(1)} %get-tuple-element.40.refs_3_, ...), custom_call_target="tpu_custom_call" | custom-call | flops 536870912 | bytes 4194304 | tf_op jit(solution)/shard_map/finish/pallas_call | solution.py:435
Async XLA Ops:
  0.6 7.2 %collective-permute-start = (bf16[32,3072]{1,0:T(8,128)(2,1)}, bf16[32,3072]{1,0:T(8,128)(2,1)S(1)}, u32[]{:S(2)}, u32[]{:S(2)}) collective-permute-start(bf16[32,3072]{1,0:T(8,128)(2,1)} %refs_0_.3), channel_id=1, source_target_pairs={{0,2},{1,5},{2,0},{3,7},{4,6},{5,1},{6,4},{7,3},{8,10},{9,13},{10,... | collective-permute-start | bytes 589832 | tf_op jit(solution)/shard_map/ppermute | solution.py:476
  3.6 10.7 %collective-permute-start.4 = (bf16[32,3072]{1,0:T(8,128)(2,1)}, bf16[32,3072]{1,0:T(8,128)(2,1)S(1)}, u32[]{:S(2)}, u32[]{:S(2)}) collective-permute-start(bf16[32,3072]{1,0:T(8,128)(2,1)} %refs_0_.3), channel_id=1, source_target_pairs={{0,8},{2,10},{4,12},{6,14},{8,0},{10,2},{12,4},{14,6},{16,24},{18,... | collective-permute-start | bytes 589832 | tf_op jit(solution)/shard_map/ppermute | solution.py:468
  5.2 11.5 %collective-permute-start.6 = (bf16[32,3072]{1,0:T(8,128)(2,1)}, bf16[32,3072]{1,0:T(8,128)(2,1)S(1)}, u32[]{:S(2)}, u32[]{:S(2)}) collective-permute-start(bf16[32,3072]{1,0:T(8,128)(2,1)} %refs_0_.3), channel_id=1, source_target_pairs={{0,16},{2,18},{4,20},{6,22},{8,24},{10,26},{12,28},{14,30},{16,0},... | collective-permute-start | bytes 589832 | tf_op jit(solution)/shard_map/ppermute | solution.py:468
  7.8 11.9 %collective-permute-start.1 = (bf16[32,3072]{1,0:T(8,128)(2,1)}, bf16[32,3072]{1,0:T(8,128)(2,1)S(1)}, u32[]{:S(2)}, u32[]{:S(2)}) collective-permute-start(bf16[32,3072]{1,0:T(8,128)(2,1)} %refs_0_.3), channel_id=1, source_target_pairs={{0,4},{1,3},{2,6},{3,1},{4,0},{5,7},{6,2},{7,5},{8,12},{9,11},{10,... | collective-permute-start | bytes 589832 | tf_op jit(solution)/shard_map/ppermute | solution.py:476
  9.5 11.6 %collective-permute-start.2 = (bf16[32,3072]{1,0:T(8,128)(2,1)S(1)}, bf16[32,3072]{1,0:T(8,128)(2,1)S(1)}, u32[]{:S(2)}, u32[]{:S(2)}) collective-permute-start(bf16[32,3072]{1,0:T(8,128)(2,1)S(1)} %collective-permute-done.refs_1_), channel_id=1, source_target_pairs={{0,4},{1,3},{2,6},{3,1},{4,0},{5,7},{6,2},{7,5},{8,12},{9,11},{10,... | collective-permute-start | bytes 589832 | tf_op jit(solution)/shard_map/ppermute | solution.py:476
  14.3 6.9 %collective-permute-start.5 = (bf16[32,3072]{1,0:T(8,128)(2,1)S(1)}, bf16[32,3072]{1,0:T(8,128)(2,1)S(1)}, u32[]{:S(2)}, u32[]{:S(2)}) collective-permute-start(bf16[32,3072]{1,0:T(8,128)(2,1)S(1)} %collective-permute-done.4.refs_0_), channel_id=1, source_target_pairs={{0,2},{1,5},{2,0},{3,7},{4,6},{5,1},{6,4},{7,3},{8,10},{9,13},{10,... | collective-permute-start | bytes 589832 | tf_op jit(solution)/shard_map/ppermute | solution.py:476
  16.7 6.0 %collective-permute-start.7 = (bf16[32,3072]{1,0:T(8,128)(2,1)S(1)}, bf16[32,3072]{1,0:T(8,128)(2,1)S(1)}, u32[]{:S(2)}, u32[]{:S(2)}) collective-permute-start(bf16[32,3072]{1,0:T(8,128)(2,1)S(1)} %collective-permute-done.4.refs_0_), channel_id=1, source_target_pairs={{0,4},{1,3},{2,6},{3,1},{4,0},{5,7},{6,2},{7,5},{8,12},{9,11},{10,... | collective-permute-start | bytes 589832 | tf_op jit(solution)/shard_map/ppermute | solution.py:476
  17.2 8.0 %collective-permute-start.3 = (bf16[32,3072]{1,0:T(8,128)(2,1)}, bf16[32,3072]{1,0:T(8,128)(2,1)S(1)}, u32[]{:S(2)}, u32[]{:S(2)}) collective-permute-start(bf16[32,3072]{1,0:T(8,128)(2,1)} %refs_0_.3), channel_id=1, source_target_pairs={{0,24},{2,26},{4,28},{6,30},{8,16},{10,18},{12,20},{14,22},{16,8},... | collective-permute-start | bytes 589832 | tf_op jit(solution)/shard_map/ppermute | solution.py:468
  19.7 7.8 %collective-permute-start.11 = (bf16[32,3072]{1,0:T(8,128)(2,1)S(1)}, bf16[32,3072]{1,0:T(8,128)(2,1)S(1)}, u32[]{:S(2)}, u32[]{:S(2)}) collective-permute-start(bf16[32,3072]{1,0:T(8,128)(2,1)S(1)} %collective-permute-done.6.refs_0_), channel_id=1, source_target_pairs={{0,2},{1,5},{2,0},{3,7},{4,6},{5,1},{6,4},{7,3},{8,10},{9,13},{10,... | collective-permute-start | bytes 589832 | tf_op jit(solution)/shard_map/ppermute | solution.py:476
  21.2 6.3 %collective-permute-start.8 = (bf16[32,3072]{1,0:T(8,128)(2,1)S(1)}, bf16[32,3072]{1,0:T(8,128)(2,1)S(1)}, u32[]{:S(2)}, u32[]{:S(2)}) collective-permute-start(bf16[32,3072]{1,0:T(8,128)(2,1)S(1)} %collective-permute-done.5.refs_1_), channel_id=1, source_target_pairs={{0,4},{1,3},{2,6},{3,1},{4,0},{5,7},{6,2},{7,5},{8,12},{9,11},{10,... | collective-permute-start | bytes 589832 | tf_op jit(solution)/shard_map/ppermute | solution.py:476
  22.7 11.8 %collective-permute-start.12 = (bf16[32,3072]{1,0:T(8,128)(2,1)S(1)}, bf16[32,3072]{1,0:T(8,128)(2,1)S(1)}, u32[]{:S(2)}, u32[]{:S(2)}) collective-permute-start(bf16[32,3072]{1,0:T(8,128)(2,1)S(1)} %collective-permute-done.6.refs_0_), channel_id=1, source_target_pairs={{0,4},{1,3},{2,6},{3,1},{4,0},{5,7},{6,2},{7,5},{8,12},{9,11},{10,... | collective-permute-start | bytes 589832 | tf_op jit(solution)/shard_map/ppermute | solution.py:476
  27.4 7.5 %collective-permute-start.13 = (bf16[32,3072]{1,0:T(8,128)(2,1)S(1)}, bf16[32,3072]{1,0:T(8,128)(2,1)S(1)}, u32[]{:S(2)}, u32[]{:S(2)}) collective-permute-start(bf16[32,3072]{1,0:T(8,128)(2,1)S(1)} %collective-permute-done.11.refs_1_), channel_id=1, source_target_pairs={{0,4},{1,3},{2,6},{3,1},{4,0},{5,7},{6,2},{7,5},{8,12},{9,11},{10,... | collective-permute-start | bytes 589832 | tf_op jit(solution)/shard_map/ppermute | solution.py:476
  29.0 6.9 %collective-permute-start.14 = (bf16[32,3072]{1,0:T(8,128)(2,1)S(1)}, bf16[32,3072]{1,0:T(8,128)(2,1)S(1)}, u32[]{:S(2)}, u32[]{:S(2)}) collective-permute-start(bf16[32,3072]{1,0:T(8,128)(2,1)S(1)} %collective-permute-done.3.refs_0_), channel_id=1, source_target_pairs={{0,2},{1,5},{2,0},{3,7},{4,6},{5,1},{6,4},{7,3},{8,10},{9,13},{10,... | collective-permute-start | bytes 589832 | tf_op jit(solution)/shard_map/ppermute | solution.py:476
  30.0 7.0 %collective-permute-start.15 = (bf16[32,3072]{1,0:T(8,128)(2,1)S(1)}, bf16[32,3072]{1,0:T(8,128)(2,1)S(1)}, u32[]{:S(2)}, u32[]{:S(2)}) collective-permute-start(bf16[32,3072]{1,0:T(8,128)(2,1)S(1)} %collective-permute-done.3.refs_0_), channel_id=1, source_target_pairs={{0,4},{1,3},{2,6},{3,1},{4,0},{5,7},{6,2},{7,5},{8,12},{9,11},{10,... | collective-permute-start | bytes 589832 | tf_op jit(solution)/shard_map/ppermute | solution.py:476
  31.7 0.9 %copy-start = (bf16[32,3072]{1,0:T(8,128)(2,1)S(1)}, bf16[32,3072]{1,0:T(8,128)(2,1)}, u32[]{:S(2)}) copy-start(bf16[32,3072]{1,0:T(8,128)(2,1)} %refs_0_.3) | copy-start | bytes 589828
  33.5 8.1 %collective-permute-start.9 = (bf16[128,2048]{1,0:T(8,128)(2,1)S(1)}, bf16[128,2048]{1,0:T(8,128)(2,1)S(1)}, u32[]{:S(2)}, u32[]{:S(2)}) collective-permute-start(bf16[128,2048]{1,0:T(8,128)(2,1)S(1)} %get-tuple-element.34), channel_id=1, source_target_pairs={{0,1},{1,0},{2,3},{3,2},{4,5},{5,4},{6,7},{7,6},{8,9},{9,8},{10,11... | collective-permute-start | bytes 1572872 | tf_op jit(solution)/shard_map/ppermute | solution.py:479
  34.5 7.2 %collective-permute-start.10 = (bf16[128,2048]{1,0:T(8,128)(2,1)S(1)}, bf16[128,2048]{1,0:T(8,128)(2,1)S(1)}, u32[]{:S(2)}, u32[]{:S(2)}) collective-permute-start(bf16[128,2048]{1,0:T(8,128)(2,1)S(1)} %get-tuple-element.35), channel_id=1, source_target_pairs={{0,1},{1,0},{2,3},{3,2},{4,5},{5,4},{6,7},{7,6},{8,9},{9,8},{10,11... | collective-permute-start | bytes 1572872 | tf_op jit(solution)/shard_map/ppermute | solution.py:479
  35.8 7.3 %collective-permute-start.16 = (bf16[128,2048]{1,0:T(8,128)(2,1)S(1)}, bf16[128,2048]{1,0:T(8,128)(2,1)S(1)}, u32[]{:S(2)}, u32[]{:S(2)}) collective-permute-start(bf16[128,2048]{1,0:T(8,128)(2,1)S(1)} %get-tuple-element.41), channel_id=1, source_target_pairs={{0,1},{1,0},{2,3},{3,2},{4,5},{5,4},{6,7},{7,6},{8,9},{9,8},{10,11... | collective-permute-start | bytes 1572872 | tf_op jit(solution)/shard_map/ppermute | solution.py:479
  35.9 5.7 %collective-permute-start.18 = (bf16[32,3072]{1,0:T(8,128)(2,1)S(1)}, bf16[32,3072]{1,0:T(8,128)(2,1)S(1)}, u32[]{:S(2)}, u32[]{:S(2)}) collective-permute-start(bf16[32,3072]{1,0:T(8,128)(2,1)S(1)} %collective-permute-done.14.refs_1_), channel_id=1, source_target_pairs={{0,4},{1,3},{2,6},{3,1},{4,0},{5,7},{6,2},{7,5},{8,12},{9,11},{10,... | collective-permute-start | bytes 589832 | tf_op jit(solution)/shard_map/ppermute | solution.py:476
  37.7 5.4 %collective-permute-start.17 = (bf16[96,2048]{1,0:T(8,128)(2,1)S(1)}, bf16[96,2048]{1,0:T(8,128)(2,1)S(1)}, u32[]{:S(2)}, u32[]{:S(2)}) collective-permute-start(bf16[96,2048]{1,0:T(8,128)(2,1)S(1)} %get-tuple-element.42), channel_id=1, source_target_pairs={{0,1},{1,0},{2,3},{3,2},{4,5},{5,4},{6,7},{7,6},{8,9},{9,8},{10,11... | collective-permute-start | bytes 1179656 | tf_op jit(solution)/shard_map/ppermute | solution.py:479
  41.6 1.4 %collective-permute-start.19 = (bf16[32,3072]{1,0:T(8,128)(2,1)S(1)}, bf16[32,3072]{1,0:T(8,128)(2,1)S(1)}, u32[]{:S(2)}, u32[]{:S(2)}) collective-permute-start(bf16[32,3072]{1,0:T(8,128)(2,1)S(1)} %collective-permute-done.18.refs_6_), channel_id=1, source_target_pairs={{0,1},{1,0},{2,3},{3,2},{4,5},{5,4},{6,7},{7,6},{8,9},{9,8},{10,11... | collective-permute-start | bytes 589832 | tf_op jit(solution)/shard_map/ppermute | solution.py:479

commit v4 on v3

--- a/solution.py
+++ b/solution.py
@@ -236,7 +236,7 @@
     return (product, mine[0] / total_tokens, mine[1] / total_tokens)
 
 
-def plan_kernel(block_count, slot_ref, tile_ref, plan):
+def plan_kernel(block_count, slot_ref, tile_ref, shard, plan, near_shard):
     col = lax.axis_index("col")
     mine = tile_ref[lax.axis_index("tok") * 2 + col]
     packed = jnp.where(mine < block_count * (block_count + 1) // 2, 1 << 24, 0)
@@ -246,18 +246,23 @@
             packed += slot_ref[member] << shift
             shift += 6
     plan[...] = jnp.full((8, 128), packed, jnp.int32)
-
-
-def make_plan(block_count, block_slot, slot_tile):
-    tables = [pltpu.with_memory_space_constraint(a, pltpu.HBM) for a in (block_slot, slot_tile)]
+    near_shard[...] = shard[...]
+
+
+def make_plan(block_count, block_slot, slot_tile, shard):
+    near = Near(True)
     return pl.pallas_call(
         lambda *refs: plan_kernel(block_count, *refs),
-        out_shape=Near(True).out((8, 128), jnp.int32),
-        in_specs=[SMEM, SMEM],
-        out_specs=VMEM,
-        compiler_params=pltpu.CompilerParams(vmem_limit_bytes=1 << 20),
+        out_shape=[near.out((8, 128), jnp.int32), near.out(shard.shape, shard.dtype)],
+        in_specs=[SMEM, SMEM, VMEM],
+        out_specs=[VMEM, VMEM],
+        compiler_params=pltpu.CompilerParams(vmem_limit_bytes=2 << 20),
         name="plan",
-    )(*tables)
+    )(hbm(block_slot), hbm(slot_tile), hbm(shard))
+
+
+def hbm(a):
+    return pltpu.with_memory_space_constraint(a, pltpu.HBM)
 
 
 def planned(plan):
@@ -291,45 +296,50 @@
             dst[pl.ds(start, ref.shape[0]), :] = ref[:, pl.ds(column, BS)]
 
 
-def wave_kernel(plan, *refs):
-    shards, (own, other, stats) = refs[:-3], refs[-3:]
-    tok_dev, width = shards[0].shape
+def wave_kernel(sizes, plan, *refs):
+    arrays, (own, other, stats) = refs[:-3], refs[-3:]
+    tok_dev, width = arrays[0].shape
     col = lax.axis_index("col")
-    first = pl.multiple_of((1 + col) * tok_dev, tok_dev)
-    second = pl.multiple_of((2 - col) * tok_dev, tok_dev)
-    starts = (0, first, second, 3 * tok_dev)
+    places = (0, 1 + col, 2 - col, 3)
+    starts, done, row = [], 0, 0
+    for size in sizes:
+        starts += [pl.multiple_of((done + p) * tok_dev, tok_dev) for p in places[:size]]
+        parts = [shard_stats(ref) for ref in arrays[done : done + size]]
+        if size == 4:
+            parts = [stat_tree(parts, tok_dev)]
+        else:
+            parts = [merge(parts[0], parts[2], tok_dev), parts[1]]
+        for part, square in parts:
+            stats[row : row + 1, :] = part
+            stats[row + 1 : row + 2, :] = square
+            row += 2
+        done += size
     mine, theirs, _ = planned(plan)
     for out, blocks in ((own, mine), (other, theirs)):
         for side, block in enumerate(blocks):
             side_out = out.at[:, side * BS : (side + 1) * BS]
-            take_block(block, col, width // BS, shards, starts, side_out)
-    parts = [shard_stats(ref) for ref in shards]
-    if len(parts) == 4:
-        parts = [stat_tree(parts, tok_dev)]
-    else:
-        parts = [merge(parts[0], parts[2], tok_dev), parts[1]]
-    for k, (part, square) in enumerate(parts):
-        stats[2 * k : 2 * k + 1, :] = part
-        stats[2 * k + 1 : 2 * k + 2, :] = square
-
-
-def wave_parts(plan, shards, skip=None):
+            take_block(block, col, width // BS, arrays, starts, side_out)
+
+
+def wave_parts(plan, *waves):
+    near = Near(True)
+    shards = [a for wave in waves for a in wave]
+    sizes = [len(wave) for wave in waves]
     tok_dev, width = shards[0].shape
-    near = Near(True)
     rows = len(shards) * tok_dev
     return pl.pallas_call(
-        wave_kernel,
+        lambda *refs: wave_kernel(sizes, *refs),
         out_shape=[
             near.out((rows, 2 * BS), jnp.bfloat16),
             near.out((rows, 2 * BS), jnp.bfloat16),
-            near.out((2 if len(shards) == 4 else 4, width), jnp.float32),
+            near.out((sum(2 if size == 4 else 4 for size in sizes), width), jnp.float32),
         ],
         in_specs=[VMEM] * (1 + len(shards)),
         out_specs=[VMEM] * 3,
         cost_estimate=pl.CostEstimate(flops=0, transcendentals=0, bytes_accessed=2 * rows * width),
         compiler_params=pltpu.CompilerParams(vmem_limit_bytes=4 << 20),
         name="wave",
-    )(near.put(plan), *[a if a is skip else near.put(a) for a in shards])
+    )(near.put(plan), *[near.put(a) for a in shards])
 
 
 def assemble(blocks, col, held, own, other, sides, start):
@@ -411,13 +421,10 @@
             pltpu.make_async_copy(result.at[here, :], out.at[0, here, :], sems.at[m])
         )
         copies[-1].start()
-    *whole, split = stats
-    last = merge(
-        (split[0:1, :], split[1:2, :]),
-        merge((split[2:3, :], split[3:4, :]), shard_stats(far), tok_dev),
-        2 * tok_dev,
-    )
-    parts = [(ref[0:1, :], ref[1:2, :]) for ref in whole] + [last]
+    *whole, split, rest = [
+        (ref[k : k + 1, :], ref[k + 1 : k + 2, :]) for ref in stats for k in range(0, ref.shape[0], 2)
+    ]
+    parts = [*whole, merge(split, merge(rest, shard_stats(far), tok_dev), 2 * tok_dev)]
     part, square = stat_tree(parts, 4 * tok_dev)
     for k, (ref, value) in enumerate(((mean, part), (var, square))):
         moments[k] = value / total_tokens
@@ -446,7 +453,7 @@
             pltpu.VMEM((tokens, BS), jnp.bfloat16),
             pltpu.VMEM((BS, BS), jnp.float32),
             pltpu.VMEM((2, 1, width), jnp.float32),
-            pltpu.SemaphoreType.DMA((6,)),
+            pltpu.SemaphoreType.DMA((10,)),
         ],
         cost_estimate=pl.CostEstimate(
             flops=2 * tokens * BS * BS, transcendentals=0, bytes_accessed=4 * BS * BS
@@ -462,7 +469,7 @@
     tok_dev, width = activations.shape
     held = width // BS
     block_count = held * 2
-    plan = make_plan(block_count, block_slot, slot_tile)
+    plan, own_shard = make_plan(block_count, block_slot, slot_tile, activations)
 
     def from_outer(a, k):
         return lax.ppermute(a, "tok", [(t, t ^ (4 * k)) for t in range(n_tok)])
@@ -484,21 +491,21 @@
     z3 = from_outer(after(activations, s0), 3)
     b0 = from_plane(after(activations, s0), False)
     f0 = from_plane(s0, False)
-    own0, out0, stats0 = wave_parts(plan, [activations, s0, b0, after(f0, z3)], activations)
-    other0 = from_sibling(out0)
     s1 = from_plane(z1, True)
     b1 = from_plane(after(z1, z2), False)
-    f1 = from_plane(after(s1, f0, b0), False)
-    own1, out1, stats1 = wave_parts(plan, [z1, s1, b1, after(f1, f1)])
-    other1 = from_sibling(out1)
+    f1 = from_plane(after(s1, b0, f0, z2), False)
     s2 = from_plane(z2, True)
     b2 = from_plane(after(z2, b1), False)
     f2 = from_plane(after(s2, f1, b1, z3), False)
-    own2, out2, stats2 = wave_parts(plan, [z2, s2, b2, f2])
-    other2 = from_sibling(out2)
     s3 = from_plane(z3, True)
     b3 = from_plane(z3, False)
     f3 = from_plane(after(s3, b1, b2), False)
+    own0, out0, stats0 = wave_parts(plan, [own_shard, s0, b0, after(f0, s3)])
+    other0 = from_sibling(out0)
+    own1, out1, stats1 = wave_parts(plan, [z1, s1, b1, after(f1, f1)])
+    other1 = from_sibling(out1)
+    own2, out2, stats2 = wave_parts(plan, [z2, s2, b2, f2])
+    other2 = from_sibling(out2)
     own3, out3, stats3 = wave_parts(plan, [z3, s3, after(b3, f2)])
     other3 = from_sibling(out3)
     acc = partial_gram(held, plan, [own0, own1], [other0, other1])

time: 46 us -> 45.2 us (0.983)
  waiting for transfers between devices: 13.9 us -> 15.5 us
  starting transfers between devices: 22.6 us -> 21.1 us
  local copies, waits for them, and re-layouts: 0.92 us -> 0 us
    ppermute x12, waiting for transfers between devices: 6.14 us -> 8.31 us  [from_plane(): return lax.ppermute(a, ('tok', 'col'), pairs)]
    ppermute x12, starting transfers between devices: 15.2 us -> 13.7 us  [from_plane(): return lax.ppermute(a, ('tok', 'col'), pairs)]
    unnamed x2 -> x0, local copies, waits for them, and re-layouts: 0.92 us -> none
    ppermute x3, waiting for transfers between devices: 7.34 us -> 6.72 us  [from_outer(): return lax.ppermute(a, 'tok', [(t, t ^ 4 * k) for t in range(n_tok)])]
  transfers between devices with their start and end apart: 20 -> 20, of which waited for: 6 -> 8; matrix products, arithmetic and copies ran while one was open for 0% -> 0% of each run, Pallas kernels for 11% -> 11%
where the time goes in v4:
time: 45.2 us; the launch traced here: 45 us
  starting transfers between devices  21.1 us (47%)
  waiting for transfers between devices  15.5 us (34%)
  Pallas kernels  7.71 us (17%)
  between operations  0.73 us (2%)
    ppermute x12, starting transfers between devices, from_plane(): return lax.ppermute(a, ('tok', 'col'), pairs)  13.7 us
    ppermute x12, waiting for transfers between devices, from_plane(): return lax.ppermute(a, ('tok', 'col'), pairs)  8.31 us
    ppermute x3, waiting for transfers between devices, from_outer(): return lax.ppermute(a, 'tok', [(t, t ^ 4 * k) for t in range(n_tok)])  6.72 us
    ppermute x3, starting transfers between devices, from_outer(): return lax.ppermute(a, 'tok', [(t, t ^ 4 * k) for t in range(n_tok)])  6.66 us
    pallas_call x4, Pallas kernels, wave_parts(): pl.pallas_call(lambda *refs: wave_kernel(sizes, *refs), out_shape=[near.o...  3.01 us
    pallas_call x1, Pallas kernels, finish(): pl.pallas_call(lambda *refs: finish_kernel(total_tokens, len(own), *refs)...  2.71 us
    pallas_call x1, Pallas kernels, partial_gram(): pl.pallas_call(lambda *refs: partial_kernel(held, *refs), out_shape=near....  1.02 us
    pallas_call x1, Pallas kernels, make_plan(): pl.pallas_call(lambda *refs: plan_kernel(block_count, *refs), out_shape=[...  0.97 us
  transfers between devices with their start and end apart: 20, of which 8 were waited for; matrix products, arithmetic and copies ran while one was open for 0% of the time, Pallas kernels for 11%

profile of v4, /device:TPU:0, one launch (start us, length us, event | category | flops | bytes accessed | tf_op | source)
XLA Modules:
  0.0 45.0 jit_solution(4897968080930148434)
XLA Ops:
  0.6 3.0 %collective-permute-start = (bf16[32,3072]{1,0:T(8,128)(2,1)}, bf16[32,3072]{1,0:T(8,128)(2,1)S(1)}, u32[]{:S(2)}, u32[]{:S(2)}) collective-permute-start(bf16[32,3072]{1,0:T(8,128)(2,1)} %refs_2_.1), channel_id=1, source_target_pairs={{0,2},{1,5},{2,0},{3,7},{4,6},{5,1},{6,4},{7,3},{8,10},{9,13},{10,... | collective-permute-start | bytes 589832 | tf_op jit(solution)/shard_map/ppermute | solution.py:483
  3.6 1.6 %collective-permute-start.5 = (bf16[32,3072]{1,0:T(8,128)(2,1)}, bf16[32,3072]{1,0:T(8,128)(2,1)S(1)}, u32[]{:S(2)}, u32[]{:S(2)}) collective-permute-start(bf16[32,3072]{1,0:T(8,128)(2,1)} %refs_2_.1), channel_id=1, source_target_pairs={{0,8},{2,10},{4,12},{6,14},{8,0},{10,2},{12,4},{14,6},{16,24},{18,... | collective-permute-start | bytes 589832 | tf_op jit(solution)/shard_map/ppermute | solution.py:475
  5.2 2.6 %collective-permute-start.7 = (bf16[32,3072]{1,0:T(8,128)(2,1)}, bf16[32,3072]{1,0:T(8,128)(2,1)S(1)}, u32[]{:S(2)}, u32[]{:S(2)}) collective-permute-start(bf16[32,3072]{1,0:T(8,128)(2,1)} %refs_2_.1), channel_id=1, source_target_pairs={{0,16},{2,18},{4,20},{6,22},{8,24},{10,26},{12,28},{14,30},{16,0},... | collective-permute-start | bytes 589832 | tf_op jit(solution)/shard_map/ppermute | solution.py:475
  7.8 0.0 collective-permute-done.refs_2_
  7.8 1.7 %collective-permute-start.1 = (bf16[32,3072]{1,0:T(8,128)(2,1)}, bf16[32,3072]{1,0:T(8,128)(2,1)S(1)}, u32[]{:S(2)}, u32[]{:S(2)}) collective-permute-start(bf16[32,3072]{1,0:T(8,128)(2,1)} %refs_2_.1), channel_id=1, source_target_pairs={{0,4},{1,3},{2,6},{3,1},{4,0},{5,7},{6,2},{7,5},{8,12},{9,11},{10,... | collective-permute-start | bytes 589832 | tf_op jit(solution)/shard_map/ppermute | solution.py:483
  9.5 0.3 collective-permute-start.2
  9.8 4.5 %collective-permute-done.5.refs_1_ = bf16[32,3072]{1,0:T(8,128)(2,1)S(1)} collective-permute-done((bf16[32,3072]{1,0:T(8,128)(2,1)}, bf16[32,3072]{1,0:T(8,128)(2,1)S(1)}, u32[]{:S(2)}, u32[]{:S(2)}) %collective-permute-start.5) | collective-permute-done | bytes 196640 | tf_op jit(solution)/shard_map/ppermute | solution.py:475
  14.3 1.5 %collective-permute-start.6 = (bf16[32,3072]{1,0:T(8,128)(2,1)S(1)}, bf16[32,3072]{1,0:T(8,128)(2,1)S(1)}, u32[]{:S(2)}, u32[]{:S(2)}) collective-permute-start(bf16[32,3072]{1,0:T(8,128)(2,1)S(1)} %collective-permute-done.5.refs_1_), channel_id=1, source_target_pairs={{0,2},{1,5},{2,0},{3,7},{4,6},{5,1},{6,4},{7,3},{8,10},{9,13},{10,... | collective-permute-start | bytes 589832 | tf_op jit(solution)/shard_map/ppermute | solution.py:483
  15.8 2.5 %collective-permute-start.3 = (bf16[32,3072]{1,0:T(8,128)(2,1)}, bf16[32,3072]{1,0:T(8,128)(2,1)S(1)}, u32[]{:S(2)}, u32[]{:S(2)}) collective-permute-start(bf16[32,3072]{1,0:T(8,128)(2,1)} %refs_2_.1), channel_id=1, source_target_pairs={{0,24},{2,26},{4,28},{6,30},{8,16},{10,18},{12,20},{14,22},{16,8},... | collective-permute-start | bytes 589832 | tf_op jit(solution)/shard_map/ppermute | solution.py:475
  18.3 0.0 collective-permute-done.7.refs_1_
  18.3 0.5 %collective-permute-start.8 = (bf16[32,3072]{1,0:T(8,128)(2,1)S(1)}, bf16[32,3072]{1,0:T(8,128)(2,1)S(1)}, u32[]{:S(2)}, u32[]{:S(2)}) collective-permute-start(bf16[32,3072]{1,0:T(8,128)(2,1)S(1)} %collective-permute-done.5.refs_1_), channel_id=1, source_target_pairs={{0,4},{1,3},{2,6},{3,1},{4,0},{5,7},{6,2},{7,5},{8,12},{9,11},{10,... | collective-permute-start | bytes 589832 | tf_op jit(solution)/shard_map/ppermute | solution.py:483
  18.8 0.0 collective-permute-done.1.refs_3_
  18.8 0.7 %collective-permute-start.12 = (bf16[32,3072]{1,0:T(8,128)(2,1)S(1)}, bf16[32,3072]{1,0:T(8,128)(2,1)S(1)}, u32[]{:S(2)}, u32[]{:S(2)}) collective-permute-start(bf16[32,3072]{1,0:T(8,128)(2,1)S(1)} %collective-permute-done.7.refs_1_), channel_id=1, source_target_pairs={{0,2},{1,5},{2,0},{3,7},{4,6},{5,1},{6,4},{7,3},{8,10},{9,13},{10,... | collective-permute-start | bytes 589832 | tf_op jit(solution)/shard_map/ppermute | solution.py:483
  19.5 0.0 collective-permute-done.2.refs_4_
  19.5 1.9 %collective-permute-done.6.refs_2_ = bf16[32,3072]{1,0:T(8,128)(2,1)S(1)} collective-permute-done((bf16[32,3072]{1,0:T(8,128)(2,1)S(1)}, bf16[32,3072]{1,0:T(8,128)(2,1)S(1)}, u32[]{:S(2)}, u32[]{:S(2)}) %collective-permute-start.6) | collective-permute-done | bytes 196640 | tf_op jit(solution)/shard_map/ppermute | solution.py:483
  21.4 0.0 collective-permute-start.9
  21.4 2.2 %collective-permute-done.3.refs_1_ = bf16[32,3072]{1,0:T(8,128)(2,1)S(1)} collective-permute-done((bf16[32,3072]{1,0:T(8,128)(2,1)}, bf16[32,3072]{1,0:T(8,128)(2,1)S(1)}, u32[]{:S(2)}, u32[]{:S(2)}) %collective-permute-start.3) | collective-permute-done | bytes 196640 | tf_op jit(solution)/shard_map/ppermute | solution.py:475
  23.6 1.2 %collective-permute-start.4 = (bf16[32,3072]{1,0:T(8,128)(2,1)S(1)}, bf16[32,3072]{1,0:T(8,128)(2,1)S(1)}, u32[]{:S(2)}, u32[]{:S(2)}) collective-permute-start(bf16[32,3072]{1,0:T(8,128)(2,1)S(1)} %collective-permute-done.3.refs_1_), channel_id=1, source_target_pairs={{0,2},{1,5},{2,0},{3,7},{4,6},{5,1},{6,4},{7,3},{8,10},{9,13},{10,... | collective-permute-start | bytes 589832 | tf_op jit(solution)/shard_map/ppermute | solution.py:483
  24.8 0.8 %collective-permute-done.8.refs_3_ = bf16[32,3072]{1,0:T(8,128)(2,1)S(1)} collective-permute-done((bf16[32,3072]{1,0:T(8,128)(2,1)S(1)}, bf16[32,3072]{1,0:T(8,128)(2,1)S(1)}, u32[]{:S(2)}, u32[]{:S(2)}) %collective-permute-start.8) | collective-permute-done | bytes 196640 | tf_op jit(solution)/shard_map/ppermute | solution.py:483
  25.6 0.9 %collective-permute-start.13 = (bf16[32,3072]{1,0:T(8,128)(2,1)S(1)}, bf16[32,3072]{1,0:T(8,128)(2,1)S(1)}, u32[]{:S(2)}, u32[]{:S(2)}) collective-permute-start(bf16[32,3072]{1,0:T(8,128)(2,1)S(1)} %collective-permute-done.7.refs_1_), channel_id=1, source_target_pairs={{0,4},{1,3},{2,6},{3,1},{4,0},{5,7},{6,2},{7,5},{8,12},{9,11},{10,... | collective-permute-start | bytes 589832 | tf_op jit(solution)/shard_map/ppermute | solution.py:483
  26.5 0.0 collective-permute-done.12.refs_2_
  26.5 2.0 %collective-permute-done.9.refs_4_ = bf16[32,3072]{1,0:T(8,128)(2,1)S(1)} collective-permute-done((bf16[32,3072]{1,0:T(8,128)(2,1)S(1)}, bf16[32,3072]{1,0:T(8,128)(2,1)S(1)}, u32[]{:S(2)}, u32[]{:S(2)}) %collective-permute-start.9) | collective-permute-done | bytes 196640 | tf_op jit(solution)/shard_map/ppermute | solution.py:483
  28.5 1.7 %collective-permute-start.14 = (bf16[32,3072]{1,0:T(8,128)(2,1)S(1)}, bf16[32,3072]{1,0:T(8,128)(2,1)S(1)}, u32[]{:S(2)}, u32[]{:S(2)}) collective-permute-start(bf16[32,3072]{1,0:T(8,128)(2,1)S(1)} %collective-permute-done.12.refs_2_), channel_id=1, source_target_pairs={{0,4},{1,3},{2,6},{3,1},{4,0},{5,7},{6,2},{7,5},{8,12},{9,11},{10,... | collective-permute-start | bytes 589832 | tf_op jit(solution)/shard_map/ppermute | solution.py:483
  30.3 0.3 collective-permute-start.15
  30.6 1.0 %plan.1 = (s32[8,128]{1,0:T(8,128)S(1)}, bf16[32,3072]{1,0:T(8,128)(2,1)S(1)}) custom-call(s32[6]{0:T(128)} %refs_0_.1, s32[32]{0:T(128)} %refs_1_.1, bf16[32,3072]{1,0:T(8,128)(2,1)} %refs_2_.1), custom_call_target="tpu_custom_call" | custom-call | tf_op jit(solution)/shard_map/plan/pallas_call | solution.py:254
  31.5 0.0 collective-permute-done.4.refs_2_
  31.6 0.8 %wave.5 = (bf16[128,2048]{1,0:T(8,128)(2,1)S(1)}, bf16[128,2048]{1,0:T(8,128)(2,1)S(1)}, f32[2,3072]{1,0:T(2,128)S(1)}) custom-call(s32[8,128]{1,0:T(8,128)S(1)} %get-tuple-element.29.refs_0_, bf16[32,3072]{1,0:T(8,128)(2,1)S(1)} %collective-permute-done.5.refs_1_, bf16[32,3072]{1,0:T(8,128)(2,1)S(1)} %collective-permute-done.6.refs_2_, ...), custom_call_target="tpu_custom_call" | custom-call | bytes 786432 | tf_op jit(solution)/shard_map/wave/pallas_call | solution.py:330
  32.4 0.1 collective-permute-start.11
  32.4 0.8 %wave.4 = (bf16[128,2048]{1,0:T(8,128)(2,1)S(1)}, bf16[128,2048]{1,0:T(8,128)(2,1)S(1)}, f32[2,3072]{1,0:T(2,128)S(1)}) custom-call(s32[8,128]{1,0:T(8,128)S(1)} %get-tuple-element.29.refs_0_, bf16[32,3072]{1,0:T(8,128)(2,1)S(1)} %get-tuple-element.30.refs_1_, bf16[32,3072]{1,0:T(8,128)(2,1)S(1)} %collective-permute-done.refs_2_, ...), custom_call_target="tpu_custom_call" | custom-call | bytes 786432 | tf_op jit(solution)/shard_map/wave/pallas_call | solution.py:330
  33.2 0.6 %collective-permute-start.10 = (bf16[128,2048]{1,0:T(8,128)(2,1)S(1)}, bf16[128,2048]{1,0:T(8,128)(2,1)S(1)}, u32[]{:S(2)}, u32[]{:S(2)}) collective-permute-start(bf16[128,2048]{1,0:T(8,128)(2,1)S(1)} %get-tuple-element.38), channel_id=1, source_target_pairs={{0,1},{1,0},{2,3},{3,2},{4,5},{5,4},{6,7},{7,6},{8,9},{9,8},{10,11... | collective-permute-start | bytes 1572872 | tf_op jit(solution)/shard_map/ppermute | solution.py:486
  33.8 0.0 collective-permute-done.13.refs_3_
  33.8 0.4 collective-permute-done.14.refs_4_
  34.2 0.8 %wave.6 = (bf16[128,2048]{1,0:T(8,128)(2,1)S(1)}, bf16[128,2048]{1,0:T(8,128)(2,1)S(1)}, f32[2,3072]{1,0:T(2,128)S(1)}) custom-call(s32[8,128]{1,0:T(8,128)S(1)} %get-tuple-element.29.refs_0_, bf16[32,3072]{1,0:T(8,128)(2,1)S(1)} %collective-permute-done.7.refs_1_, bf16[32,3072]{1,0:T(8,128)(2,1)S(1)} %collective-permute-done.12.refs_2_, ...), custom_call_target="tpu_custom_call" | custom-call | bytes 786432 | tf_op jit(solution)/shard_map/wave/pallas_call | solution.py:330
  35.0 0.1 collective-permute-start.16
  35.1 1.8 %collective-permute-start.18 = (bf16[32,3072]{1,0:T(8,128)(2,1)S(1)}, bf16[32,3072]{1,0:T(8,128)(2,1)S(1)}, u32[]{:S(2)}, u32[]{:S(2)}) collective-permute-start(bf16[32,3072]{1,0:T(8,128)(2,1)S(1)} %collective-permute-done.4.refs_2_), channel_id=1, source_target_pairs={{0,4},{1,3},{2,6},{3,1},{4,0},{5,7},{6,2},{7,5},{8,12},{9,11},{10,... | collective-permute-start | bytes 589832 | tf_op jit(solution)/shard_map/ppermute | solution.py:483
  36.9 0.0 collective-permute-done.15.refs_3_
  36.9 0.6 %wave.7 = (bf16[96,2048]{1,0:T(8,128)(2,1)S(1)}, bf16[96,2048]{1,0:T(8,128)(2,1)S(1)}, f32[4,3072]{1,0:T(4,128)S(1)}) custom-call(s32[8,128]{1,0:T(8,128)S(1)} %get-tuple-element.29.refs_0_, bf16[32,3072]{1,0:T(8,128)(2,1)S(1)} %collective-permute-done.3.refs_1_, bf16[32,3072]{1,0:T(8,128)(2,1)S(1)} %collective-permute-done.4.refs_2_, ...), custom_call_target="tpu_custom_call" | custom-call | bytes 589824 | tf_op jit(solution)/shard_map/wave/pallas_call | solution.py:330
  37.5 0.1 collective-permute-start.17
  37.6 3.2 %collective-permute-done.18.refs_6_ = bf16[32,3072]{1,0:T(8,128)(2,1)S(1)} collective-permute-done((bf16[32,3072]{1,0:T(8,128)(2,1)S(1)}, bf16[32,3072]{1,0:T(8,128)(2,1)S(1)}, u32[]{:S(2)}, u32[]{:S(2)}) %collective-permute-start.18) | collective-permute-done | bytes 196640 | tf_op jit(solution)/shard_map/ppermute | solution.py:483
  40.8 0.0 collective-permute-start.19
  40.8 0.0 collective-permute-done.11.refs_4_
  40.8 0.0 collective-permute-done.10.refs_3_
  40.8 1.0 %partial.1.refs_1_ = f32[1024,1024]{1,0:T(8,128)S(1)} custom-call(s32[8,128]{1,0:T(8,128)S(1)} %get-tuple-element.29.refs_0_, bf16[128,2048]{1,0:T(8,128)(2,1)S(1)} %get-tuple-element.33.refs_1_, bf16[128,2048]{1,0:T(8,128)(2,1)S(1)} %get-tuple-element.37.refs_2_, bf16[128,2048]{1,0:T(8,128)(2,1)S(1)} %collective-permute-done.10.refs_3_, ...), custom_call_target="tpu_custom_call" | custom-call | flops 536870912 | tf_op jit(solution)/shard_map/partial/pallas_call | solution.py:384
  41.9 0.4 collective-permute-done.19.refs_7_
  42.3 0.0 collective-permute-done.17.refs_5_
  42.3 0.0 collective-permute-done.16.refs_4_
  42.3 2.7 %finish.1 = (f32[1,1024,1024]{2,1,0:T(8,128)}, f32[1,3072]{1,0:T(1,128)}, f32[1,3072]{1,0:T(1,128)}) custom-call(s32[8,128]{1,0:T(8,128)S(1)} %get-tuple-element.29.refs_0_, f32[1024,1024]{1,0:T(8,128)S(1)} %partial.1.refs_1_, bf16[128,2048]{1,0:T(8,128)(2,1)S(1)} %get-tuple-element.42.refs_2_, bf16[96,2048]{1,0:T(8,128)(2,1)S(1)} %get-tuple-element.44.refs_3_, ...), custom_call_target="tpu_custom_call" | custom-call | flops 536870912 | bytes 4194304 | tf_op jit(solution)/shard_map/finish/pallas_call | solution.py:442
Async XLA Ops:
  0.6 7.2 %collective-permute-start = (bf16[32,3072]{1,0:T(8,128)(2,1)}, bf16[32,3072]{1,0:T(8,128)(2,1)S(1)}, u32[]{:S(2)}, u32[]{:S(2)}) collective-permute-start(bf16[32,3072]{1,0:T(8,128)(2,1)} %refs_2_.1), channel_id=1, source_target_pairs={{0,2},{1,5},{2,0},{3,7},{4,6},{5,1},{6,4},{7,3},{8,10},{9,13},{10,... | collective-permute-start | bytes 589832 | tf_op jit(solution)/shard_map/ppermute | solution.py:483
  3.6 10.7 %collective-permute-start.5 = (bf16[32,3072]{1,0:T(8,128)(2,1)}, bf16[32,3072]{1,0:T(8,128)(2,1)S(1)}, u32[]{:S(2)}, u32[]{:S(2)}) collective-permute-start(bf16[32,3072]{1,0:T(8,128)(2,1)} %refs_2_.1), channel_id=1, source_target_pairs={{0,8},{2,10},{4,12},{6,14},{8,0},{10,2},{12,4},{14,6},{16,24},{18,... | collective-permute-start | bytes 589832 | tf_op jit(solution)/shard_map/ppermute | solution.py:475
  5.2 13.1 %collective-permute-start.7 = (bf16[32,3072]{1,0:T(8,128)(2,1)}, bf16[32,3072]{1,0:T(8,128)(2,1)S(1)}, u32[]{:S(2)}, u32[]{:S(2)}) collective-permute-start(bf16[32,3072]{1,0:T(8,128)(2,1)} %refs_2_.1), channel_id=1, source_target_pairs={{0,16},{2,18},{4,20},{6,22},{8,24},{10,26},{12,28},{14,30},{16,0},... | collective-permute-start | bytes 589832 | tf_op jit(solution)/shard_map/ppermute | solution.py:475
  7.8 11.0 %collective-permute-start.1 = (bf16[32,3072]{1,0:T(8,128)(2,1)}, bf16[32,3072]{1,0:T(8,128)(2,1)S(1)}, u32[]{:S(2)}, u32[]{:S(2)}) collective-permute-start(bf16[32,3072]{1,0:T(8,128)(2,1)} %refs_2_.1), channel_id=1, source_target_pairs={{0,4},{1,3},{2,6},{3,1},{4,0},{5,7},{6,2},{7,5},{8,12},{9,11},{10,... | collective-permute-start | bytes 589832 | tf_op jit(solution)/shard_map/ppermute | solution.py:483
  9.5 9.9 %collective-permute-start.2 = (bf16[32,3072]{1,0:T(8,128)(2,1)S(1)}, bf16[32,3072]{1,0:T(8,128)(2,1)S(1)}, u32[]{:S(2)}, u32[]{:S(2)}) collective-permute-start(bf16[32,3072]{1,0:T(8,128)(2,1)S(1)} %collective-permute-done.refs_2_), channel_id=1, source_target_pairs={{0,4},{1,3},{2,6},{3,1},{4,0},{5,7},{6,2},{7,5},{8,12},{9,11},{10,... | collective-permute-start | bytes 589832 | tf_op jit(solution)/shard_map/ppermute | solution.py:483
  14.3 7.0 %collective-permute-start.6 = (bf16[32,3072]{1,0:T(8,128)(2,1)S(1)}, bf16[32,3072]{1,0:T(8,128)(2,1)S(1)}, u32[]{:S(2)}, u32[]{:S(2)}) collective-permute-start(bf16[32,3072]{1,0:T(8,128)(2,1)S(1)} %collective-permute-done.5.refs_1_), channel_id=1, source_target_pairs={{0,2},{1,5},{2,0},{3,7},{4,6},{5,1},{6,4},{7,3},{8,10},{9,13},{10,... | collective-permute-start | bytes 589832 | tf_op jit(solution)/shard_map/ppermute | solution.py:483
  15.8 7.8 %collective-permute-start.3 = (bf16[32,3072]{1,0:T(8,128)(2,1)}, bf16[32,3072]{1,0:T(8,128)(2,1)S(1)}, u32[]{:S(2)}, u32[]{:S(2)}) collective-permute-start(bf16[32,3072]{1,0:T(8,128)(2,1)} %refs_2_.1), channel_id=1, source_target_pairs={{0,24},{2,26},{4,28},{6,30},{8,16},{10,18},{12,20},{14,22},{16,8},... | collective-permute-start | bytes 589832 | tf_op jit(solution)/shard_map/ppermute | solution.py:475
  18.3 7.3 %collective-permute-start.8 = (bf16[32,3072]{1,0:T(8,128)(2,1)S(1)}, bf16[32,3072]{1,0:T(8,128)(2,1)S(1)}, u32[]{:S(2)}, u32[]{:S(2)}) collective-permute-start(bf16[32,3072]{1,0:T(8,128)(2,1)S(1)} %collective-permute-done.5.refs_1_), channel_id=1, source_target_pairs={{0,4},{1,3},{2,6},{3,1},{4,0},{5,7},{6,2},{7,5},{8,12},{9,11},{10,... | collective-permute-start | bytes 589832 | tf_op jit(solution)/shard_map/ppermute | solution.py:483
  18.8 7.7 %collective-permute-start.12 = (bf16[32,3072]{1,0:T(8,128)(2,1)S(1)}, bf16[32,3072]{1,0:T(8,128)(2,1)S(1)}, u32[]{:S(2)}, u32[]{:S(2)}) collective-permute-start(bf16[32,3072]{1,0:T(8,128)(2,1)S(1)} %collective-permute-done.7.refs_1_), channel_id=1, source_target_pairs={{0,2},{1,5},{2,0},{3,7},{4,6},{5,1},{6,4},{7,3},{8,10},{9,13},{10,... | collective-permute-start | bytes 589832 | tf_op jit(solution)/shard_map/ppermute | solution.py:483
  21.4 7.2 %collective-permute-start.9 = (bf16[32,3072]{1,0:T(8,128)(2,1)S(1)}, bf16[32,3072]{1,0:T(8,128)(2,1)S(1)}, u32[]{:S(2)}, u32[]{:S(2)}) collective-permute-start(bf16[32,3072]{1,0:T(8,128)(2,1)S(1)} %collective-permute-done.6.refs_2_), channel_id=1, source_target_pairs={{0,4},{1,3},{2,6},{3,1},{4,0},{5,7},{6,2},{7,5},{8,12},{9,11},{10,... | collective-permute-start | bytes 589832 | tf_op jit(solution)/shard_map/ppermute | solution.py:483
  23.6 8.0 %collective-permute-start.4 = (bf16[32,3072]{1,0:T(8,128)(2,1)S(1)}, bf16[32,3072]{1,0:T(8,128)(2,1)S(1)}, u32[]{:S(2)}, u32[]{:S(2)}) collective-permute-start(bf16[32,3072]{1,0:T(8,128)(2,1)S(1)} %collective-permute-done.3.refs_1_), channel_id=1, source_target_pairs={{0,2},{1,5},{2,0},{3,7},{4,6},{5,1},{6,4},{7,3},{8,10},{9,13},{10,... | collective-permute-start | bytes 589832 | tf_op jit(solution)/shard_map/ppermute | solution.py:483
  25.6 8.2 %collective-permute-start.13 = (bf16[32,3072]{1,0:T(8,128)(2,1)S(1)}, bf16[32,3072]{1,0:T(8,128)(2,1)S(1)}, u32[]{:S(2)}, u32[]{:S(2)}) collective-permute-start(bf16[32,3072]{1,0:T(8,128)(2,1)S(1)} %collective-permute-done.7.refs_1_), channel_id=1, source_target_pairs={{0,4},{1,3},{2,6},{3,1},{4,0},{5,7},{6,2},{7,5},{8,12},{9,11},{10,... | collective-permute-start | bytes 589832 | tf_op jit(solution)/shard_map/ppermute | solution.py:483
  28.5 5.7 %collective-permute-start.14 = (bf16[32,3072]{1,0:T(8,128)(2,1)S(1)}, bf16[32,3072]{1,0:T(8,128)(2,1)S(1)}, u32[]{:S(2)}, u32[]{:S(2)}) collective-permute-start(bf16[32,3072]{1,0:T(8,128)(2,1)S(1)} %collective-permute-done.12.refs_2_), channel_id=1, source_target_pairs={{0,4},{1,3},{2,6},{3,1},{4,0},{5,7},{6,2},{7,5},{8,12},{9,11},{10,... | collective-permute-start | bytes 589832 | tf_op jit(solution)/shard_map/ppermute | solution.py:483
  30.3 6.6 %collective-permute-start.15 = (bf16[32,3072]{1,0:T(8,128)(2,1)S(1)}, bf16[32,3072]{1,0:T(8,128)(2,1)S(1)}, u32[]{:S(2)}, u32[]{:S(2)}) collective-permute-start(bf16[32,3072]{1,0:T(8,128)(2,1)S(1)} %collective-permute-done.3.refs_1_), channel_id=1, source_target_pairs={{0,4},{1,3},{2,6},{3,1},{4,0},{5,7},{6,2},{7,5},{8,12},{9,11},{10,... | collective-permute-start | bytes 589832 | tf_op jit(solution)/shard_map/ppermute | solution.py:483
  32.4 8.5 %collective-permute-start.11 = (bf16[128,2048]{1,0:T(8,128)(2,1)S(1)}, bf16[128,2048]{1,0:T(8,128)(2,1)S(1)}, u32[]{:S(2)}, u32[]{:S(2)}) collective-permute-start(bf16[128,2048]{1,0:T(8,128)(2,1)S(1)} %get-tuple-element.39), channel_id=1, source_target_pairs={{0,1},{1,0},{2,3},{3,2},{4,5},{5,4},{6,7},{7,6},{8,9},{9,8},{10,11... | collective-permute-start | bytes 1572872 | tf_op jit(solution)/shard_map/ppermute | solution.py:486
  33.2 7.6 %collective-permute-start.10 = (bf16[128,2048]{1,0:T(8,128)(2,1)S(1)}, bf16[128,2048]{1,0:T(8,128)(2,1)S(1)}, u32[]{:S(2)}, u32[]{:S(2)}) collective-permute-start(bf16[128,2048]{1,0:T(8,128)(2,1)S(1)} %get-tuple-element.38), channel_id=1, source_target_pairs={{0,1},{1,0},{2,3},{3,2},{4,5},{5,4},{6,7},{7,6},{8,9},{9,8},{10,11... | collective-permute-start | bytes 1572872 | tf_op jit(solution)/shard_map/ppermute | solution.py:486
  35.0 7.3 %collective-permute-start.16 = (bf16[128,2048]{1,0:T(8,128)(2,1)S(1)}, bf16[128,2048]{1,0:T(8,128)(2,1)S(1)}, u32[]{:S(2)}, u32[]{:S(2)}) collective-permute-start(bf16[128,2048]{1,0:T(8,128)(2,1)S(1)} %get-tuple-element.45), channel_id=1, source_target_pairs={{0,1},{1,0},{2,3},{3,2},{4,5},{5,4},{6,7},{7,6},{8,9},{9,8},{10,11... | collective-permute-start | bytes 1572872 | tf_op jit(solution)/shard_map/ppermute | solution.py:486
  35.1 5.7 %collective-permute-start.18 = (bf16[32,3072]{1,0:T(8,128)(2,1)S(1)}, bf16[32,3072]{1,0:T(8,128)(2,1)S(1)}, u32[]{:S(2)}, u32[]{:S(2)}) collective-permute-start(bf16[32,3072]{1,0:T(8,128)(2,1)S(1)} %collective-permute-done.4.refs_2_), channel_id=1, source_target_pairs={{0,4},{1,3},{2,6},{3,1},{4,0},{5,7},{6,2},{7,5},{8,12},{9,11},{10,... | collective-permute-start | bytes 589832 | tf_op jit(solution)/shard_map/ppermute | solution.py:483
  37.5 4.8 %collective-permute-start.17 = (bf16[96,2048]{1,0:T(8,128)(2,1)S(1)}, bf16[96,2048]{1,0:T(8,128)(2,1)S(1)}, u32[]{:S(2)}, u32[]{:S(2)}) collective-permute-start(bf16[96,2048]{1,0:T(8,128)(2,1)S(1)} %get-tuple-element.46), channel_id=1, source_target_pairs={{0,1},{1,0},{2,3},{3,2},{4,5},{5,4},{6,7},{7,6},{8,9},{9,8},{10,11... | collective-permute-start | bytes 1179656 | tf_op jit(solution)/shard_map/ppermute | solution.py:486
  40.8 1.4 %collective-permute-start.19 = (bf16[32,3072]{1,0:T(8,128)(2,1)S(1)}, bf16[32,3072]{1,0:T(8,128)(2,1)S(1)}, u32[]{:S(2)}, u32[]{:S(2)}) collective-permute-start(bf16[32,3072]{1,0:T(8,128)(2,1)S(1)} %collective-permute-done.18.refs_6_), channel_id=1, source_target_pairs={{0,1},{1,0},{2,3},{3,2},{4,5},{5,4},{6,7},{7,6},{8,9},{9,8},{10,11... | collective-permute-start | bytes 589832 | tf_op jit(solution)/shard_map/ppermute | solution.py:486

commit v5 on v4

--- a/solution.py
+++ b/solution.py
@@ -490,17 +490,17 @@
     s0 = from_plane(activations, True)
     z3 = from_outer(after(activations, s0), 3)
     b0 = from_plane(after(activations, s0), False)
-    f0 = from_plane(s0, False)
+    f0 = from_plane(after(s0, plan), False)
     s1 = from_plane(z1, True)
     b1 = from_plane(after(z1, z2), False)
     f1 = from_plane(after(s1, b0, f0, z2), False)
     s2 = from_plane(z2, True)
     b2 = from_plane(after(z2, b1), False)
-    f2 = from_plane(after(s2, f1, b1, z3), False)
     s3 = from_plane(z3, True)
     b3 = from_plane(z3, False)
     f3 = from_plane(after(s3, b1, b2), False)
-    own0, out0, stats0 = wave_parts(plan, [own_shard, s0, b0, after(f0, s3)])
+    own0, out0, stats0 = wave_parts(plan, [own_shard, s0, b0, after(f0, s1)])
+    f2 = from_plane(after(s2, f1, b1, z3, own0), False)
     other0 = from_sibling(out0)
     own1, out1, stats1 = wave_parts(plan, [z1, s1, b1, after(f1, f1)])
     other1 = from_sibling(out1)

time: 45.2 us -> 44.9 us (level)
  waiting for transfers between devices: 15.5 us -> 13 us
  starting transfers between devices: 21.1 us -> 23.2 us
    ppermute x12, starting transfers between devices: 13.7 us -> 15.9 us  [from_plane(): return lax.ppermute(a, ('tok', 'col'), pairs)]
    ppermute x3, waiting for transfers between devices: 6.72 us -> 5.44 us  [from_outer(): return lax.ppermute(a, 'tok', [(t, t ^ 4 * k) for t in range(n_tok)])]
    ppermute x12, waiting for transfers between devices: 8.31 us -> 7.11 us  [from_plane(): return lax.ppermute(a, ('tok', 'col'), pairs)]
where the time goes in v5:
time: 44.9 us; the launch traced here: 44.7 us
  starting transfers between devices  23.2 us (52%)
  waiting for transfers between devices  13 us (29%)
  Pallas kernels  7.8 us (17%)
  between operations  0.73 us (2%)
    ppermute x12, starting transfers between devices, from_plane(): return lax.ppermute(a, ('tok', 'col'), pairs)  15.9 us
    ppermute x12, waiting for transfers between devices, from_plane(): return lax.ppermute(a, ('tok', 'col'), pairs)  7.11 us
    ppermute x3, starting transfers between devices, from_outer(): return lax.ppermute(a, 'tok', [(t, t ^ 4 * k) for t in range(n_tok)])  6.64 us
    ppermute x3, waiting for transfers between devices, from_outer(): return lax.ppermute(a, 'tok', [(t, t ^ 4 * k) for t in range(n_tok)])  5.44 us
    pallas_call x4, Pallas kernels, wave_parts(): pl.pallas_call(lambda *refs: wave_kernel(sizes, *refs), out_shape=[near.o...  3.07 us
    pallas_call x1, Pallas kernels, finish(): pl.pallas_call(lambda *refs: finish_kernel(total_tokens, len(own), *refs)...  2.72 us
    pallas_call x1, Pallas kernels, partial_gram(): pl.pallas_call(lambda *refs: partial_kernel(held, *refs), out_shape=near....  1.02 us
    pallas_call x1, Pallas kernels, make_plan(): pl.pallas_call(lambda *refs: plan_kernel(block_count, *refs), out_shape=[...  1 us
  transfers between devices with their start and end apart: 20, of which 8 were waited for; matrix products, arithmetic and copies ran while one was open for 0% of the time, Pallas kernels for 11%

profile of v5, /device:TPU:0, one launch (start us, length us, event | category | flops | bytes accessed | tf_op | source)
XLA Modules:
  0.0 44.7 jit_solution(9790511280448930146)
XLA Ops:
  0.6 3.0 %collective-permute-start = (bf16[32,3072]{1,0:T(8,128)(2,1)}, bf16[32,3072]{1,0:T(8,128)(2,1)S(1)}, u32[]{:S(2)}, u32[]{:S(2)}) collective-permute-start(bf16[32,3072]{1,0:T(8,128)(2,1)} %refs_2_.1), channel_id=1, source_target_pairs={{0,2},{1,5},{2,0},{3,7},{4,6},{5,1},{6,4},{7,3},{8,10},{9,13},{10,... | collective-permute-start | bytes 589832 | tf_op jit(solution)/shard_map/ppermute | solution.py:483
  3.6 1.6 %collective-permute-start.3 = (bf16[32,3072]{1,0:T(8,128)(2,1)}, bf16[32,3072]{1,0:T(8,128)(2,1)S(1)}, u32[]{:S(2)}, u32[]{:S(2)}) collective-permute-start(bf16[32,3072]{1,0:T(8,128)(2,1)} %refs_2_.1), channel_id=1, source_target_pairs={{0,8},{2,10},{4,12},{6,14},{8,0},{10,2},{12,4},{14,6},{16,24},{18,... | collective-permute-start | bytes 589832 | tf_op jit(solution)/shard_map/ppermute | solution.py:475
  5.2 2.6 %collective-permute-start.5 = (bf16[32,3072]{1,0:T(8,128)(2,1)}, bf16[32,3072]{1,0:T(8,128)(2,1)S(1)}, u32[]{:S(2)}, u32[]{:S(2)}) collective-permute-start(bf16[32,3072]{1,0:T(8,128)(2,1)} %refs_2_.1), channel_id=1, source_target_pairs={{0,16},{2,18},{4,20},{6,22},{8,24},{10,26},{12,28},{14,30},{16,0},... | collective-permute-start | bytes 589832 | tf_op jit(solution)/shard_map/ppermute | solution.py:475
  7.8 1.0 %plan.1 = (s32[8,128]{1,0:T(8,128)S(1)}, bf16[32,3072]{1,0:T(8,128)(2,1)S(1)}) custom-call(s32[6]{0:T(128)} %refs_0_.1, s32[32]{0:T(128)} %refs_1_.1, bf16[32,3072]{1,0:T(8,128)(2,1)} %refs_2_.1), custom_call_target="tpu_custom_call" | custom-call | tf_op jit(solution)/shard_map/plan/pallas_call | solution.py:254
  8.8 0.0 collective-permute-done.refs_2_
  8.8 1.6 %collective-permute-start.1 = (bf16[32,3072]{1,0:T(8,128)(2,1)}, bf16[32,3072]{1,0:T(8,128)(2,1)S(1)}, u32[]{:S(2)}, u32[]{:S(2)}) collective-permute-start(bf16[32,3072]{1,0:T(8,128)(2,1)} %refs_2_.1), channel_id=1, source_target_pairs={{0,4},{1,3},{2,6},{3,1},{4,0},{5,7},{6,2},{7,5},{8,12},{9,11},{10,... | collective-permute-start | bytes 589832 | tf_op jit(solution)/shard_map/ppermute | solution.py:483
  10.4 0.5 %collective-permute-start.2 = (bf16[32,3072]{1,0:T(8,128)(2,1)S(1)}, bf16[32,3072]{1,0:T(8,128)(2,1)S(1)}, u32[]{:S(2)}, u32[]{:S(2)}) collective-permute-start(bf16[32,3072]{1,0:T(8,128)(2,1)S(1)} %collective-permute-done.refs_2_), channel_id=1, source_target_pairs={{0,4},{1,3},{2,6},{3,1},{4,0},{5,7},{6,2},{7,5},{8,12},{9,11},{10,... | collective-permute-start | bytes 589832 | tf_op jit(solution)/shard_map/ppermute | solution.py:483
  10.9 3.4 %collective-permute-done.3.refs_1_ = bf16[32,3072]{1,0:T(8,128)(2,1)S(1)} collective-permute-done((bf16[32,3072]{1,0:T(8,128)(2,1)}, bf16[32,3072]{1,0:T(8,128)(2,1)S(1)}, u32[]{:S(2)}, u32[]{:S(2)}) %collective-permute-start.3) | collective-permute-done | bytes 196640 | tf_op jit(solution)/shard_map/ppermute | solution.py:475
  14.3 1.5 %collective-permute-start.4 = (bf16[32,3072]{1,0:T(8,128)(2,1)S(1)}, bf16[32,3072]{1,0:T(8,128)(2,1)S(1)}, u32[]{:S(2)}, u32[]{:S(2)}) collective-permute-start(bf16[32,3072]{1,0:T(8,128)(2,1)S(1)} %collective-permute-done.3.refs_1_), channel_id=1, source_target_pairs={{0,2},{1,5},{2,0},{3,7},{4,6},{5,1},{6,4},{7,3},{8,10},{9,13},{10,... | collective-permute-start | bytes 589832 | tf_op jit(solution)/shard_map/ppermute | solution.py:483
  15.8 0.9 %collective-permute-done.5.refs_1_ = bf16[32,3072]{1,0:T(8,128)(2,1)S(1)} collective-permute-done((bf16[32,3072]{1,0:T(8,128)(2,1)}, bf16[32,3072]{1,0:T(8,128)(2,1)S(1)}, u32[]{:S(2)}, u32[]{:S(2)}) %collective-permute-start.5) | collective-permute-done | bytes 196640 | tf_op jit(solution)/shard_map/ppermute | solution.py:475
  16.7 0.5 %collective-permute-start.6 = (bf16[32,3072]{1,0:T(8,128)(2,1)S(1)}, bf16[32,3072]{1,0:T(8,128)(2,1)S(1)}, u32[]{:S(2)}, u32[]{:S(2)}) collective-permute-start(bf16[32,3072]{1,0:T(8,128)(2,1)S(1)} %collective-permute-done.3.refs_1_), channel_id=1, source_target_pairs={{0,4},{1,3},{2,6},{3,1},{4,0},{5,7},{6,2},{7,5},{8,12},{9,11},{10,... | collective-permute-start | bytes 589832 | tf_op jit(solution)/shard_map/ppermute | solution.py:483
  17.2 2.5 %collective-permute-start.12 = (bf16[32,3072]{1,0:T(8,128)(2,1)}, bf16[32,3072]{1,0:T(8,128)(2,1)S(1)}, u32[]{:S(2)}, u32[]{:S(2)}) collective-permute-start(bf16[32,3072]{1,0:T(8,128)(2,1)} %refs_2_.1), channel_id=1, source_target_pairs={{0,24},{2,26},{4,28},{6,30},{8,16},{10,18},{12,20},{14,22},{16,8},... | collective-permute-start | bytes 589832 | tf_op jit(solution)/shard_map/ppermute | solution.py:475
  19.7 0.0 collective-permute-done.1.refs_3_
  19.7 1.5 %collective-permute-start.10 = (bf16[32,3072]{1,0:T(8,128)(2,1)S(1)}, bf16[32,3072]{1,0:T(8,128)(2,1)S(1)}, u32[]{:S(2)}, u32[]{:S(2)}) collective-permute-start(bf16[32,3072]{1,0:T(8,128)(2,1)S(1)} %collective-permute-done.5.refs_1_), channel_id=1, source_target_pairs={{0,2},{1,5},{2,0},{3,7},{4,6},{5,1},{6,4},{7,3},{8,10},{9,13},{10,... | collective-permute-start | bytes 589832 | tf_op jit(solution)/shard_map/ppermute | solution.py:483
  21.2 0.0 collective-permute-done.2.refs_4_
  21.2 0.0 collective-permute-done.4.refs_2_
  21.2 1.5 %collective-permute-start.7 = (bf16[32,3072]{1,0:T(8,128)(2,1)S(1)}, bf16[32,3072]{1,0:T(8,128)(2,1)S(1)}, u32[]{:S(2)}, u32[]{:S(2)}) collective-permute-start(bf16[32,3072]{1,0:T(8,128)(2,1)S(1)} %collective-permute-done.4.refs_2_), channel_id=1, source_target_pairs={{0,4},{1,3},{2,6},{3,1},{4,0},{5,7},{6,2},{7,5},{8,12},{9,11},{10,... | collective-permute-start | bytes 589832 | tf_op jit(solution)/shard_map/ppermute | solution.py:483
  22.7 0.0 collective-permute-done.6.refs_3_
  22.7 0.5 %collective-permute-start.11 = (bf16[32,3072]{1,0:T(8,128)(2,1)S(1)}, bf16[32,3072]{1,0:T(8,128)(2,1)S(1)}, u32[]{:S(2)}, u32[]{:S(2)}) collective-permute-start(bf16[32,3072]{1,0:T(8,128)(2,1)S(1)} %collective-permute-done.5.refs_1_), channel_id=1, source_target_pairs={{0,4},{1,3},{2,6},{3,1},{4,0},{5,7},{6,2},{7,5},{8,12},{9,11},{10,... | collective-permute-start | bytes 589832 | tf_op jit(solution)/shard_map/ppermute | solution.py:483
  23.2 0.8 %wave.4 = (bf16[128,2048]{1,0:T(8,128)(2,1)S(1)}, bf16[128,2048]{1,0:T(8,128)(2,1)S(1)}, f32[2,3072]{1,0:T(2,128)S(1)}) custom-call(s32[8,128]{1,0:T(8,128)S(1)} %get-tuple-element.30.refs_0_, bf16[32,3072]{1,0:T(8,128)(2,1)S(1)} %get-tuple-element.31.refs_1_, bf16[32,3072]{1,0:T(8,128)(2,1)S(1)} %collective-permute-done.refs_2_, ...), custom_call_target="tpu_custom_call" | custom-call | bytes 786432 | tf_op jit(solution)/shard_map/wave/pallas_call | solution.py:330
  24.1 1.1 %collective-permute-done.12.refs_1_ = bf16[32,3072]{1,0:T(8,128)(2,1)S(1)} collective-permute-done((bf16[32,3072]{1,0:T(8,128)(2,1)}, bf16[32,3072]{1,0:T(8,128)(2,1)S(1)}, u32[]{:S(2)}, u32[]{:S(2)}) %collective-permute-start.12) | collective-permute-done | bytes 196640 | tf_op jit(solution)/shard_map/ppermute | solution.py:475
  25.2 2.2 %collective-permute-done.10.refs_2_ = bf16[32,3072]{1,0:T(8,128)(2,1)S(1)} collective-permute-done((bf16[32,3072]{1,0:T(8,128)(2,1)S(1)}, bf16[32,3072]{1,0:T(8,128)(2,1)S(1)}, u32[]{:S(2)}, u32[]{:S(2)}) %collective-permute-start.10) | collective-permute-done | bytes 196640 | tf_op jit(solution)/shard_map/ppermute | solution.py:483
  27.4 0.0 collective-permute-done.7.refs_4_
  27.4 1.5 %collective-permute-start.13 = (bf16[32,3072]{1,0:T(8,128)(2,1)S(1)}, bf16[32,3072]{1,0:T(8,128)(2,1)S(1)}, u32[]{:S(2)}, u32[]{:S(2)}) collective-permute-start(bf16[32,3072]{1,0:T(8,128)(2,1)S(1)} %collective-permute-done.10.refs_2_), channel_id=1, source_target_pairs={{0,4},{1,3},{2,6},{3,1},{4,0},{5,7},{6,2},{7,5},{8,12},{9,11},{10,... | collective-permute-start | bytes 589832 | tf_op jit(solution)/shard_map/ppermute | solution.py:483
  29.0 1.1 %collective-permute-start.14 = (bf16[32,3072]{1,0:T(8,128)(2,1)S(1)}, bf16[32,3072]{1,0:T(8,128)(2,1)S(1)}, u32[]{:S(2)}, u32[]{:S(2)}) collective-permute-start(bf16[32,3072]{1,0:T(8,128)(2,1)S(1)} %collective-permute-done.12.refs_1_), channel_id=1, source_target_pairs={{0,2},{1,5},{2,0},{3,7},{4,6},{5,1},{6,4},{7,3},{8,10},{9,13},{10,... | collective-permute-start | bytes 589832 | tf_op jit(solution)/shard_map/ppermute | solution.py:483
  30.0 1.0 %collective-permute-start.15 = (bf16[32,3072]{1,0:T(8,128)(2,1)S(1)}, bf16[32,3072]{1,0:T(8,128)(2,1)S(1)}, u32[]{:S(2)}, u32[]{:S(2)}) collective-permute-start(bf16[32,3072]{1,0:T(8,128)(2,1)S(1)} %collective-permute-done.12.refs_1_), channel_id=1, source_target_pairs={{0,4},{1,3},{2,6},{3,1},{4,0},{5,7},{6,2},{7,5},{8,12},{9,11},{10,... | collective-permute-start | bytes 589832 | tf_op jit(solution)/shard_map/ppermute | solution.py:483
  31.0 0.0 collective-permute-start.8
  31.0 0.8 %wave.5 = (bf16[128,2048]{1,0:T(8,128)(2,1)S(1)}, bf16[128,2048]{1,0:T(8,128)(2,1)S(1)}, f32[2,3072]{1,0:T(2,128)S(1)}) custom-call(s32[8,128]{1,0:T(8,128)S(1)} %get-tuple-element.30.refs_0_, bf16[32,3072]{1,0:T(8,128)(2,1)S(1)} %collective-permute-done.3.refs_1_, bf16[32,3072]{1,0:T(8,128)(2,1)S(1)} %collective-permute-done.4.refs_2_, ...), custom_call_target="tpu_custom_call" | custom-call | bytes 786432 | tf_op jit(solution)/shard_map/wave/pallas_call | solution.py:330
  31.9 0.0 collective-permute-done.11.refs_3_
  31.9 0.5 %collective-permute-start.9 = (bf16[128,2048]{1,0:T(8,128)(2,1)S(1)}, bf16[128,2048]{1,0:T(8,128)(2,1)S(1)}, u32[]{:S(2)}, u32[]{:S(2)}) collective-permute-start(bf16[128,2048]{1,0:T(8,128)(2,1)S(1)} %get-tuple-element.41), channel_id=1, source_target_pairs={{0,1},{1,0},{2,3},{3,2},{4,5},{5,4},{6,7},{7,6},{8,9},{9,8},{10,11... | collective-permute-start | bytes 1572872 | tf_op jit(solution)/shard_map/ppermute | solution.py:486
  32.4 0.8 %collective-permute-done.13.refs_4_ = bf16[32,3072]{1,0:T(8,128)(2,1)S(1)} collective-permute-done((bf16[32,3072]{1,0:T(8,128)(2,1)S(1)}, bf16[32,3072]{1,0:T(8,128)(2,1)S(1)}, u32[]{:S(2)}, u32[]{:S(2)}) %collective-permute-start.13) | collective-permute-done | bytes 196640 | tf_op jit(solution)/shard_map/ppermute | solution.py:483
  33.2 0.8 %wave.6 = (bf16[128,2048]{1,0:T(8,128)(2,1)S(1)}, bf16[128,2048]{1,0:T(8,128)(2,1)S(1)}, f32[2,3072]{1,0:T(2,128)S(1)}) custom-call(s32[8,128]{1,0:T(8,128)S(1)} %get-tuple-element.30.refs_0_, bf16[32,3072]{1,0:T(8,128)(2,1)S(1)} %collective-permute-done.5.refs_1_, bf16[32,3072]{1,0:T(8,128)(2,1)S(1)} %collective-permute-done.10.refs_2_, ...), custom_call_target="tpu_custom_call" | custom-call | bytes 786432 | tf_op jit(solution)/shard_map/wave/pallas_call | solution.py:330
  34.0 0.1 collective-permute-start.16
  34.1 0.8 %collective-permute-done.14.refs_2_ = bf16[32,3072]{1,0:T(8,128)(2,1)S(1)} collective-permute-done((bf16[32,3072]{1,0:T(8,128)(2,1)S(1)}, bf16[32,3072]{1,0:T(8,128)(2,1)S(1)}, u32[]{:S(2)}, u32[]{:S(2)}) %collective-permute-start.14) | collective-permute-done | bytes 196640 | tf_op jit(solution)/shard_map/ppermute | solution.py:483
  34.9 1.7 %collective-permute-start.18 = (bf16[32,3072]{1,0:T(8,128)(2,1)S(1)}, bf16[32,3072]{1,0:T(8,128)(2,1)S(1)}, u32[]{:S(2)}, u32[]{:S(2)}) collective-permute-start(bf16[32,3072]{1,0:T(8,128)(2,1)S(1)} %collective-permute-done.14.refs_2_), channel_id=1, source_target_pairs={{0,4},{1,3},{2,6},{3,1},{4,0},{5,7},{6,2},{7,5},{8,12},{9,11},{10,... | collective-permute-start | bytes 589832 | tf_op jit(solution)/shard_map/ppermute | solution.py:483
  36.5 0.0 collective-permute-done.15.refs_3_
  36.5 0.6 %wave.7 = (bf16[96,2048]{1,0:T(8,128)(2,1)S(1)}, bf16[96,2048]{1,0:T(8,128)(2,1)S(1)}, f32[4,3072]{1,0:T(4,128)S(1)}) custom-call(s32[8,128]{1,0:T(8,128)S(1)} %get-tuple-element.30.refs_0_, bf16[32,3072]{1,0:T(8,128)(2,1)S(1)} %collective-permute-done.12.refs_1_, bf16[32,3072]{1,0:T(8,128)(2,1)S(1)} %collective-permute-done.14.refs_2_, ...), custom_call_target="tpu_custom_call" | custom-call | bytes 589824 | tf_op jit(solution)/shard_map/wave/pallas_call | solution.py:330
  37.2 0.1 collective-permute-start.17
  37.2 3.3 %collective-permute-done.18.refs_6_ = bf16[32,3072]{1,0:T(8,128)(2,1)S(1)} collective-permute-done((bf16[32,3072]{1,0:T(8,128)(2,1)S(1)}, bf16[32,3072]{1,0:T(8,128)(2,1)S(1)}, u32[]{:S(2)}, u32[]{:S(2)}) %collective-permute-start.18) | collective-permute-done | bytes 196640 | tf_op jit(solution)/shard_map/ppermute | solution.py:483
  40.5 0.0 collective-permute-start.19
  40.5 0.0 collective-permute-done.8.refs_3_
  40.5 0.0 collective-permute-done.9.refs_4_
  40.5 1.0 %partial.1.refs_1_ = f32[1024,1024]{1,0:T(8,128)S(1)} custom-call(s32[8,128]{1,0:T(8,128)S(1)} %get-tuple-element.30.refs_0_, bf16[128,2048]{1,0:T(8,128)(2,1)S(1)} %get-tuple-element.35.refs_1_, bf16[128,2048]{1,0:T(8,128)(2,1)S(1)} %get-tuple-element.39.refs_2_, bf16[128,2048]{1,0:T(8,128)(2,1)S(1)} %collective-permute-done.8.refs_3_, ...), custom_call_target="tpu_custom_call" | custom-call | flops 536870912 | tf_op jit(solution)/shard_map/partial/pallas_call | solution.py:384
  41.6 0.4 collective-permute-done.19.refs_7_
  42.0 0.0 collective-permute-done.17.refs_5_
  42.0 0.0 collective-permute-done.16.refs_4_
  42.0 2.7 %finish.1 = (f32[1,1024,1024]{2,1,0:T(8,128)}, f32[1,3072]{1,0:T(1,128)}, f32[1,3072]{1,0:T(1,128)}) custom-call(s32[8,128]{1,0:T(8,128)S(1)} %get-tuple-element.30.refs_0_, f32[1024,1024]{1,0:T(8,128)S(1)} %partial.1.refs_1_, bf16[128,2048]{1,0:T(8,128)(2,1)S(1)} %get-tuple-element.44.refs_2_, bf16[96,2048]{1,0:T(8,128)(2,1)S(1)} %get-tuple-element.46.refs_3_, ...), custom_call_target="tpu_custom_call" | custom-call | flops 536870912 | bytes 4194304 | tf_op jit(solution)/shard_map/finish/pallas_call | solution.py:442
Async XLA Ops:
  0.6 8.2 %collective-permute-start = (bf16[32,3072]{1,0:T(8,128)(2,1)}, bf16[32,3072]{1,0:T(8,128)(2,1)S(1)}, u32[]{:S(2)}, u32[]{:S(2)}) collective-permute-start(bf16[32,3072]{1,0:T(8,128)(2,1)} %refs_2_.1), channel_id=1, source_target_pairs={{0,2},{1,5},{2,0},{3,7},{4,6},{5,1},{6,4},{7,3},{8,10},{9,13},{10,... | collective-permute-start | bytes 589832 | tf_op jit(solution)/shard_map/ppermute | solution.py:483
  3.6 10.7 %collective-permute-start.3 = (bf16[32,3072]{1,0:T(8,128)(2,1)}, bf16[32,3072]{1,0:T(8,128)(2,1)S(1)}, u32[]{:S(2)}, u32[]{:S(2)}) collective-permute-start(bf16[32,3072]{1,0:T(8,128)(2,1)} %refs_2_.1), channel_id=1, source_target_pairs={{0,8},{2,10},{4,12},{6,14},{8,0},{10,2},{12,4},{14,6},{16,24},{18,... | collective-permute-start | bytes 589832 | tf_op jit(solution)/shard_map/ppermute | solution.py:475
  5.2 11.5 %collective-permute-start.5 = (bf16[32,3072]{1,0:T(8,128)(2,1)}, bf16[32,3072]{1,0:T(8,128)(2,1)S(1)}, u32[]{:S(2)}, u32[]{:S(2)}) collective-permute-start(bf16[32,3072]{1,0:T(8,128)(2,1)} %refs_2_.1), channel_id=1, source_target_pairs={{0,16},{2,18},{4,20},{6,22},{8,24},{10,26},{12,28},{14,30},{16,0},... | collective-permute-start | bytes 589832 | tf_op jit(solution)/shard_map/ppermute | solution.py:475
  8.8 10.9 %collective-permute-start.1 = (bf16[32,3072]{1,0:T(8,128)(2,1)}, bf16[32,3072]{1,0:T(8,128)(2,1)S(1)}, u32[]{:S(2)}, u32[]{:S(2)}) collective-permute-start(bf16[32,3072]{1,0:T(8,128)(2,1)} %refs_2_.1), channel_id=1, source_target_pairs={{0,4},{1,3},{2,6},{3,1},{4,0},{5,7},{6,2},{7,5},{8,12},{9,11},{10,... | collective-permute-start | bytes 589832 | tf_op jit(solution)/shard_map/ppermute | solution.py:483
  10.4 10.8 %collective-permute-start.2 = (bf16[32,3072]{1,0:T(8,128)(2,1)S(1)}, bf16[32,3072]{1,0:T(8,128)(2,1)S(1)}, u32[]{:S(2)}, u32[]{:S(2)}) collective-permute-start(bf16[32,3072]{1,0:T(8,128)(2,1)S(1)} %collective-permute-done.refs_2_), channel_id=1, source_target_pairs={{0,4},{1,3},{2,6},{3,1},{4,0},{5,7},{6,2},{7,5},{8,12},{9,11},{10,... | collective-permute-start | bytes 589832 | tf_op jit(solution)/shard_map/ppermute | solution.py:483
  14.3 6.9 %collective-permute-start.4 = (bf16[32,3072]{1,0:T(8,128)(2,1)S(1)}, bf16[32,3072]{1,0:T(8,128)(2,1)S(1)}, u32[]{:S(2)}, u32[]{:S(2)}) collective-permute-start(bf16[32,3072]{1,0:T(8,128)(2,1)S(1)} %collective-permute-done.3.refs_1_), channel_id=1, source_target_pairs={{0,2},{1,5},{2,0},{3,7},{4,6},{5,1},{6,4},{7,3},{8,10},{9,13},{10,... | collective-permute-start | bytes 589832 | tf_op jit(solution)/shard_map/ppermute | solution.py:483
  16.7 6.0 %collective-permute-start.6 = (bf16[32,3072]{1,0:T(8,128)(2,1)S(1)}, bf16[32,3072]{1,0:T(8,128)(2,1)S(1)}, u32[]{:S(2)}, u32[]{:S(2)}) collective-permute-start(bf16[32,3072]{1,0:T(8,128)(2,1)S(1)} %collective-permute-done.3.refs_1_), channel_id=1, source_target_pairs={{0,4},{1,3},{2,6},{3,1},{4,0},{5,7},{6,2},{7,5},{8,12},{9,11},{10,... | collective-permute-start | bytes 589832 | tf_op jit(solution)/shard_map/ppermute | solution.py:483
  17.2 8.0 %collective-permute-start.12 = (bf16[32,3072]{1,0:T(8,128)(2,1)}, bf16[32,3072]{1,0:T(8,128)(2,1)S(1)}, u32[]{:S(2)}, u32[]{:S(2)}) collective-permute-start(bf16[32,3072]{1,0:T(8,128)(2,1)} %refs_2_.1), channel_id=1, source_target_pairs={{0,24},{2,26},{4,28},{6,30},{8,16},{10,18},{12,20},{14,22},{16,8},... | collective-permute-start | bytes 589832 | tf_op jit(solution)/shard_map/ppermute | solution.py:475
  19.7 7.8 %collective-permute-start.10 = (bf16[32,3072]{1,0:T(8,128)(2,1)S(1)}, bf16[32,3072]{1,0:T(8,128)(2,1)S(1)}, u32[]{:S(2)}, u32[]{:S(2)}) collective-permute-start(bf16[32,3072]{1,0:T(8,128)(2,1)S(1)} %collective-permute-done.5.refs_1_), channel_id=1, source_target_pairs={{0,2},{1,5},{2,0},{3,7},{4,6},{5,1},{6,4},{7,3},{8,10},{9,13},{10,... | collective-permute-start | bytes 589832 | tf_op jit(solution)/shard_map/ppermute | solution.py:483
  21.2 6.3 %collective-permute-start.7 = (bf16[32,3072]{1,0:T(8,128)(2,1)S(1)}, bf16[32,3072]{1,0:T(8,128)(2,1)S(1)}, u32[]{:S(2)}, u32[]{:S(2)}) collective-permute-start(bf16[32,3072]{1,0:T(8,128)(2,1)S(1)} %collective-permute-done.4.refs_2_), channel_id=1, source_target_pairs={{0,4},{1,3},{2,6},{3,1},{4,0},{5,7},{6,2},{7,5},{8,12},{9,11},{10,... | collective-permute-start | bytes 589832 | tf_op jit(solution)/shard_map/ppermute | solution.py:483
  22.7 9.2 %collective-permute-start.11 = (bf16[32,3072]{1,0:T(8,128)(2,1)S(1)}, bf16[32,3072]{1,0:T(8,128)(2,1)S(1)}, u32[]{:S(2)}, u32[]{:S(2)}) collective-permute-start(bf16[32,3072]{1,0:T(8,128)(2,1)S(1)} %collective-permute-done.5.refs_1_), channel_id=1, source_target_pairs={{0,4},{1,3},{2,6},{3,1},{4,0},{5,7},{6,2},{7,5},{8,12},{9,11},{10,... | collective-permute-start | bytes 589832 | tf_op jit(solution)/shard_map/ppermute | solution.py:483
  27.4 5.7 %collective-permute-start.13 = (bf16[32,3072]{1,0:T(8,128)(2,1)S(1)}, bf16[32,3072]{1,0:T(8,128)(2,1)S(1)}, u32[]{:S(2)}, u32[]{:S(2)}) collective-permute-start(bf16[32,3072]{1,0:T(8,128)(2,1)S(1)} %collective-permute-done.10.refs_2_), channel_id=1, source_target_pairs={{0,4},{1,3},{2,6},{3,1},{4,0},{5,7},{6,2},{7,5},{8,12},{9,11},{10,... | collective-permute-start | bytes 589832 | tf_op jit(solution)/shard_map/ppermute | solution.py:483
  29.0 5.9 %collective-permute-start.14 = (bf16[32,3072]{1,0:T(8,128)(2,1)S(1)}, bf16[32,3072]{1,0:T(8,128)(2,1)S(1)}, u32[]{:S(2)}, u32[]{:S(2)}) collective-permute-start(bf16[32,3072]{1,0:T(8,128)(2,1)S(1)} %collective-permute-done.12.refs_1_), channel_id=1, source_target_pairs={{0,2},{1,5},{2,0},{3,7},{4,6},{5,1},{6,4},{7,3},{8,10},{9,13},{10,... | collective-permute-start | bytes 589832 | tf_op jit(solution)/shard_map/ppermute | solution.py:483
  30.0 6.5 %collective-permute-start.15 = (bf16[32,3072]{1,0:T(8,128)(2,1)S(1)}, bf16[32,3072]{1,0:T(8,128)(2,1)S(1)}, u32[]{:S(2)}, u32[]{:S(2)}) collective-permute-start(bf16[32,3072]{1,0:T(8,128)(2,1)S(1)} %collective-permute-done.12.refs_1_), channel_id=1, source_target_pairs={{0,4},{1,3},{2,6},{3,1},{4,0},{5,7},{6,2},{7,5},{8,12},{9,11},{10,... | collective-permute-start | bytes 589832 | tf_op jit(solution)/shard_map/ppermute | solution.py:483
  31.0 9.5 %collective-permute-start.8 = (bf16[128,2048]{1,0:T(8,128)(2,1)S(1)}, bf16[128,2048]{1,0:T(8,128)(2,1)S(1)}, u32[]{:S(2)}, u32[]{:S(2)}) collective-permute-start(bf16[128,2048]{1,0:T(8,128)(2,1)S(1)} %get-tuple-element.40), channel_id=1, source_target_pairs={{0,1},{1,0},{2,3},{3,2},{4,5},{5,4},{6,7},{7,6},{8,9},{9,8},{10,11... | collective-permute-start | bytes 1572872 | tf_op jit(solution)/shard_map/ppermute | solution.py:486
  31.9 8.7 %collective-permute-start.9 = (bf16[128,2048]{1,0:T(8,128)(2,1)S(1)}, bf16[128,2048]{1,0:T(8,128)(2,1)S(1)}, u32[]{:S(2)}, u32[]{:S(2)}) collective-permute-start(bf16[128,2048]{1,0:T(8,128)(2,1)S(1)} %get-tuple-element.41), channel_id=1, source_target_pairs={{0,1},{1,0},{2,3},{3,2},{4,5},{5,4},{6,7},{7,6},{8,9},{9,8},{10,11... | collective-permute-start | bytes 1572872 | tf_op jit(solution)/shard_map/ppermute | solution.py:486
  34.0 8.0 %collective-permute-start.16 = (bf16[128,2048]{1,0:T(8,128)(2,1)S(1)}, bf16[128,2048]{1,0:T(8,128)(2,1)S(1)}, u32[]{:S(2)}, u32[]{:S(2)}) collective-permute-start(bf16[128,2048]{1,0:T(8,128)(2,1)S(1)} %get-tuple-element.47), channel_id=1, source_target_pairs={{0,1},{1,0},{2,3},{3,2},{4,5},{5,4},{6,7},{7,6},{8,9},{9,8},{10,11... | collective-permute-start | bytes 1572872 | tf_op jit(solution)/shard_map/ppermute | solution.py:486
  34.9 5.7 %collective-permute-start.18 = (bf16[32,3072]{1,0:T(8,128)(2,1)S(1)}, bf16[32,3072]{1,0:T(8,128)(2,1)S(1)}, u32[]{:S(2)}, u32[]{:S(2)}) collective-permute-start(bf16[32,3072]{1,0:T(8,128)(2,1)S(1)} %collective-permute-done.14.refs_2_), channel_id=1, source_target_pairs={{0,4},{1,3},{2,6},{3,1},{4,0},{5,7},{6,2},{7,5},{8,12},{9,11},{10,... | collective-permute-start | bytes 589832 | tf_op jit(solution)/shard_map/ppermute | solution.py:483
  37.2 4.8 %collective-permute-start.17 = (bf16[96,2048]{1,0:T(8,128)(2,1)S(1)}, bf16[96,2048]{1,0:T(8,128)(2,1)S(1)}, u32[]{:S(2)}, u32[]{:S(2)}) collective-permute-start(bf16[96,2048]{1,0:T(8,128)(2,1)S(1)} %get-tuple-element.48), channel_id=1, source_target_pairs={{0,1},{1,0},{2,3},{3,2},{4,5},{5,4},{6,7},{7,6},{8,9},{9,8},{10,11... | collective-permute-start | bytes 1179656 | tf_op jit(solution)/shard_map/ppermute | solution.py:486
  40.5 1.4 %collective-permute-start.19 = (bf16[32,3072]{1,0:T(8,128)(2,1)S(1)}, bf16[32,3072]{1,0:T(8,128)(2,1)S(1)}, u32[]{:S(2)}, u32[]{:S(2)}) collective-permute-start(bf16[32,3072]{1,0:T(8,128)(2,1)S(1)} %collective-permute-done.18.refs_6_), channel_id=1, source_target_pairs={{0,1},{1,0},{2,3},{3,2},{4,5},{5,4},{6,7},{7,6},{8,9},{9,8},{10,11... | collective-permute-start | bytes 589832 | tf_op jit(solution)/shard_map/ppermute | solution.py:486

commit v6 on v5

--- a/solution.py
+++ b/solution.py
@@ -398,6 +398,10 @@
     )(*arrays)
 
 
+def mean_over(total, count):
+    return total * (1.0 / count) if count & (count - 1) == 0 else total / count
+
+
 def finish_kernel(total_tokens, n_parts, plan, acc, *refs):
     own, other = refs[:n_parts], refs[n_parts : 2 * n_parts]
     far, far_other, *stats = refs[2 * n_parts : -8]
@@ -416,7 +420,7 @@
     for m in range(chunks):
         here = slice(m * rows, (m + 1) * rows)
         total = acc[here, :] + product_rows(left, right, m, rows)
-        result[here, :] = jnp.where(live, total / total_tokens, 0.0)
+        result[here, :] = jnp.where(live, mean_over(total, total_tokens), 0.0)
         copies.append(
             pltpu.make_async_copy(result.at[here, :], out.at[0, here, :], sems.at[m])
         )

time: 44.9 us -> 44.9 us (level)
  no operation moved by 1% of the time
where the time goes in v6:
time: 44.9 us; the launch traced here: 44.7 us
  starting transfers between devices  23.2 us (52%)
  waiting for transfers between devices  13 us (29%)
  Pallas kernels  7.74 us (17%)
  between operations  0.73 us (2%)
    ppermute x12, starting transfers between devices, from_plane(): return lax.ppermute(a, ('tok', 'col'), pairs)  15.9 us
    ppermute x12, waiting for transfers between devices, from_plane(): return lax.ppermute(a, ('tok', 'col'), pairs)  7.12 us
    ppermute x3, starting transfers between devices, from_outer(): return lax.ppermute(a, 'tok', [(t, t ^ 4 * k) for t in range(n_tok)])  6.64 us
    ppermute x3, waiting for transfers between devices, from_outer(): return lax.ppermute(a, 'tok', [(t, t ^ 4 * k) for t in range(n_tok)])  5.46 us
    pallas_call x4, Pallas kernels, wave_parts(): pl.pallas_call(lambda *refs: wave_kernel(sizes, *refs), out_shape=[near.o...  3.01 us
    pallas_call x1, Pallas kernels, finish(): pl.pallas_call(lambda *refs: finish_kernel(total_tokens, len(own), *refs)...  2.72 us
    pallas_call x1, Pallas kernels, partial_gram(): pl.pallas_call(lambda *refs: partial_kernel(held, *refs), out_shape=near....  1.02 us
    pallas_call x1, Pallas kernels, make_plan(): pl.pallas_call(lambda *refs: plan_kernel(block_count, *refs), out_shape=[...  1 us
  transfers between devices with their start and end apart: 20, of which 8 were waited for; matrix products, arithmetic and copies ran while one was open for 0% of the time, Pallas kernels for 11%

profile of v6, /device:TPU:0, one launch (start us, length us, event | category | flops | bytes accessed | tf_op | source)
XLA Modules:
  0.0 44.7 jit_solution(9790511280448930146)
XLA Ops:
  0.6 3.0 %collective-permute-start = (bf16[32,3072]{1,0:T(8,128)(2,1)}, bf16[32,3072]{1,0:T(8,128)(2,1)S(1)}, u32[]{:S(2)}, u32[]{:S(2)}) collective-permute-start(bf16[32,3072]{1,0:T(8,128)(2,1)} %refs_2_.1), channel_id=1, source_target_pairs={{0,2},{1,5},{2,0},{3,7},{4,6},{5,1},{6,4},{7,3},{8,10},{9,13},{10,... | collective-permute-start | bytes 589832 | tf_op jit(solution)/shard_map/ppermute | solution.py:487
  3.6 1.6 %collective-permute-start.3 = (bf16[32,3072]{1,0:T(8,128)(2,1)}, bf16[32,3072]{1,0:T(8,128)(2,1)S(1)}, u32[]{:S(2)}, u32[]{:S(2)}) collective-permute-start(bf16[32,3072]{1,0:T(8,128)(2,1)} %refs_2_.1), channel_id=1, source_target_pairs={{0,8},{2,10},{4,12},{6,14},{8,0},{10,2},{12,4},{14,6},{16,24},{18,... | collective-permute-start | bytes 589832 | tf_op jit(solution)/shard_map/ppermute | solution.py:479
  5.2 2.6 %collective-permute-start.5 = (bf16[32,3072]{1,0:T(8,128)(2,1)}, bf16[32,3072]{1,0:T(8,128)(2,1)S(1)}, u32[]{:S(2)}, u32[]{:S(2)}) collective-permute-start(bf16[32,3072]{1,0:T(8,128)(2,1)} %refs_2_.1), channel_id=1, source_target_pairs={{0,16},{2,18},{4,20},{6,22},{8,24},{10,26},{12,28},{14,30},{16,0},... | collective-permute-start | bytes 589832 | tf_op jit(solution)/shard_map/ppermute | solution.py:479
  7.8 1.0 %plan.1 = (s32[8,128]{1,0:T(8,128)S(1)}, bf16[32,3072]{1,0:T(8,128)(2,1)S(1)}) custom-call(s32[6]{0:T(128)} %refs_0_.1, s32[32]{0:T(128)} %refs_1_.1, bf16[32,3072]{1,0:T(8,128)(2,1)} %refs_2_.1), custom_call_target="tpu_custom_call" | custom-call | tf_op jit(solution)/shard_map/plan/pallas_call | solution.py:254
  8.8 0.0 collective-permute-done.refs_2_
  8.8 1.6 %collective-permute-start.1 = (bf16[32,3072]{1,0:T(8,128)(2,1)}, bf16[32,3072]{1,0:T(8,128)(2,1)S(1)}, u32[]{:S(2)}, u32[]{:S(2)}) collective-permute-start(bf16[32,3072]{1,0:T(8,128)(2,1)} %refs_2_.1), channel_id=1, source_target_pairs={{0,4},{1,3},{2,6},{3,1},{4,0},{5,7},{6,2},{7,5},{8,12},{9,11},{10,... | collective-permute-start | bytes 589832 | tf_op jit(solution)/shard_map/ppermute | solution.py:487
  10.4 0.5 %collective-permute-start.2 = (bf16[32,3072]{1,0:T(8,128)(2,1)S(1)}, bf16[32,3072]{1,0:T(8,128)(2,1)S(1)}, u32[]{:S(2)}, u32[]{:S(2)}) collective-permute-start(bf16[32,3072]{1,0:T(8,128)(2,1)S(1)} %collective-permute-done.refs_2_), channel_id=1, source_target_pairs={{0,4},{1,3},{2,6},{3,1},{4,0},{5,7},{6,2},{7,5},{8,12},{9,11},{10,... | collective-permute-start | bytes 589832 | tf_op jit(solution)/shard_map/ppermute | solution.py:487
  10.9 3.4 %collective-permute-done.3.refs_1_ = bf16[32,3072]{1,0:T(8,128)(2,1)S(1)} collective-permute-done((bf16[32,3072]{1,0:T(8,128)(2,1)}, bf16[32,3072]{1,0:T(8,128)(2,1)S(1)}, u32[]{:S(2)}, u32[]{:S(2)}) %collective-permute-start.3) | collective-permute-done | bytes 196640 | tf_op jit(solution)/shard_map/ppermute | solution.py:479
  14.3 1.5 %collective-permute-start.4 = (bf16[32,3072]{1,0:T(8,128)(2,1)S(1)}, bf16[32,3072]{1,0:T(8,128)(2,1)S(1)}, u32[]{:S(2)}, u32[]{:S(2)}) collective-permute-start(bf16[32,3072]{1,0:T(8,128)(2,1)S(1)} %collective-permute-done.3.refs_1_), channel_id=1, source_target_pairs={{0,2},{1,5},{2,0},{3,7},{4,6},{5,1},{6,4},{7,3},{8,10},{9,13},{10,... | collective-permute-start | bytes 589832 | tf_op jit(solution)/shard_map/ppermute | solution.py:487
  15.8 0.9 %collective-permute-done.5.refs_1_ = bf16[32,3072]{1,0:T(8,128)(2,1)S(1)} collective-permute-done((bf16[32,3072]{1,0:T(8,128)(2,1)}, bf16[32,3072]{1,0:T(8,128)(2,1)S(1)}, u32[]{:S(2)}, u32[]{:S(2)}) %collective-permute-start.5) | collective-permute-done | bytes 196640 | tf_op jit(solution)/shard_map/ppermute | solution.py:479
  16.7 0.5 %collective-permute-start.6 = (bf16[32,3072]{1,0:T(8,128)(2,1)S(1)}, bf16[32,3072]{1,0:T(8,128)(2,1)S(1)}, u32[]{:S(2)}, u32[]{:S(2)}) collective-permute-start(bf16[32,3072]{1,0:T(8,128)(2,1)S(1)} %collective-permute-done.3.refs_1_), channel_id=1, source_target_pairs={{0,4},{1,3},{2,6},{3,1},{4,0},{5,7},{6,2},{7,5},{8,12},{9,11},{10,... | collective-permute-start | bytes 589832 | tf_op jit(solution)/shard_map/ppermute | solution.py:487
  17.2 2.5 %collective-permute-start.12 = (bf16[32,3072]{1,0:T(8,128)(2,1)}, bf16[32,3072]{1,0:T(8,128)(2,1)S(1)}, u32[]{:S(2)}, u32[]{:S(2)}) collective-permute-start(bf16[32,3072]{1,0:T(8,128)(2,1)} %refs_2_.1), channel_id=1, source_target_pairs={{0,24},{2,26},{4,28},{6,30},{8,16},{10,18},{12,20},{14,22},{16,8},... | collective-permute-start | bytes 589832 | tf_op jit(solution)/shard_map/ppermute | solution.py:479
  19.7 0.0 collective-permute-done.1.refs_3_
  19.7 1.5 %collective-permute-start.10 = (bf16[32,3072]{1,0:T(8,128)(2,1)S(1)}, bf16[32,3072]{1,0:T(8,128)(2,1)S(1)}, u32[]{:S(2)}, u32[]{:S(2)}) collective-permute-start(bf16[32,3072]{1,0:T(8,128)(2,1)S(1)} %collective-permute-done.5.refs_1_), channel_id=1, source_target_pairs={{0,2},{1,5},{2,0},{3,7},{4,6},{5,1},{6,4},{7,3},{8,10},{9,13},{10,... | collective-permute-start | bytes 589832 | tf_op jit(solution)/shard_map/ppermute | solution.py:487
  21.2 0.0 collective-permute-done.2.refs_4_
  21.2 0.0 collective-permute-done.4.refs_2_
  21.2 1.5 %collective-permute-start.7 = (bf16[32,3072]{1,0:T(8,128)(2,1)S(1)}, bf16[32,3072]{1,0:T(8,128)(2,1)S(1)}, u32[]{:S(2)}, u32[]{:S(2)}) collective-permute-start(bf16[32,3072]{1,0:T(8,128)(2,1)S(1)} %collective-permute-done.4.refs_2_), channel_id=1, source_target_pairs={{0,4},{1,3},{2,6},{3,1},{4,0},{5,7},{6,2},{7,5},{8,12},{9,11},{10,... | collective-permute-start | bytes 589832 | tf_op jit(solution)/shard_map/ppermute | solution.py:487
  22.7 0.0 collective-permute-done.6.refs_3_
  22.7 0.5 %collective-permute-start.11 = (bf16[32,3072]{1,0:T(8,128)(2,1)S(1)}, bf16[32,3072]{1,0:T(8,128)(2,1)S(1)}, u32[]{:S(2)}, u32[]{:S(2)}) collective-permute-start(bf16[32,3072]{1,0:T(8,128)(2,1)S(1)} %collective-permute-done.5.refs_1_), channel_id=1, source_target_pairs={{0,4},{1,3},{2,6},{3,1},{4,0},{5,7},{6,2},{7,5},{8,12},{9,11},{10,... | collective-permute-start | bytes 589832 | tf_op jit(solution)/shard_map/ppermute | solution.py:487
  23.2 0.8 %wave.4 = (bf16[128,2048]{1,0:T(8,128)(2,1)S(1)}, bf16[128,2048]{1,0:T(8,128)(2,1)S(1)}, f32[2,3072]{1,0:T(2,128)S(1)}) custom-call(s32[8,128]{1,0:T(8,128)S(1)} %get-tuple-element.30.refs_0_, bf16[32,3072]{1,0:T(8,128)(2,1)S(1)} %get-tuple-element.31.refs_1_, bf16[32,3072]{1,0:T(8,128)(2,1)S(1)} %collective-permute-done.refs_2_, ...), custom_call_target="tpu_custom_call" | custom-call | bytes 786432 | tf_op jit(solution)/shard_map/wave/pallas_call | solution.py:330
  24.0 1.2 %collective-permute-done.12.refs_1_ = bf16[32,3072]{1,0:T(8,128)(2,1)S(1)} collective-permute-done((bf16[32,3072]{1,0:T(8,128)(2,1)}, bf16[32,3072]{1,0:T(8,128)(2,1)S(1)}, u32[]{:S(2)}, u32[]{:S(2)}) %collective-permute-start.12) | collective-permute-done | bytes 196640 | tf_op jit(solution)/shard_map/ppermute | solution.py:479
  25.2 2.2 %collective-permute-done.10.refs_2_ = bf16[32,3072]{1,0:T(8,128)(2,1)S(1)} collective-permute-done((bf16[32,3072]{1,0:T(8,128)(2,1)S(1)}, bf16[32,3072]{1,0:T(8,128)(2,1)S(1)}, u32[]{:S(2)}, u32[]{:S(2)}) %collective-permute-start.10) | collective-permute-done | bytes 196640 | tf_op jit(solution)/shard_map/ppermute | solution.py:487
  27.4 0.0 collective-permute-done.7.refs_4_
  27.4 1.5 %collective-permute-start.13 = (bf16[32,3072]{1,0:T(8,128)(2,1)S(1)}, bf16[32,3072]{1,0:T(8,128)(2,1)S(1)}, u32[]{:S(2)}, u32[]{:S(2)}) collective-permute-start(bf16[32,3072]{1,0:T(8,128)(2,1)S(1)} %collective-permute-done.10.refs_2_), channel_id=1, source_target_pairs={{0,4},{1,3},{2,6},{3,1},{4,0},{5,7},{6,2},{7,5},{8,12},{9,11},{10,... | collective-permute-start | bytes 589832 | tf_op jit(solution)/shard_map/ppermute | solution.py:487
  29.0 1.1 %collective-permute-start.14 = (bf16[32,3072]{1,0:T(8,128)(2,1)S(1)}, bf16[32,3072]{1,0:T(8,128)(2,1)S(1)}, u32[]{:S(2)}, u32[]{:S(2)}) collective-permute-start(bf16[32,3072]{1,0:T(8,128)(2,1)S(1)} %collective-permute-done.12.refs_1_), channel_id=1, source_target_pairs={{0,2},{1,5},{2,0},{3,7},{4,6},{5,1},{6,4},{7,3},{8,10},{9,13},{10,... | collective-permute-start | bytes 589832 | tf_op jit(solution)/shard_map/ppermute | solution.py:487
  30.0 1.0 %collective-permute-start.15 = (bf16[32,3072]{1,0:T(8,128)(2,1)S(1)}, bf16[32,3072]{1,0:T(8,128)(2,1)S(1)}, u32[]{:S(2)}, u32[]{:S(2)}) collective-permute-start(bf16[32,3072]{1,0:T(8,128)(2,1)S(1)} %collective-permute-done.12.refs_1_), channel_id=1, source_target_pairs={{0,4},{1,3},{2,6},{3,1},{4,0},{5,7},{6,2},{7,5},{8,12},{9,11},{10,... | collective-permute-start | bytes 589832 | tf_op jit(solution)/shard_map/ppermute | solution.py:487
  31.0 0.0 collective-permute-start.8
  31.0 0.8 %wave.5 = (bf16[128,2048]{1,0:T(8,128)(2,1)S(1)}, bf16[128,2048]{1,0:T(8,128)(2,1)S(1)}, f32[2,3072]{1,0:T(2,128)S(1)}) custom-call(s32[8,128]{1,0:T(8,128)S(1)} %get-tuple-element.30.refs_0_, bf16[32,3072]{1,0:T(8,128)(2,1)S(1)} %collective-permute-done.3.refs_1_, bf16[32,3072]{1,0:T(8,128)(2,1)S(1)} %collective-permute-done.4.refs_2_, ...), custom_call_target="tpu_custom_call" | custom-call | bytes 786432 | tf_op jit(solution)/shard_map/wave/pallas_call | solution.py:330
  31.8 0.0 collective-permute-done.11.refs_3_
  31.8 0.6 %collective-permute-start.9 = (bf16[128,2048]{1,0:T(8,128)(2,1)S(1)}, bf16[128,2048]{1,0:T(8,128)(2,1)S(1)}, u32[]{:S(2)}, u32[]{:S(2)}) collective-permute-start(bf16[128,2048]{1,0:T(8,128)(2,1)S(1)} %get-tuple-element.41), channel_id=1, source_target_pairs={{0,1},{1,0},{2,3},{3,2},{4,5},{5,4},{6,7},{7,6},{8,9},{9,8},{10,11... | collective-permute-start | bytes 1572872 | tf_op jit(solution)/shard_map/ppermute | solution.py:490
  32.4 0.7 %collective-permute-done.13.refs_4_ = bf16[32,3072]{1,0:T(8,128)(2,1)S(1)} collective-permute-done((bf16[32,3072]{1,0:T(8,128)(2,1)S(1)}, bf16[32,3072]{1,0:T(8,128)(2,1)S(1)}, u32[]{:S(2)}, u32[]{:S(2)}) %collective-permute-start.13) | collective-permute-done | bytes 196640 | tf_op jit(solution)/shard_map/ppermute | solution.py:487
  33.2 0.8 %wave.6 = (bf16[128,2048]{1,0:T(8,128)(2,1)S(1)}, bf16[128,2048]{1,0:T(8,128)(2,1)S(1)}, f32[2,3072]{1,0:T(2,128)S(1)}) custom-call(s32[8,128]{1,0:T(8,128)S(1)} %get-tuple-element.30.refs_0_, bf16[32,3072]{1,0:T(8,128)(2,1)S(1)} %collective-permute-done.5.refs_1_, bf16[32,3072]{1,0:T(8,128)(2,1)S(1)} %collective-permute-done.10.refs_2_, ...), custom_call_target="tpu_custom_call" | custom-call | bytes 786432 | tf_op jit(solution)/shard_map/wave/pallas_call | solution.py:330
  34.0 0.1 collective-permute-start.16
  34.0 0.8 %collective-permute-done.14.refs_2_ = bf16[32,3072]{1,0:T(8,128)(2,1)S(1)} collective-permute-done((bf16[32,3072]{1,0:T(8,128)(2,1)S(1)}, bf16[32,3072]{1,0:T(8,128)(2,1)S(1)}, u32[]{:S(2)}, u32[]{:S(2)}) %collective-permute-start.14) | collective-permute-done | bytes 196640 | tf_op jit(solution)/shard_map/ppermute | solution.py:487
  34.9 1.7 %collective-permute-start.18 = (bf16[32,3072]{1,0:T(8,128)(2,1)S(1)}, bf16[32,3072]{1,0:T(8,128)(2,1)S(1)}, u32[]{:S(2)}, u32[]{:S(2)}) collective-permute-start(bf16[32,3072]{1,0:T(8,128)(2,1)S(1)} %collective-permute-done.14.refs_2_), channel_id=1, source_target_pairs={{0,4},{1,3},{2,6},{3,1},{4,0},{5,7},{6,2},{7,5},{8,12},{9,11},{10,... | collective-permute-start | bytes 589832 | tf_op jit(solution)/shard_map/ppermute | solution.py:487
  36.5 0.0 collective-permute-done.15.refs_3_
  36.5 0.6 %wave.7 = (bf16[96,2048]{1,0:T(8,128)(2,1)S(1)}, bf16[96,2048]{1,0:T(8,128)(2,1)S(1)}, f32[4,3072]{1,0:T(4,128)S(1)}) custom-call(s32[8,128]{1,0:T(8,128)S(1)} %get-tuple-element.30.refs_0_, bf16[32,3072]{1,0:T(8,128)(2,1)S(1)} %collective-permute-done.12.refs_1_, bf16[32,3072]{1,0:T(8,128)(2,1)S(1)} %collective-permute-done.14.refs_2_, ...), custom_call_target="tpu_custom_call" | custom-call | bytes 589824 | tf_op jit(solution)/shard_map/wave/pallas_call | solution.py:330
  37.2 0.1 collective-permute-start.17
  37.2 3.3 %collective-permute-done.18.refs_6_ = bf16[32,3072]{1,0:T(8,128)(2,1)S(1)} collective-permute-done((bf16[32,3072]{1,0:T(8,128)(2,1)S(1)}, bf16[32,3072]{1,0:T(8,128)(2,1)S(1)}, u32[]{:S(2)}, u32[]{:S(2)}) %collective-permute-start.18) | collective-permute-done | bytes 196640 | tf_op jit(solution)/shard_map/ppermute | solution.py:487
  40.5 0.0 collective-permute-start.19
  40.5 0.0 collective-permute-done.8.refs_3_
  40.5 0.0 collective-permute-done.9.refs_4_
  40.5 1.0 %partial.1.refs_1_ = f32[1024,1024]{1,0:T(8,128)S(1)} custom-call(s32[8,128]{1,0:T(8,128)S(1)} %get-tuple-element.30.refs_0_, bf16[128,2048]{1,0:T(8,128)(2,1)S(1)} %get-tuple-element.35.refs_1_, bf16[128,2048]{1,0:T(8,128)(2,1)S(1)} %get-tuple-element.39.refs_2_, bf16[128,2048]{1,0:T(8,128)(2,1)S(1)} %collective-permute-done.8.refs_3_, ...), custom_call_target="tpu_custom_call" | custom-call | flops 536870912 | tf_op jit(solution)/shard_map/partial/pallas_call | solution.py:384
  41.6 0.4 collective-permute-done.19.refs_7_
  42.0 0.0 collective-permute-done.17.refs_5_
  42.0 0.0 collective-permute-done.16.refs_4_
  42.0 2.7 %finish.1 = (f32[1,1024,1024]{2,1,0:T(8,128)}, f32[1,3072]{1,0:T(1,128)}, f32[1,3072]{1,0:T(1,128)}) custom-call(s32[8,128]{1,0:T(8,128)S(1)} %get-tuple-element.30.refs_0_, f32[1024,1024]{1,0:T(8,128)S(1)} %partial.1.refs_1_, bf16[128,2048]{1,0:T(8,128)(2,1)S(1)} %get-tuple-element.44.refs_2_, bf16[96,2048]{1,0:T(8,128)(2,1)S(1)} %get-tuple-element.46.refs_3_, ...), custom_call_target="tpu_custom_call" | custom-call | flops 536870912 | bytes 4194304 | tf_op jit(solution)/shard_map/finish/pallas_call | solution.py:446
Async XLA Ops:
  0.6 8.2 %collective-permute-start = (bf16[32,3072]{1,0:T(8,128)(2,1)}, bf16[32,3072]{1,0:T(8,128)(2,1)S(1)}, u32[]{:S(2)}, u32[]{:S(2)}) collective-permute-start(bf16[32,3072]{1,0:T(8,128)(2,1)} %refs_2_.1), channel_id=1, source_target_pairs={{0,2},{1,5},{2,0},{3,7},{4,6},{5,1},{6,4},{7,3},{8,10},{9,13},{10,... | collective-permute-start | bytes 589832 | tf_op jit(solution)/shard_map/ppermute | solution.py:487
  3.6 10.7 %collective-permute-start.3 = (bf16[32,3072]{1,0:T(8,128)(2,1)}, bf16[32,3072]{1,0:T(8,128)(2,1)S(1)}, u32[]{:S(2)}, u32[]{:S(2)}) collective-permute-start(bf16[32,3072]{1,0:T(8,128)(2,1)} %refs_2_.1), channel_id=1, source_target_pairs={{0,8},{2,10},{4,12},{6,14},{8,0},{10,2},{12,4},{14,6},{16,24},{18,... | collective-permute-start | bytes 589832 | tf_op jit(solution)/shard_map/ppermute | solution.py:479
  5.2 11.5 %collective-permute-start.5 = (bf16[32,3072]{1,0:T(8,128)(2,1)}, bf16[32,3072]{1,0:T(8,128)(2,1)S(1)}, u32[]{:S(2)}, u32[]{:S(2)}) collective-permute-start(bf16[32,3072]{1,0:T(8,128)(2,1)} %refs_2_.1), channel_id=1, source_target_pairs={{0,16},{2,18},{4,20},{6,22},{8,24},{10,26},{12,28},{14,30},{16,0},... | collective-permute-start | bytes 589832 | tf_op jit(solution)/shard_map/ppermute | solution.py:479
  8.8 10.9 %collective-permute-start.1 = (bf16[32,3072]{1,0:T(8,128)(2,1)}, bf16[32,3072]{1,0:T(8,128)(2,1)S(1)}, u32[]{:S(2)}, u32[]{:S(2)}) collective-permute-start(bf16[32,3072]{1,0:T(8,128)(2,1)} %refs_2_.1), channel_id=1, source_target_pairs={{0,4},{1,3},{2,6},{3,1},{4,0},{5,7},{6,2},{7,5},{8,12},{9,11},{10,... | collective-permute-start | bytes 589832 | tf_op jit(solution)/shard_map/ppermute | solution.py:487
  10.4 10.8 %collective-permute-start.2 = (bf16[32,3072]{1,0:T(8,128)(2,1)S(1)}, bf16[32,3072]{1,0:T(8,128)(2,1)S(1)}, u32[]{:S(2)}, u32[]{:S(2)}) collective-permute-start(bf16[32,3072]{1,0:T(8,128)(2,1)S(1)} %collective-permute-done.refs_2_), channel_id=1, source_target_pairs={{0,4},{1,3},{2,6},{3,1},{4,0},{5,7},{6,2},{7,5},{8,12},{9,11},{10,... | collective-permute-start | bytes 589832 | tf_op jit(solution)/shard_map/ppermute | solution.py:487
  14.3 6.9 %collective-permute-start.4 = (bf16[32,3072]{1,0:T(8,128)(2,1)S(1)}, bf16[32,3072]{1,0:T(8,128)(2,1)S(1)}, u32[]{:S(2)}, u32[]{:S(2)}) collective-permute-start(bf16[32,3072]{1,0:T(8,128)(2,1)S(1)} %collective-permute-done.3.refs_1_), channel_id=1, source_target_pairs={{0,2},{1,5},{2,0},{3,7},{4,6},{5,1},{6,4},{7,3},{8,10},{9,13},{10,... | collective-permute-start | bytes 589832 | tf_op jit(solution)/shard_map/ppermute | solution.py:487
  16.7 6.0 %collective-permute-start.6 = (bf16[32,3072]{1,0:T(8,128)(2,1)S(1)}, bf16[32,3072]{1,0:T(8,128)(2,1)S(1)}, u32[]{:S(2)}, u32[]{:S(2)}) collective-permute-start(bf16[32,3072]{1,0:T(8,128)(2,1)S(1)} %collective-permute-done.3.refs_1_), channel_id=1, source_target_pairs={{0,4},{1,3},{2,6},{3,1},{4,0},{5,7},{6,2},{7,5},{8,12},{9,11},{10,... | collective-permute-start | bytes 589832 | tf_op jit(solution)/shard_map/ppermute | solution.py:487
  17.2 8.0 %collective-permute-start.12 = (bf16[32,3072]{1,0:T(8,128)(2,1)}, bf16[32,3072]{1,0:T(8,128)(2,1)S(1)}, u32[]{:S(2)}, u32[]{:S(2)}) collective-permute-start(bf16[32,3072]{1,0:T(8,128)(2,1)} %refs_2_.1), channel_id=1, source_target_pairs={{0,24},{2,26},{4,28},{6,30},{8,16},{10,18},{12,20},{14,22},{16,8},... | collective-permute-start | bytes 589832 | tf_op jit(solution)/shard_map/ppermute | solution.py:479
  19.7 7.8 %collective-permute-start.10 = (bf16[32,3072]{1,0:T(8,128)(2,1)S(1)}, bf16[32,3072]{1,0:T(8,128)(2,1)S(1)}, u32[]{:S(2)}, u32[]{:S(2)}) collective-permute-start(bf16[32,3072]{1,0:T(8,128)(2,1)S(1)} %collective-permute-done.5.refs_1_), channel_id=1, source_target_pairs={{0,2},{1,5},{2,0},{3,7},{4,6},{5,1},{6,4},{7,3},{8,10},{9,13},{10,... | collective-permute-start | bytes 589832 | tf_op jit(solution)/shard_map/ppermute | solution.py:487
  21.2 6.3 %collective-permute-start.7 = (bf16[32,3072]{1,0:T(8,128)(2,1)S(1)}, bf16[32,3072]{1,0:T(8,128)(2,1)S(1)}, u32[]{:S(2)}, u32[]{:S(2)}) collective-permute-start(bf16[32,3072]{1,0:T(8,128)(2,1)S(1)} %collective-permute-done.4.refs_2_), channel_id=1, source_target_pairs={{0,4},{1,3},{2,6},{3,1},{4,0},{5,7},{6,2},{7,5},{8,12},{9,11},{10,... | collective-permute-start | bytes 589832 | tf_op jit(solution)/shard_map/ppermute | solution.py:487
  22.7 9.1 %collective-permute-start.11 = (bf16[32,3072]{1,0:T(8,128)(2,1)S(1)}, bf16[32,3072]{1,0:T(8,128)(2,1)S(1)}, u32[]{:S(2)}, u32[]{:S(2)}) collective-permute-start(bf16[32,3072]{1,0:T(8,128)(2,1)S(1)} %collective-permute-done.5.refs_1_), channel_id=1, source_target_pairs={{0,4},{1,3},{2,6},{3,1},{4,0},{5,7},{6,2},{7,5},{8,12},{9,11},{10,... | collective-permute-start | bytes 589832 | tf_op jit(solution)/shard_map/ppermute | solution.py:487
  27.4 5.7 %collective-permute-start.13 = (bf16[32,3072]{1,0:T(8,128)(2,1)S(1)}, bf16[32,3072]{1,0:T(8,128)(2,1)S(1)}, u32[]{:S(2)}, u32[]{:S(2)}) collective-permute-start(bf16[32,3072]{1,0:T(8,128)(2,1)S(1)} %collective-permute-done.10.refs_2_), channel_id=1, source_target_pairs={{0,4},{1,3},{2,6},{3,1},{4,0},{5,7},{6,2},{7,5},{8,12},{9,11},{10,... | collective-permute-start | bytes 589832 | tf_op jit(solution)/shard_map/ppermute | solution.py:487
  29.0 5.9 %collective-permute-start.14 = (bf16[32,3072]{1,0:T(8,128)(2,1)S(1)}, bf16[32,3072]{1,0:T(8,128)(2,1)S(1)}, u32[]{:S(2)}, u32[]{:S(2)}) collective-permute-start(bf16[32,3072]{1,0:T(8,128)(2,1)S(1)} %collective-permute-done.12.refs_1_), channel_id=1, source_target_pairs={{0,2},{1,5},{2,0},{3,7},{4,6},{5,1},{6,4},{7,3},{8,10},{9,13},{10,... | collective-permute-start | bytes 589832 | tf_op jit(solution)/shard_map/ppermute | solution.py:487
  30.0 6.5 %collective-permute-start.15 = (bf16[32,3072]{1,0:T(8,128)(2,1)S(1)}, bf16[32,3072]{1,0:T(8,128)(2,1)S(1)}, u32[]{:S(2)}, u32[]{:S(2)}) collective-permute-start(bf16[32,3072]{1,0:T(8,128)(2,1)S(1)} %collective-permute-done.12.refs_1_), channel_id=1, source_target_pairs={{0,4},{1,3},{2,6},{3,1},{4,0},{5,7},{6,2},{7,5},{8,12},{9,11},{10,... | collective-permute-start | bytes 589832 | tf_op jit(solution)/shard_map/ppermute | solution.py:487
  31.0 9.5 %collective-permute-start.8 = (bf16[128,2048]{1,0:T(8,128)(2,1)S(1)}, bf16[128,2048]{1,0:T(8,128)(2,1)S(1)}, u32[]{:S(2)}, u32[]{:S(2)}) collective-permute-start(bf16[128,2048]{1,0:T(8,128)(2,1)S(1)} %get-tuple-element.40), channel_id=1, source_target_pairs={{0,1},{1,0},{2,3},{3,2},{4,5},{5,4},{6,7},{7,6},{8,9},{9,8},{10,11... | collective-permute-start | bytes 1572872 | tf_op jit(solution)/shard_map/ppermute | solution.py:490
  31.8 8.7 %collective-permute-start.9 = (bf16[128,2048]{1,0:T(8,128)(2,1)S(1)}, bf16[128,2048]{1,0:T(8,128)(2,1)S(1)}, u32[]{:S(2)}, u32[]{:S(2)}) collective-permute-start(bf16[128,2048]{1,0:T(8,128)(2,1)S(1)} %get-tuple-element.41), channel_id=1, source_target_pairs={{0,1},{1,0},{2,3},{3,2},{4,5},{5,4},{6,7},{7,6},{8,9},{9,8},{10,11... | collective-permute-start | bytes 1572872 | tf_op jit(solution)/shard_map/ppermute | solution.py:490
  34.0 8.0 %collective-permute-start.16 = (bf16[128,2048]{1,0:T(8,128)(2,1)S(1)}, bf16[128,2048]{1,0:T(8,128)(2,1)S(1)}, u32[]{:S(2)}, u32[]{:S(2)}) collective-permute-start(bf16[128,2048]{1,0:T(8,128)(2,1)S(1)} %get-tuple-element.47), channel_id=1, source_target_pairs={{0,1},{1,0},{2,3},{3,2},{4,5},{5,4},{6,7},{7,6},{8,9},{9,8},{10,11... | collective-permute-start | bytes 1572872 | tf_op jit(solution)/shard_map/ppermute | solution.py:490
  34.9 5.7 %collective-permute-start.18 = (bf16[32,3072]{1,0:T(8,128)(2,1)S(1)}, bf16[32,3072]{1,0:T(8,128)(2,1)S(1)}, u32[]{:S(2)}, u32[]{:S(2)}) collective-permute-start(bf16[32,3072]{1,0:T(8,128)(2,1)S(1)} %collective-permute-done.14.refs_2_), channel_id=1, source_target_pairs={{0,4},{1,3},{2,6},{3,1},{4,0},{5,7},{6,2},{7,5},{8,12},{9,11},{10,... | collective-permute-start | bytes 589832 | tf_op jit(solution)/shard_map/ppermute | solution.py:487
  37.2 4.8 %collective-permute-start.17 = (bf16[96,2048]{1,0:T(8,128)(2,1)S(1)}, bf16[96,2048]{1,0:T(8,128)(2,1)S(1)}, u32[]{:S(2)}, u32[]{:S(2)}) collective-permute-start(bf16[96,2048]{1,0:T(8,128)(2,1)S(1)} %get-tuple-element.48), channel_id=1, source_target_pairs={{0,1},{1,0},{2,3},{3,2},{4,5},{5,4},{6,7},{7,6},{8,9},{9,8},{10,11... | collective-permute-start | bytes 1179656 | tf_op jit(solution)/shard_map/ppermute | solution.py:490
  40.5 1.4 %collective-permute-start.19 = (bf16[32,3072]{1,0:T(8,128)(2,1)S(1)}, bf16[32,3072]{1,0:T(8,128)(2,1)S(1)}, u32[]{:S(2)}, u32[]{:S(2)}) collective-permute-start(bf16[32,3072]{1,0:T(8,128)(2,1)S(1)} %collective-permute-done.18.refs_6_), channel_id=1, source_target_pairs={{0,1},{1,0},{2,3},{3,2},{4,5},{5,4},{6,7},{7,6},{8,9},{9,8},{10,11... | collective-permute-start | bytes 589832 | tf_op jit(solution)/shard_map/ppermute | solution.py:490

commit v7 on v5

--- a/solution.py
+++ b/solution.py
@@ -498,11 +498,11 @@
     b2 = from_plane(after(z2, b1), False)
     s3 = from_plane(z3, True)
     b3 = from_plane(z3, False)
-    f3 = from_plane(after(s3, b1, b2), False)
     own0, out0, stats0 = wave_parts(plan, [own_shard, s0, b0, after(f0, s1)])
     f2 = from_plane(after(s2, f1, b1, z3, own0), False)
     other0 = from_sibling(out0)
     own1, out1, stats1 = wave_parts(plan, [z1, s1, b1, after(f1, f1)])
+    f3 = from_plane(after(s3, b1, b2, own1), False)
     other1 = from_sibling(out1)
     own2, out2, stats2 = wave_parts(plan, [z2, s2, b2, f2])
     other2 = from_sibling(out2)

time: 44.9 us -> 44.9 us (level)
  no operation moved by 1% of the time
where the time goes in v7:
time: 44.9 us; the launch traced here: 44.7 us
  starting transfers between devices  23.2 us (52%)
  waiting for transfers between devices  13 us (29%)
  Pallas kernels  7.74 us (17%)
  between operations  0.73 us (2%)
    ppermute x12, starting transfers between devices, from_plane(): return lax.ppermute(a, ('tok', 'col'), pairs)  15.9 us
    ppermute x12, waiting for transfers between devices, from_plane(): return lax.ppermute(a, ('tok', 'col'), pairs)  7.12 us
    ppermute x3, starting transfers between devices, from_outer(): return lax.ppermute(a, 'tok', [(t, t ^ 4 * k) for t in range(n_tok)])  6.64 us
    ppermute x3, waiting for transfers between devices, from_outer(): return lax.ppermute(a, 'tok', [(t, t ^ 4 * k) for t in range(n_tok)])  5.46 us
    pallas_call x4, Pallas kernels, wave_parts(): pl.pallas_call(lambda *refs: wave_kernel(sizes, *refs), out_shape=[near.o...  3.01 us
    pallas_call x1, Pallas kernels, finish(): pl.pallas_call(lambda *refs: finish_kernel(total_tokens, len(own), *refs)...  2.72 us
    pallas_call x1, Pallas kernels, partial_gram(): pl.pallas_call(lambda *refs: partial_kernel(held, *refs), out_shape=near....  1.02 us
    pallas_call x1, Pallas kernels, make_plan(): pl.pallas_call(lambda *refs: plan_kernel(block_count, *refs), out_shape=[...  1 us
  transfers between devices with their start and end apart: 20, of which 8 were waited for; matrix products, arithmetic and copies ran while one was open for 0% of the time, Pallas kernels for 11%

profile of v7, /device:TPU:0, one launch (start us, length us, event | category | flops | bytes accessed | tf_op | source)
XLA Modules:
  0.0 44.7 jit_solution(9790511280448930146)
XLA Ops:
  0.6 3.0 %collective-permute-start = (bf16[32,3072]{1,0:T(8,128)(2,1)}, bf16[32,3072]{1,0:T(8,128)(2,1)S(1)}, u32[]{:S(2)}, u32[]{:S(2)}) collective-permute-start(bf16[32,3072]{1,0:T(8,128)(2,1)} %refs_2_.1), channel_id=1, source_target_pairs={{0,2},{1,5},{2,0},{3,7},{4,6},{5,1},{6,4},{7,3},{8,10},{9,13},{10,... | collective-permute-start | bytes 589832 | tf_op jit(solution)/shard_map/ppermute | solution.py:483
  3.6 1.6 %collective-permute-start.3 = (bf16[32,3072]{1,0:T(8,128)(2,1)}, bf16[32,3072]{1,0:T(8,128)(2,1)S(1)}, u32[]{:S(2)}, u32[]{:S(2)}) collective-permute-start(bf16[32,3072]{1,0:T(8,128)(2,1)} %refs_2_.1), channel_id=1, source_target_pairs={{0,8},{2,10},{4,12},{6,14},{8,0},{10,2},{12,4},{14,6},{16,24},{18,... | collective-permute-start | bytes 589832 | tf_op jit(solution)/shard_map/ppermute | solution.py:475
  5.2 2.6 %collective-permute-start.5 = (bf16[32,3072]{1,0:T(8,128)(2,1)}, bf16[32,3072]{1,0:T(8,128)(2,1)S(1)}, u32[]{:S(2)}, u32[]{:S(2)}) collective-permute-start(bf16[32,3072]{1,0:T(8,128)(2,1)} %refs_2_.1), channel_id=1, source_target_pairs={{0,16},{2,18},{4,20},{6,22},{8,24},{10,26},{12,28},{14,30},{16,0},... | collective-permute-start | bytes 589832 | tf_op jit(solution)/shard_map/ppermute | solution.py:475
  7.8 1.0 %plan.1 = (s32[8,128]{1,0:T(8,128)S(1)}, bf16[32,3072]{1,0:T(8,128)(2,1)S(1)}) custom-call(s32[6]{0:T(128)} %refs_0_.1, s32[32]{0:T(128)} %refs_1_.1, bf16[32,3072]{1,0:T(8,128)(2,1)} %refs_2_.1), custom_call_target="tpu_custom_call" | custom-call | tf_op jit(solution)/shard_map/plan/pallas_call | solution.py:254
  8.8 0.0 collective-permute-done.refs_2_
  8.8 1.6 %collective-permute-start.1 = (bf16[32,3072]{1,0:T(8,128)(2,1)}, bf16[32,3072]{1,0:T(8,128)(2,1)S(1)}, u32[]{:S(2)}, u32[]{:S(2)}) collective-permute-start(bf16[32,3072]{1,0:T(8,128)(2,1)} %refs_2_.1), channel_id=1, source_target_pairs={{0,4},{1,3},{2,6},{3,1},{4,0},{5,7},{6,2},{7,5},{8,12},{9,11},{10,... | collective-permute-start | bytes 589832 | tf_op jit(solution)/shard_map/ppermute | solution.py:483
  10.4 0.5 %collective-permute-start.2 = (bf16[32,3072]{1,0:T(8,128)(2,1)S(1)}, bf16[32,3072]{1,0:T(8,128)(2,1)S(1)}, u32[]{:S(2)}, u32[]{:S(2)}) collective-permute-start(bf16[32,3072]{1,0:T(8,128)(2,1)S(1)} %collective-permute-done.refs_2_), channel_id=1, source_target_pairs={{0,4},{1,3},{2,6},{3,1},{4,0},{5,7},{6,2},{7,5},{8,12},{9,11},{10,... | collective-permute-start | bytes 589832 | tf_op jit(solution)/shard_map/ppermute | solution.py:483
  10.9 3.4 %collective-permute-done.3.refs_1_ = bf16[32,3072]{1,0:T(8,128)(2,1)S(1)} collective-permute-done((bf16[32,3072]{1,0:T(8,128)(2,1)}, bf16[32,3072]{1,0:T(8,128)(2,1)S(1)}, u32[]{:S(2)}, u32[]{:S(2)}) %collective-permute-start.3) | collective-permute-done | bytes 196640 | tf_op jit(solution)/shard_map/ppermute | solution.py:475
  14.3 1.5 %collective-permute-start.4 = (bf16[32,3072]{1,0:T(8,128)(2,1)S(1)}, bf16[32,3072]{1,0:T(8,128)(2,1)S(1)}, u32[]{:S(2)}, u32[]{:S(2)}) collective-permute-start(bf16[32,3072]{1,0:T(8,128)(2,1)S(1)} %collective-permute-done.3.refs_1_), channel_id=1, source_target_pairs={{0,2},{1,5},{2,0},{3,7},{4,6},{5,1},{6,4},{7,3},{8,10},{9,13},{10,... | collective-permute-start | bytes 589832 | tf_op jit(solution)/shard_map/ppermute | solution.py:483
  15.8 0.9 %collective-permute-done.5.refs_1_ = bf16[32,3072]{1,0:T(8,128)(2,1)S(1)} collective-permute-done((bf16[32,3072]{1,0:T(8,128)(2,1)}, bf16[32,3072]{1,0:T(8,128)(2,1)S(1)}, u32[]{:S(2)}, u32[]{:S(2)}) %collective-permute-start.5) | collective-permute-done | bytes 196640 | tf_op jit(solution)/shard_map/ppermute | solution.py:475
  16.7 0.5 %collective-permute-start.6 = (bf16[32,3072]{1,0:T(8,128)(2,1)S(1)}, bf16[32,3072]{1,0:T(8,128)(2,1)S(1)}, u32[]{:S(2)}, u32[]{:S(2)}) collective-permute-start(bf16[32,3072]{1,0:T(8,128)(2,1)S(1)} %collective-permute-done.3.refs_1_), channel_id=1, source_target_pairs={{0,4},{1,3},{2,6},{3,1},{4,0},{5,7},{6,2},{7,5},{8,12},{9,11},{10,... | collective-permute-start | bytes 589832 | tf_op jit(solution)/shard_map/ppermute | solution.py:483
  17.2 2.5 %collective-permute-start.12 = (bf16[32,3072]{1,0:T(8,128)(2,1)}, bf16[32,3072]{1,0:T(8,128)(2,1)S(1)}, u32[]{:S(2)}, u32[]{:S(2)}) collective-permute-start(bf16[32,3072]{1,0:T(8,128)(2,1)} %refs_2_.1), channel_id=1, source_target_pairs={{0,24},{2,26},{4,28},{6,30},{8,16},{10,18},{12,20},{14,22},{16,8},... | collective-permute-start | bytes 589832 | tf_op jit(solution)/shard_map/ppermute | solution.py:475
  19.7 0.0 collective-permute-done.1.refs_3_
  19.7 1.5 %collective-permute-start.10 = (bf16[32,3072]{1,0:T(8,128)(2,1)S(1)}, bf16[32,3072]{1,0:T(8,128)(2,1)S(1)}, u32[]{:S(2)}, u32[]{:S(2)}) collective-permute-start(bf16[32,3072]{1,0:T(8,128)(2,1)S(1)} %collective-permute-done.5.refs_1_), channel_id=1, source_target_pairs={{0,2},{1,5},{2,0},{3,7},{4,6},{5,1},{6,4},{7,3},{8,10},{9,13},{10,... | collective-permute-start | bytes 589832 | tf_op jit(solution)/shard_map/ppermute | solution.py:483
  21.2 0.0 collective-permute-done.2.refs_4_
  21.2 0.0 collective-permute-done.4.refs_2_
  21.2 1.5 %collective-permute-start.7 = (bf16[32,3072]{1,0:T(8,128)(2,1)S(1)}, bf16[32,3072]{1,0:T(8,128)(2,1)S(1)}, u32[]{:S(2)}, u32[]{:S(2)}) collective-permute-start(bf16[32,3072]{1,0:T(8,128)(2,1)S(1)} %collective-permute-done.4.refs_2_), channel_id=1, source_target_pairs={{0,4},{1,3},{2,6},{3,1},{4,0},{5,7},{6,2},{7,5},{8,12},{9,11},{10,... | collective-permute-start | bytes 589832 | tf_op jit(solution)/shard_map/ppermute | solution.py:483
  22.7 0.0 collective-permute-done.6.refs_3_
  22.7 0.5 %collective-permute-start.11 = (bf16[32,3072]{1,0:T(8,128)(2,1)S(1)}, bf16[32,3072]{1,0:T(8,128)(2,1)S(1)}, u32[]{:S(2)}, u32[]{:S(2)}) collective-permute-start(bf16[32,3072]{1,0:T(8,128)(2,1)S(1)} %collective-permute-done.5.refs_1_), channel_id=1, source_target_pairs={{0,4},{1,3},{2,6},{3,1},{4,0},{5,7},{6,2},{7,5},{8,12},{9,11},{10,... | collective-permute-start | bytes 589832 | tf_op jit(solution)/shard_map/ppermute | solution.py:483
  23.2 0.8 %wave.4 = (bf16[128,2048]{1,0:T(8,128)(2,1)S(1)}, bf16[128,2048]{1,0:T(8,128)(2,1)S(1)}, f32[2,3072]{1,0:T(2,128)S(1)}) custom-call(s32[8,128]{1,0:T(8,128)S(1)} %get-tuple-element.30.refs_0_, bf16[32,3072]{1,0:T(8,128)(2,1)S(1)} %get-tuple-element.31.refs_1_, bf16[32,3072]{1,0:T(8,128)(2,1)S(1)} %collective-permute-done.refs_2_, ...), custom_call_target="tpu_custom_call" | custom-call | bytes 786432 | tf_op jit(solution)/shard_map/wave/pallas_call | solution.py:330
  24.0 1.2 %collective-permute-done.12.refs_1_ = bf16[32,3072]{1,0:T(8,128)(2,1)S(1)} collective-permute-done((bf16[32,3072]{1,0:T(8,128)(2,1)}, bf16[32,3072]{1,0:T(8,128)(2,1)S(1)}, u32[]{:S(2)}, u32[]{:S(2)}) %collective-permute-start.12) | collective-permute-done | bytes 196640 | tf_op jit(solution)/shard_map/ppermute | solution.py:475
  25.2 2.2 %collective-permute-done.10.refs_2_ = bf16[32,3072]{1,0:T(8,128)(2,1)S(1)} collective-permute-done((bf16[32,3072]{1,0:T(8,128)(2,1)S(1)}, bf16[32,3072]{1,0:T(8,128)(2,1)S(1)}, u32[]{:S(2)}, u32[]{:S(2)}) %collective-permute-start.10) | collective-permute-done | bytes 196640 | tf_op jit(solution)/shard_map/ppermute | solution.py:483
  27.4 0.0 collective-permute-done.7.refs_4_
  27.4 1.5 %collective-permute-start.13 = (bf16[32,3072]{1,0:T(8,128)(2,1)S(1)}, bf16[32,3072]{1,0:T(8,128)(2,1)S(1)}, u32[]{:S(2)}, u32[]{:S(2)}) collective-permute-start(bf16[32,3072]{1,0:T(8,128)(2,1)S(1)} %collective-permute-done.10.refs_2_), channel_id=1, source_target_pairs={{0,4},{1,3},{2,6},{3,1},{4,0},{5,7},{6,2},{7,5},{8,12},{9,11},{10,... | collective-permute-start | bytes 589832 | tf_op jit(solution)/shard_map/ppermute | solution.py:483
  29.0 1.1 %collective-permute-start.14 = (bf16[32,3072]{1,0:T(8,128)(2,1)S(1)}, bf16[32,3072]{1,0:T(8,128)(2,1)S(1)}, u32[]{:S(2)}, u32[]{:S(2)}) collective-permute-start(bf16[32,3072]{1,0:T(8,128)(2,1)S(1)} %collective-permute-done.12.refs_1_), channel_id=1, source_target_pairs={{0,2},{1,5},{2,0},{3,7},{4,6},{5,1},{6,4},{7,3},{8,10},{9,13},{10,... | collective-permute-start | bytes 589832 | tf_op jit(solution)/shard_map/ppermute | solution.py:483
  30.0 1.0 %collective-permute-start.15 = (bf16[32,3072]{1,0:T(8,128)(2,1)S(1)}, bf16[32,3072]{1,0:T(8,128)(2,1)S(1)}, u32[]{:S(2)}, u32[]{:S(2)}) collective-permute-start(bf16[32,3072]{1,0:T(8,128)(2,1)S(1)} %collective-permute-done.12.refs_1_), channel_id=1, source_target_pairs={{0,4},{1,3},{2,6},{3,1},{4,0},{5,7},{6,2},{7,5},{8,12},{9,11},{10,... | collective-permute-start | bytes 589832 | tf_op jit(solution)/shard_map/ppermute | solution.py:483
  31.0 0.0 collective-permute-start.8
  31.0 0.8 %wave.5 = (bf16[128,2048]{1,0:T(8,128)(2,1)S(1)}, bf16[128,2048]{1,0:T(8,128)(2,1)S(1)}, f32[2,3072]{1,0:T(2,128)S(1)}) custom-call(s32[8,128]{1,0:T(8,128)S(1)} %get-tuple-element.30.refs_0_, bf16[32,3072]{1,0:T(8,128)(2,1)S(1)} %collective-permute-done.3.refs_1_, bf16[32,3072]{1,0:T(8,128)(2,1)S(1)} %collective-permute-done.4.refs_2_, ...), custom_call_target="tpu_custom_call" | custom-call | bytes 786432 | tf_op jit(solution)/shard_map/wave/pallas_call | solution.py:330
  31.8 0.0 collective-permute-done.11.refs_3_
  31.8 0.6 %collective-permute-start.9 = (bf16[128,2048]{1,0:T(8,128)(2,1)S(1)}, bf16[128,2048]{1,0:T(8,128)(2,1)S(1)}, u32[]{:S(2)}, u32[]{:S(2)}) collective-permute-start(bf16[128,2048]{1,0:T(8,128)(2,1)S(1)} %get-tuple-element.41), channel_id=1, source_target_pairs={{0,1},{1,0},{2,3},{3,2},{4,5},{5,4},{6,7},{7,6},{8,9},{9,8},{10,11... | collective-permute-start | bytes 1572872 | tf_op jit(solution)/shard_map/ppermute | solution.py:486
  32.4 0.7 %collective-permute-done.13.refs_4_ = bf16[32,3072]{1,0:T(8,128)(2,1)S(1)} collective-permute-done((bf16[32,3072]{1,0:T(8,128)(2,1)S(1)}, bf16[32,3072]{1,0:T(8,128)(2,1)S(1)}, u32[]{:S(2)}, u32[]{:S(2)}) %collective-permute-start.13) | collective-permute-done | bytes 196640 | tf_op jit(solution)/shard_map/ppermute | solution.py:483
  33.2 0.8 %wave.6 = (bf16[128,2048]{1,0:T(8,128)(2,1)S(1)}, bf16[128,2048]{1,0:T(8,128)(2,1)S(1)}, f32[2,3072]{1,0:T(2,128)S(1)}) custom-call(s32[8,128]{1,0:T(8,128)S(1)} %get-tuple-element.30.refs_0_, bf16[32,3072]{1,0:T(8,128)(2,1)S(1)} %collective-permute-done.5.refs_1_, bf16[32,3072]{1,0:T(8,128)(2,1)S(1)} %collective-permute-done.10.refs_2_, ...), custom_call_target="tpu_custom_call" | custom-call | bytes 786432 | tf_op jit(solution)/shard_map/wave/pallas_call | solution.py:330
  34.0 0.1 collective-permute-start.16
  34.0 0.8 %collective-permute-done.14.refs_2_ = bf16[32,3072]{1,0:T(8,128)(2,1)S(1)} collective-permute-done((bf16[32,3072]{1,0:T(8,128)(2,1)S(1)}, bf16[32,3072]{1,0:T(8,128)(2,1)S(1)}, u32[]{:S(2)}, u32[]{:S(2)}) %collective-permute-start.14) | collective-permute-done | bytes 196640 | tf_op jit(solution)/shard_map/ppermute | solution.py:483
  34.9 1.7 %collective-permute-start.18 = (bf16[32,3072]{1,0:T(8,128)(2,1)S(1)}, bf16[32,3072]{1,0:T(8,128)(2,1)S(1)}, u32[]{:S(2)}, u32[]{:S(2)}) collective-permute-start(bf16[32,3072]{1,0:T(8,128)(2,1)S(1)} %collective-permute-done.14.refs_2_), channel_id=1, source_target_pairs={{0,4},{1,3},{2,6},{3,1},{4,0},{5,7},{6,2},{7,5},{8,12},{9,11},{10,... | collective-permute-start | bytes 589832 | tf_op jit(solution)/shard_map/ppermute | solution.py:483
  36.5 0.0 collective-permute-done.15.refs_3_
  36.5 0.6 %wave.7 = (bf16[96,2048]{1,0:T(8,128)(2,1)S(1)}, bf16[96,2048]{1,0:T(8,128)(2,1)S(1)}, f32[4,3072]{1,0:T(4,128)S(1)}) custom-call(s32[8,128]{1,0:T(8,128)S(1)} %get-tuple-element.30.refs_0_, bf16[32,3072]{1,0:T(8,128)(2,1)S(1)} %collective-permute-done.12.refs_1_, bf16[32,3072]{1,0:T(8,128)(2,1)S(1)} %collective-permute-done.14.refs_2_, ...), custom_call_target="tpu_custom_call" | custom-call | bytes 589824 | tf_op jit(solution)/shard_map/wave/pallas_call | solution.py:330
  37.2 0.1 collective-permute-start.17
  37.2 3.3 %collective-permute-done.18.refs_6_ = bf16[32,3072]{1,0:T(8,128)(2,1)S(1)} collective-permute-done((bf16[32,3072]{1,0:T(8,128)(2,1)S(1)}, bf16[32,3072]{1,0:T(8,128)(2,1)S(1)}, u32[]{:S(2)}, u32[]{:S(2)}) %collective-permute-start.18) | collective-permute-done | bytes 196640 | tf_op jit(solution)/shard_map/ppermute | solution.py:483
  40.5 0.0 collective-permute-start.19
  40.5 0.0 collective-permute-done.8.refs_3_
  40.5 0.0 collective-permute-done.9.refs_4_
  40.5 1.0 %partial.1.refs_1_ = f32[1024,1024]{1,0:T(8,128)S(1)} custom-call(s32[8,128]{1,0:T(8,128)S(1)} %get-tuple-element.30.refs_0_, bf16[128,2048]{1,0:T(8,128)(2,1)S(1)} %get-tuple-element.35.refs_1_, bf16[128,2048]{1,0:T(8,128)(2,1)S(1)} %get-tuple-element.39.refs_2_, bf16[128,2048]{1,0:T(8,128)(2,1)S(1)} %collective-permute-done.8.refs_3_, ...), custom_call_target="tpu_custom_call" | custom-call | flops 536870912 | tf_op jit(solution)/shard_map/partial/pallas_call | solution.py:384
  41.6 0.4 collective-permute-done.19.refs_7_
  42.0 0.0 collective-permute-done.17.refs_5_
  42.0 0.0 collective-permute-done.16.refs_4_
  42.0 2.7 %finish.1 = (f32[1,1024,1024]{2,1,0:T(8,128)}, f32[1,3072]{1,0:T(1,128)}, f32[1,3072]{1,0:T(1,128)}) custom-call(s32[8,128]{1,0:T(8,128)S(1)} %get-tuple-element.30.refs_0_, f32[1024,1024]{1,0:T(8,128)S(1)} %partial.1.refs_1_, bf16[128,2048]{1,0:T(8,128)(2,1)S(1)} %get-tuple-element.44.refs_2_, bf16[96,2048]{1,0:T(8,128)(2,1)S(1)} %get-tuple-element.46.refs_3_, ...), custom_call_target="tpu_custom_call" | custom-call | flops 536870912 | bytes 4194304 | tf_op jit(solution)/shard_map/finish/pallas_call | solution.py:442
Async XLA Ops:
  0.6 8.2 %collective-permute-start = (bf16[32,3072]{1,0:T(8,128)(2,1)}, bf16[32,3072]{1,0:T(8,128)(2,1)S(1)}, u32[]{:S(2)}, u32[]{:S(2)}) collective-permute-start(bf16[32,3072]{1,0:T(8,128)(2,1)} %refs_2_.1), channel_id=1, source_target_pairs={{0,2},{1,5},{2,0},{3,7},{4,6},{5,1},{6,4},{7,3},{8,10},{9,13},{10,... | collective-permute-start | bytes 589832 | tf_op jit(solution)/shard_map/ppermute | solution.py:483
  3.6 10.7 %collective-permute-start.3 = (bf16[32,3072]{1,0:T(8,128)(2,1)}, bf16[32,3072]{1,0:T(8,128)(2,1)S(1)}, u32[]{:S(2)}, u32[]{:S(2)}) collective-permute-start(bf16[32,3072]{1,0:T(8,128)(2,1)} %refs_2_.1), channel_id=1, source_target_pairs={{0,8},{2,10},{4,12},{6,14},{8,0},{10,2},{12,4},{14,6},{16,24},{18,... | collective-permute-start | bytes 589832 | tf_op jit(solution)/shard_map/ppermute | solution.py:475
  5.2 11.5 %collective-permute-start.5 = (bf16[32,3072]{1,0:T(8,128)(2,1)}, bf16[32,3072]{1,0:T(8,128)(2,1)S(1)}, u32[]{:S(2)}, u32[]{:S(2)}) collective-permute-start(bf16[32,3072]{1,0:T(8,128)(2,1)} %refs_2_.1), channel_id=1, source_target_pairs={{0,16},{2,18},{4,20},{6,22},{8,24},{10,26},{12,28},{14,30},{16,0},... | collective-permute-start | bytes 589832 | tf_op jit(solution)/shard_map/ppermute | solution.py:475
  8.8 10.9 %collective-permute-start.1 = (bf16[32,3072]{1,0:T(8,128)(2,1)}, bf16[32,3072]{1,0:T(8,128)(2,1)S(1)}, u32[]{:S(2)}, u32[]{:S(2)}) collective-permute-start(bf16[32,3072]{1,0:T(8,128)(2,1)} %refs_2_.1), channel_id=1, source_target_pairs={{0,4},{1,3},{2,6},{3,1},{4,0},{5,7},{6,2},{7,5},{8,12},{9,11},{10,... | collective-permute-start | bytes 589832 | tf_op jit(solution)/shard_map/ppermute | solution.py:483
  10.4 10.8 %collective-permute-start.2 = (bf16[32,3072]{1,0:T(8,128)(2,1)S(1)}, bf16[32,3072]{1,0:T(8,128)(2,1)S(1)}, u32[]{:S(2)}, u32[]{:S(2)}) collective-permute-start(bf16[32,3072]{1,0:T(8,128)(2,1)S(1)} %collective-permute-done.refs_2_), channel_id=1, source_target_pairs={{0,4},{1,3},{2,6},{3,1},{4,0},{5,7},{6,2},{7,5},{8,12},{9,11},{10,... | collective-permute-start | bytes 589832 | tf_op jit(solution)/shard_map/ppermute | solution.py:483
  14.3 6.9 %collective-permute-start.4 = (bf16[32,3072]{1,0:T(8,128)(2,1)S(1)}, bf16[32,3072]{1,0:T(8,128)(2,1)S(1)}, u32[]{:S(2)}, u32[]{:S(2)}) collective-permute-start(bf16[32,3072]{1,0:T(8,128)(2,1)S(1)} %collective-permute-done.3.refs_1_), channel_id=1, source_target_pairs={{0,2},{1,5},{2,0},{3,7},{4,6},{5,1},{6,4},{7,3},{8,10},{9,13},{10,... | collective-permute-start | bytes 589832 | tf_op jit(solution)/shard_map/ppermute | solution.py:483
  16.7 6.0 %collective-permute-start.6 = (bf16[32,3072]{1,0:T(8,128)(2,1)S(1)}, bf16[32,3072]{1,0:T(8,128)(2,1)S(1)}, u32[]{:S(2)}, u32[]{:S(2)}) collective-permute-start(bf16[32,3072]{1,0:T(8,128)(2,1)S(1)} %collective-permute-done.3.refs_1_), channel_id=1, source_target_pairs={{0,4},{1,3},{2,6},{3,1},{4,0},{5,7},{6,2},{7,5},{8,12},{9,11},{10,... | collective-permute-start | bytes 589832 | tf_op jit(solution)/shard_map/ppermute | solution.py:483
  17.2 8.0 %collective-permute-start.12 = (bf16[32,3072]{1,0:T(8,128)(2,1)}, bf16[32,3072]{1,0:T(8,128)(2,1)S(1)}, u32[]{:S(2)}, u32[]{:S(2)}) collective-permute-start(bf16[32,3072]{1,0:T(8,128)(2,1)} %refs_2_.1), channel_id=1, source_target_pairs={{0,24},{2,26},{4,28},{6,30},{8,16},{10,18},{12,20},{14,22},{16,8},... | collective-permute-start | bytes 589832 | tf_op jit(solution)/shard_map/ppermute | solution.py:475
  19.7 7.8 %collective-permute-start.10 = (bf16[32,3072]{1,0:T(8,128)(2,1)S(1)}, bf16[32,3072]{1,0:T(8,128)(2,1)S(1)}, u32[]{:S(2)}, u32[]{:S(2)}) collective-permute-start(bf16[32,3072]{1,0:T(8,128)(2,1)S(1)} %collective-permute-done.5.refs_1_), channel_id=1, source_target_pairs={{0,2},{1,5},{2,0},{3,7},{4,6},{5,1},{6,4},{7,3},{8,10},{9,13},{10,... | collective-permute-start | bytes 589832 | tf_op jit(solution)/shard_map/ppermute | solution.py:483
  21.2 6.3 %collective-permute-start.7 = (bf16[32,3072]{1,0:T(8,128)(2,1)S(1)}, bf16[32,3072]{1,0:T(8,128)(2,1)S(1)}, u32[]{:S(2)}, u32[]{:S(2)}) collective-permute-start(bf16[32,3072]{1,0:T(8,128)(2,1)S(1)} %collective-permute-done.4.refs_2_), channel_id=1, source_target_pairs={{0,4},{1,3},{2,6},{3,1},{4,0},{5,7},{6,2},{7,5},{8,12},{9,11},{10,... | collective-permute-start | bytes 589832 | tf_op jit(solution)/shard_map/ppermute | solution.py:483
  22.7 9.1 %collective-permute-start.11 = (bf16[32,3072]{1,0:T(8,128)(2,1)S(1)}, bf16[32,3072]{1,0:T(8,128)(2,1)S(1)}, u32[]{:S(2)}, u32[]{:S(2)}) collective-permute-start(bf16[32,3072]{1,0:T(8,128)(2,1)S(1)} %collective-permute-done.5.refs_1_), channel_id=1, source_target_pairs={{0,4},{1,3},{2,6},{3,1},{4,0},{5,7},{6,2},{7,5},{8,12},{9,11},{10,... | collective-permute-start | bytes 589832 | tf_op jit(solution)/shard_map/ppermute | solution.py:483
  27.4 5.7 %collective-permute-start.13 = (bf16[32,3072]{1,0:T(8,128)(2,1)S(1)}, bf16[32,3072]{1,0:T(8,128)(2,1)S(1)}, u32[]{:S(2)}, u32[]{:S(2)}) collective-permute-start(bf16[32,3072]{1,0:T(8,128)(2,1)S(1)} %collective-permute-done.10.refs_2_), channel_id=1, source_target_pairs={{0,4},{1,3},{2,6},{3,1},{4,0},{5,7},{6,2},{7,5},{8,12},{9,11},{10,... | collective-permute-start | bytes 589832 | tf_op jit(solution)/shard_map/ppermute | solution.py:483
  29.0 5.9 %collective-permute-start.14 = (bf16[32,3072]{1,0:T(8,128)(2,1)S(1)}, bf16[32,3072]{1,0:T(8,128)(2,1)S(1)}, u32[]{:S(2)}, u32[]{:S(2)}) collective-permute-start(bf16[32,3072]{1,0:T(8,128)(2,1)S(1)} %collective-permute-done.12.refs_1_), channel_id=1, source_target_pairs={{0,2},{1,5},{2,0},{3,7},{4,6},{5,1},{6,4},{7,3},{8,10},{9,13},{10,... | collective-permute-start | bytes 589832 | tf_op jit(solution)/shard_map/ppermute | solution.py:483
  30.0 6.5 %collective-permute-start.15 = (bf16[32,3072]{1,0:T(8,128)(2,1)S(1)}, bf16[32,3072]{1,0:T(8,128)(2,1)S(1)}, u32[]{:S(2)}, u32[]{:S(2)}) collective-permute-start(bf16[32,3072]{1,0:T(8,128)(2,1)S(1)} %collective-permute-done.12.refs_1_), channel_id=1, source_target_pairs={{0,4},{1,3},{2,6},{3,1},{4,0},{5,7},{6,2},{7,5},{8,12},{9,11},{10,... | collective-permute-start | bytes 589832 | tf_op jit(solution)/shard_map/ppermute | solution.py:483
  31.0 9.5 %collective-permute-start.8 = (bf16[128,2048]{1,0:T(8,128)(2,1)S(1)}, bf16[128,2048]{1,0:T(8,128)(2,1)S(1)}, u32[]{:S(2)}, u32[]{:S(2)}) collective-permute-start(bf16[128,2048]{1,0:T(8,128)(2,1)S(1)} %get-tuple-element.40), channel_id=1, source_target_pairs={{0,1},{1,0},{2,3},{3,2},{4,5},{5,4},{6,7},{7,6},{8,9},{9,8},{10,11... | collective-permute-start | bytes 1572872 | tf_op jit(solution)/shard_map/ppermute | solution.py:486
  31.8 8.7 %collective-permute-start.9 = (bf16[128,2048]{1,0:T(8,128)(2,1)S(1)}, bf16[128,2048]{1,0:T(8,128)(2,1)S(1)}, u32[]{:S(2)}, u32[]{:S(2)}) collective-permute-start(bf16[128,2048]{1,0:T(8,128)(2,1)S(1)} %get-tuple-element.41), channel_id=1, source_target_pairs={{0,1},{1,0},{2,3},{3,2},{4,5},{5,4},{6,7},{7,6},{8,9},{9,8},{10,11... | collective-permute-start | bytes 1572872 | tf_op jit(solution)/shard_map/ppermute | solution.py:486
  34.0 8.0 %collective-permute-start.16 = (bf16[128,2048]{1,0:T(8,128)(2,1)S(1)}, bf16[128,2048]{1,0:T(8,128)(2,1)S(1)}, u32[]{:S(2)}, u32[]{:S(2)}) collective-permute-start(bf16[128,2048]{1,0:T(8,128)(2,1)S(1)} %get-tuple-element.47), channel_id=1, source_target_pairs={{0,1},{1,0},{2,3},{3,2},{4,5},{5,4},{6,7},{7,6},{8,9},{9,8},{10,11... | collective-permute-start | bytes 1572872 | tf_op jit(solution)/shard_map/ppermute | solution.py:486
  34.9 5.7 %collective-permute-start.18 = (bf16[32,3072]{1,0:T(8,128)(2,1)S(1)}, bf16[32,3072]{1,0:T(8,128)(2,1)S(1)}, u32[]{:S(2)}, u32[]{:S(2)}) collective-permute-start(bf16[32,3072]{1,0:T(8,128)(2,1)S(1)} %collective-permute-done.14.refs_2_), channel_id=1, source_target_pairs={{0,4},{1,3},{2,6},{3,1},{4,0},{5,7},{6,2},{7,5},{8,12},{9,11},{10,... | collective-permute-start | bytes 589832 | tf_op jit(solution)/shard_map/ppermute | solution.py:483
  37.2 4.8 %collective-permute-start.17 = (bf16[96,2048]{1,0:T(8,128)(2,1)S(1)}, bf16[96,2048]{1,0:T(8,128)(2,1)S(1)}, u32[]{:S(2)}, u32[]{:S(2)}) collective-permute-start(bf16[96,2048]{1,0:T(8,128)(2,1)S(1)} %get-tuple-element.48), channel_id=1, source_target_pairs={{0,1},{1,0},{2,3},{3,2},{4,5},{5,4},{6,7},{7,6},{8,9},{9,8},{10,11... | collective-permute-start | bytes 1179656 | tf_op jit(solution)/shard_map/ppermute | solution.py:486
  40.5 1.4 %collective-permute-start.19 = (bf16[32,3072]{1,0:T(8,128)(2,1)S(1)}, bf16[32,3072]{1,0:T(8,128)(2,1)S(1)}, u32[]{:S(2)}, u32[]{:S(2)}) collective-permute-start(bf16[32,3072]{1,0:T(8,128)(2,1)S(1)} %collective-permute-done.18.refs_6_), channel_id=1, source_target_pairs={{0,1},{1,0},{2,3},{3,2},{4,5},{5,4},{6,7},{7,6},{8,9},{9,8},{10,11... | collective-permute-start | bytes 589832 | tf_op jit(solution)/shard_map/ppermute | solution.py:486
